TPU v7x, 32 devices: a whole 2x2x4 slice. The times are simulated.
32 devices in a mesh: aux: 8 (over z, x), row: 4 (over y, core).
Axes of the slice: x: 2, y: 2, z: 4, core: 2. Of those that a mesh axis runs over, the one named last changes fastest.
Arguments:
- density: float32 [2, 16, 512, 512], P(None, 'aux', 'row'), may hold values from -6 to 6
- couplings: float32 [4, 512], replicated, may hold values from -3 to 3
- weight_real: float32 [4], replicated, may hold values from -1 to 1
- weight_imag: float32 [4], replicated, may hold values from -1 to 1
- mode_rates: float32 [4], replicated, may hold values from 0.05 to 0.5
- tier_counts: int32 [16, 4], P('aux'), may hold values from 0 to 2
- link_index: int32 [16, 8], replicated, may hold values from -1 to 15, as said below
- link_mirror: int32 [16, 8], replicated, may hold values from 0 to 1, as said below
- block_diagonal: bfloat16 [8, 64, 64], replicated, may hold values from -0.5 to 0.5
- block_outer: bfloat16 [8, 64, 64], replicated, may hold values from -0.5 to 0.5
- block_column: int32 [8], replicated, may hold values from 0 to 7
Outputs:
- evolved: float32 [2, 16, 512, 512], P(None, 'aux', 'row')
Inputs may be any that keep to these rules, and one draw needn't show every extreme that they name: Auxiliary a is stored on index a // 2 of aux. For any two different indices of aux, the links of the auxiliaries stored on one of them name at most one distinct pair (link_index, link_mirror) of auxiliaries stored on the other. link_mirror is 0 where link_index is -1.
All inputs are finite; a program needn't handle non-finite values.
Results may differ from a plain program's by a relative error of at most 0.0031.
Values may be sent and summed in bfloat16 or wider, within the bound.
No kernel may reach another device: no remote copies, remote signals or barrier semaphores. Data moves between devices by JAX's collectives and lax.ppermute only.
A program may use at most 128 MiB of HBM per device.

v0:
```python
import functools

import jax
import jax.numpy as jnp
from jax import lax
from jax.experimental import pallas as pl
from jax.experimental.pallas import tpu as pltpu
from jax.sharding import PartitionSpec as P

MODES = 4
LINKS = 8
LANES = 128
STEP = 0.5
BOTH = ("aux", "row")

F32 = jnp.float32
BF16 = jnp.bfloat16


class Sizes:
    def __init__(self, groups, rows, per_device, band, extent):
        self.groups, self.rows, self.per_device = groups, rows, per_device
        self.band, self.extent = band, extent
        self.devices = groups * rows
        self.local = band // groups
        self.auxes = per_device * groups
        self.za = 2 * self.auxes
        self.lanes = self.local * self.za
        self.fold = max(1, LANES // self.za)
        self.tile = self.fold * self.za
        self.tiles = self.local // self.fold
        self.joined = self.local % 16 == 0


def dot(a, b, dims=((1,), (0,))):
    return lax.dot_general(a, b, (dims, ((), ())), preferred_element_type=F32)


def run(kernel, outs, args, scratch=(), flops=0, scalars=()):
    spec = pl.BlockSpec(memory_space=pltpu.VMEM)
    flat = pl.BlockSpec(memory_space=pltpu.SMEM)
    moved = sum(a.size * a.dtype.itemsize for a in args)
    moved += sum(o.size * o.dtype.itemsize for o in outs)
    return pl.pallas_call(
        kernel,
        out_shape=list(outs),
        in_specs=[flat if n in scalars else spec for n in range(len(args))],
        out_specs=[spec] * len(outs),
        scratch_shapes=list(scratch),
        compiler_params=pltpu.CompilerParams(vmem_limit_bytes=16 << 20),
        cost_estimate=pl.CostEstimate(flops=flops, bytes_accessed=moved, transcendentals=0),
    )(*args)


def shape(*dims, dtype=F32):
    return jax.ShapeDtypeStruct(dims, dtype)


def one_hot(target, count):
    return (target[:, None] == jnp.arange(count, dtype=jnp.int32)[None, :]).astype(BF16)


def matrix_index(s, index, device):
    group, row = device // s.rows, device % s.rows
    return row * s.band + index * s.groups + group


def row_blocks(extent, size=128):
    return range(0, extent, size)


def send_start_kernel(d_ref, pick_rows, pick_cols, out_ref):
    planes, number, band, extent = d_ref.shape
    flat = d_ref[...].reshape(planes * number * band, extent).astype(BF16)
    for b in row_blocks(flat.shape[0]):
        moved = dot(pick_rows[b : b + 128, :], flat).astype(BF16)
        out_ref[b : b + 128, :] = dot(moved, pick_cols[...]).astype(BF16)


def take_start_kernel(got_ref, pick_lanes, message_rows, s_ref, m_ref):
    for b in row_blocks(got_ref.shape[1]):
        s_ref[b : b + 128, :] = dot(
            got_ref[:, b : b + 128], pick_lanes[...], ((0,), (0,))
        ).astype(BF16)
    for b in row_blocks(m_ref.shape[0]):
        m_ref[b : b + 128, :] = dot(message_rows[b : b + 128, :], s_ref[...]).astype(BF16)


def turn(s, load, order, swap, put):
    size = order.shape[0]
    span = size // s.local
    for block in range(s.extent // size):
        moved = dot(order[...], load(block * size, size))
        parts = []
        for ih in range(s.tiles):
            for jh in range(s.tiles):
                lanes = slice(jh * s.tile, (jh + 1) * s.tile)
                pieces = [
                    moved[(ih * s.fold + f) * span : (ih * s.fold + f + 1) * span, lanes]
                    for f in range(s.fold)
                ]
                parts.append(jnp.concatenate(pieces, axis=1) if s.fold > 1 else pieces[0])
        turned = dot(jnp.concatenate(parts, axis=0).astype(BF16), swap[...])
        for ih in range(s.tiles):
            for jh in range(s.tiles):
                start = (ih * s.tiles + jh) * span
                for f in range(s.fold):
                    first = (jh * s.fold + f) * s.devices + block * span
                    put(
                        slice(first, first + span),
                        slice(ih * s.tile, (ih + 1) * s.tile),
                        turned[start : start + span, f * s.tile : (f + 1) * s.tile],
                    )


def take_columns_kernel(s, got_ref, order, swap, first_rows, left_rows, s_ref, t_ref, *message):
    def put(rows, lanes, value):
        t_ref[rows, lanes] = value.astype(BF16)

    turn(s, lambda start, size: got_ref[start : start + size, :], order, swap, put)
    write_messages(s, first_rows, left_rows, s_ref, t_ref, message)


def write_messages(s, right_rows, left_rows, s_ref, t_ref, message):
    pairs = ((left_rows, t_ref), (right_rows, s_ref))
    if not s.joined and len(message) == 1:
        pairs = pairs[:1]
    both = s.joined and message[0].shape[0] == 2 * s.extent
    for part, (matrix, state) in enumerate(pairs):
        if s.joined and part == 1 and not both:
            continue
        for b in row_blocks(s.extent):
            product = dot(matrix[b : b + 128, :], state[...]).astype(BF16)
            if not s.joined:
                message[part][b : b + 128, :] = product
            elif not both:
                message[0][b : b + 128, :] = product
            else:
                for k in range(128 // s.local):
                    start = ((b // s.local + k) * 2 + part) * s.local
                    message[0][start : start + s.local, :] = product[
                        k * s.local : (k + 1) * s.local, :
                    ]


def slope_kernel(
    s, with_columns, s_ref, t_ref, ys_ref, yt_ref, damp, q_ref, right, left, unit, wa_s, wb_s, wa_t, wb_t, *rest
):
    if with_columns:
        ks_ref, kt_ref, turned = rest
    else:
        ks_ref, turned = rest

    def one(direct, mirror, y_ref, h, wa, wb, out_ref, sign):
        for th in range(s.tiles):
            lanes = slice(th * s.tile, (th + 1) * s.tile)
            turned[:, lanes] = dot(direct[:, lanes], unit[...]).astype(BF16)
        for b in row_blocks(s.extent):
            rows = slice(b, b + 128)
            whole = dot(h[rows, :], turned[...])
            for th in range(s.tiles):
                lanes = slice(th * s.tile, (th + 1) * s.tile)
                source = jnp.concatenate([direct[rows, lanes], mirror[rows, lanes]], axis=1)
                source = jnp.concatenate([source, source], axis=1)
                total = dot(source, wa[th]) - damp[:, lanes] * y_ref[rows, lanes].astype(F32)
                total = total + sign * whole[:, lanes]
                fields = dot(source, wb[...])
                for k in range(MODES):
                    total = total + q_ref[rows, k : k + 1] * fields[:, k * s.tile : (k + 1) * s.tile]
                out_ref[rows, lanes] = total

    one(s_ref, t_ref, ys_ref, right, wa_s, wb_s, ks_ref, -1.0)
    if with_columns:
        one(t_ref, s_ref, yt_ref, left, wa_t, wb_t, kt_ref, 1.0)


def part_loader(s, refs, part):
    def load(start, size):
        if not s.joined:
            return refs[part][start : start + size, :]
        step = s.local
        pieces = []
        for first in range(start, start + size, step):
            at = (first // step * 2 + part) * step
            pieces.append(refs[0][at : at + step, :])
        return jnp.concatenate(pieces, axis=0)

    return load


def next_kernel(s, weight, step, has_total, both, got_count, *refs):
    got = refs[:got_count]
    refs = refs[got_count:]
    order, swap, right_rows, left_rows, ks_ref, kt_ref, ds_ref, dt_ref = refs[:8]
    refs = refs[8:]
    total_in = None
    if has_total:
        total_in, refs = refs[0], refs[1:]
    s_ref, t_ref, ys_ref, yt_ref, total_ref = refs[:5]
    message, arrived = refs[5:-1], refs[-1]

    def put(rows, lanes, value):
        arrived[rows, lanes] = value

    for part in range(2):
        turn(s, part_loader(s, got, part), order, swap, put)
        for b in row_blocks(s.extent, 64):
            rows = slice(b, b + 64)
            if part == 0:
                slope = ks_ref[rows, :] + arrived[rows, :]
                grown = weight * slope
                total_ref[rows, :] = total_in[rows, :] + grown if has_total else grown
                state = ds_ref[rows, :].astype(F32) + step * slope
                ys_ref[rows, :] = state
                s_ref[rows, :] = state.astype(BF16)
            else:
                slope = kt_ref[rows, :] - arrived[rows, :]
                state = dt_ref[rows, :].astype(F32) + step * slope
                yt_ref[rows, :] = state
                t_ref[rows, :] = state.astype(BF16)
    if message:
        write_messages(s, right_rows, left_rows, s_ref, t_ref, message)


def last_kernel(s, weight, got_ref, order, swap, ks_ref, total_in, pick_lanes, out_ref, arrived, grown):
    def put(rows, lanes, value):
        arrived[rows, lanes] = value

    turn(s, lambda start, size: got_ref[start : start + size, :], order, swap, put)
    for b in row_blocks(s.extent, 64):
        rows = slice(b, b + 64)
        change = total_in[rows, :] + weight * (ks_ref[rows, :] + arrived[rows, :])
        grown[rows, :] = change.astype(BF16)
    for b in row_blocks(s.lanes):
        out_ref[b : b + 128, :] = dot(
            pick_lanes[b : b + 128, :], grown[...], ((1,), (1,))
        ).astype(BF16)


def finish_kernel(got_ref, place_rows, place_cols, d_ref, out_ref):
    planes, number, band, extent = d_ref.shape
    for z in range(planes):
        for n in range(number):
            at = (z * number + n) * band
            for b in range(0, band, min(band, 128)):
                size = min(band, 128)
                rows = slice(at + b, at + b + size)
                moved = dot(place_rows[rows, :], got_ref[...]).astype(BF16)
                out_ref[z, n, b : b + size, :] = d_ref[z, n, b : b + size, :] + dot(
                    moved, place_cols[...]
                )


def link_matrices(s, counts, weight_real, weight_imag, link_index, link_mirror):
    ones = jnp.ones_like(counts)
    real = jnp.stack([ones, counts * weight_real[None, :]], 1)
    imag = jnp.stack([jnp.zeros_like(counts), counts * weight_imag[None, :]], 1)
    index = link_index.reshape(s.auxes, 2, MODES)
    mirror = link_mirror.reshape(s.auxes, 2, MODES)
    source = jnp.arange(s.auxes, dtype=jnp.int32)
    hit = index[None] == source[:, None, None, None]
    kinds = jnp.stack([hit & (mirror[None] == 0), hit & (mirror[None] == 1)]).astype(F32)
    along = jnp.sum(kinds * real, 3)
    cross = jnp.sum(kinds * imag, 3)
    along, cross = (jnp.transpose(m, (0, 3, 1, 2)) for m in (along, cross))
    flip = jnp.array([1.0, -1.0], F32).reshape(2, 1, 1, 1)

    def build(sign):
        upper = jnp.concatenate([cross, -sign * along], 3)
        lower = jnp.concatenate([sign * along, cross], 3) * flip
        return jnp.concatenate([upper, lower], 2)

    return build(1.0), build(-1.0)


def two_pieces(weights, axis):
    high = lax.reduce_precision(weights, 8, 7)
    low = weights - high
    return jnp.concatenate([high.astype(BF16), low.astype(BF16)], axis)


def coupling_weights(s, by_local, by_first, local_q):
    eye = jnp.eye(s.fold, dtype=F32)
    near = jnp.einsum("ki,xkuv->ixuv", local_q, by_local, precision=lax.Precision.HIGHEST)
    near = near.reshape(s.tiles, s.fold, 2, s.za, s.za)
    near = jnp.transpose(near, (0, 2, 1, 3, 4))[:, :, :, :, None, :] * eye[None, None, :, None, :, None]
    near = near.reshape(s.tiles, 2 * s.tile, s.tile)
    far = jnp.transpose(by_first, (0, 2, 1, 3))[:, None, :, :, None, :] * eye[None, :, None, None, :, None]
    far = far.reshape(2 * s.tile, MODES * s.tile)
    return two_pieces(near, 1), two_pieces(far, 0)


def general_body(
    density,
    couplings,
    weight_real,
    weight_imag,
    mode_rates,
    tier_counts,
    link_index,
    link_mirror,
    block_diagonal,
    block_outer,
    block_column,
):
    planes, per_device, band, extent = density.shape
    s = Sizes(lax.axis_size("aux"), lax.axis_size("row"), per_device, band, extent)
    blocks, block = block_diagonal.shape[0], block_diagonal.shape[1]
    group, row = lax.axis_index("aux"), lax.axis_index("row")
    device = group * s.rows + row
    cube = 2 * extent * extent * s.lanes

    number = jnp.arange(extent, dtype=jnp.int32)
    first_to_matrix = matrix_index(s, number // s.devices, number % s.devices)
    posted_to_matrix = matrix_index(s, number % s.local, number // s.local)
    posted_to_first = number % s.local * s.devices + number // s.local

    wide = jnp.arange(s.lanes, dtype=jnp.int32)
    sub = planes * per_device * s.local
    start_source = wide % sub * s.groups + wide // sub
    pick_rows = one_hot(start_source, s.lanes)
    pick_cols = one_hot(first_to_matrix, extent).T
    lane_of = (
        wide % s.local * s.za
        + wide // (per_device * s.local) % planes * s.auxes
        + wide // sub * per_device
        + wide // s.local % per_device
    )
    pick_lanes = one_hot(lane_of, s.lanes)
    message_rows = one_hot(posted_to_first, extent)
    start_message = run(
        send_start_kernel,
        [shape(s.lanes, extent, dtype=BF16)],
        [density, pick_rows, pick_cols],
        flops=2 * cube,
    )[0]
    start_got = lax.all_to_all(
        start_message.reshape(s.groups, sub, extent), "aux", split_axis=0, concat_axis=0, tiled=True
    ).reshape(s.lanes, extent)

    selector = block_column[:, None] == jnp.arange(blocks, dtype=jnp.int32)[None, :]
    own = jnp.eye(blocks, dtype=F32)
    whole_h = (
        own[:, None, :, None] * block_diagonal.astype(F32)[:, :, None, :]
        + selector.astype(F32)[:, None, :, None] * block_outer.astype(F32)[:, :, None, :]
    ).reshape(extent, extent).astype(BF16)
    first_h = one_hot(first_to_matrix, extent)
    left = jnp.dot(
        jnp.dot(first_h, whole_h, preferred_element_type=BF16), first_h.T, preferred_element_type=BF16
    )
    right = left.T
    left_rows = jnp.dot(message_rows, left, preferred_element_type=BF16)
    right_rows = jnp.dot(message_rows, right, preferred_element_type=BF16)

    counts = lax.all_gather(tier_counts, "aux", axis=0, tiled=True).astype(F32)
    damping = jnp.sum(counts * mode_rates[None, :], axis=1)
    damp = jnp.tile(damping, (planes * s.local,))[None, :]
    q_first = jnp.dot(
        couplings, first_h.T.astype(F32), precision=lax.Precision.HIGHEST
    ).T
    local_pick = (matrix_index(s, jnp.arange(s.local, dtype=jnp.int32), device)[None, :] == number[:, None])
    local_q = jnp.dot(couplings, local_pick.astype(F32), precision=lax.Precision.HIGHEST)
    by_row, by_column = link_matrices(s, counts, weight_real, weight_imag, link_index, link_mirror)
    wa_s, wb_s = coupling_weights(s, by_row, by_column, local_q)
    wa_t, wb_t = coupling_weights(s, by_column, by_row, local_q)

    lane = jnp.arange(s.za, dtype=jnp.int32)
    unit = jnp.where(
        lane[:, None] == (lane[None, :] + s.auxes) % s.za,
        jnp.where(lane[None, :] < s.auxes, 1.0, -1.0),
        0.0,
    )
    eye_fold = jnp.eye(s.fold, dtype=F32)
    unit_tile = (eye_fold[:, None, :, None] * unit[None, :, None, :]).reshape(s.tile, s.tile).astype(BF16)
    swap = (
        eye_fold[:, None, None, None, :, None]
        * eye_fold[None, :, None, :, None, None]
        * unit[None, None, :, None, None, :]
    ).reshape(s.fold * s.tile, s.fold * s.tile).astype(BF16)
    keep = (
        eye_fold[:, None, None, None, :, None]
        * eye_fold[None, :, None, :, None, None]
        * jnp.eye(s.za, dtype=F32)[None, None, :, None, None, :]
    ).reshape(s.fold * s.tile, s.fold * s.tile).astype(BF16)
    size = min(extent, max(256, 16 * s.local))
    span = size // s.local
    at = jnp.arange(size, dtype=jnp.int32)
    order = one_hot(at % span * s.local + at // span, size)

    state = shape(extent, s.lanes, dtype=BF16)
    full = shape(extent, s.lanes)
    held = pltpu.VMEM((extent, s.lanes), F32)
    held_b = pltpu.VMEM((extent, s.lanes), BF16)

    def exchange(messages):
        parts = [m.reshape(s.devices, -1, s.lanes) for m in messages]
        sent = parts[0] if len(parts) == 1 else jnp.concatenate(parts, 1)
        got = lax.all_to_all(sent, BOTH, split_axis=0, concat_axis=0, tiled=True)
        if len(parts) == 1:
            return [got.reshape(-1, s.lanes)]
        height = s.local
        return [got[:, p * height : (p + 1) * height].reshape(-1, s.lanes) for p in range(2)]

    if s.joined:
        pair = [shape(2 * extent, s.lanes, dtype=BF16)]
    else:
        pair = [state, state]

    s_now, posted = run(
        take_start_kernel, [state, state], [start_got, pick_lanes, message_rows], flops=2 * cube
    )
    got = exchange([posted])
    t_now, *messages = run(
        functools.partial(take_columns_kernel, s),
        [state] + pair,
        [got[0], order, keep, right_rows, left_rows, s_now],
        flops=4 * cube,
    )
    start_s, start_t = s_now, t_now
    ys, yt = s_now, t_now
    total = None
    shares = [STEP / 6.0, STEP / 3.0, STEP / 3.0, STEP / 6.0]
    steps = [0.25, 0.25, 0.5]
    for section in range(4):
        got = exchange(messages)
        columns = section < 3
        slopes = run(
            functools.partial(slope_kernel, s, columns),
            [full, full] if columns else [full],
            [s_now, t_now, ys, yt, damp, q_first, right, left, unit_tile, wa_s, wb_s, wa_t, wb_t],
            scratch=[held_b],
            flops=(12 if columns else 6) * cube,
        )
        if columns:
            args = list(got) + [order, swap, right_rows, left_rows, *slopes, start_s, start_t]
            if total is not None:
                args.append(total)
            outs = [state, state, full, full, full]
            outs += pair if section < 2 else [state]
            s_now, t_now, ys, yt, total, *messages = run(
                functools.partial(
                    next_kernel, s, shares[section], steps[section], total is not None, section < 2, len(got)
                ),
                outs,
                args,
                scratch=[held],
                flops=6 * cube,
            )
    change = run(
        functools.partial(last_kernel, s, shares[3]),
        [shape(s.lanes, extent, dtype=BF16)],
        [got[0], order, swap, slopes[0], total, pick_lanes],
        scratch=[held, held_b],
        flops=3 * cube,
    )[0]
    back = lax.all_to_all(
        change.reshape(s.groups, sub, extent), "aux", split_axis=0, concat_axis=0, tiled=True
    ).reshape(s.lanes, extent)
    return run(
        finish_kernel,
        [shape(planes, per_device, band, extent)],
        [back, pick_rows.T, pick_cols.T, density],
        flops=2 * cube,
    )[0]


def counts_of_all(s, tier_counts, group):
    if s.groups & (s.groups - 1):
        return lax.all_gather(tier_counts, "aux", axis=0, tiled=True).astype(F32)
    whole = lax.dynamic_update_slice_in_dim(
        jnp.zeros((s.auxes, MODES), F32), tier_counts.astype(F32), group * s.per_device, 0
    )
    step = 1
    while step < s.groups:
        whole = whole + lax.ppermute(whole, "aux", [(i, i ^ step) for i in range(s.groups)])
        step *= 2
    return whole


def iotas(rows, columns):
    return (
        lax.broadcasted_iota(jnp.int32, (rows, columns), 0),
        lax.broadcasted_iota(jnp.int32, (rows, columns), 1),
    )


def post_matrix(s):
    row, column = iotas(s.extent, s.extent)
    return (column == row % s.local * s.devices + row // s.local).astype(F32).astype(BF16)


def place(s, message, part, first, value, lanes=slice(None)):
    for k in range(value.shape[0] // s.local):
        start = ((first // s.local + k) * 2 + part) * s.local
        message[start : start + s.local, lanes] = value[k * s.local : (k + 1) * s.local, :]


def even_start_kernel(s, d_ref, out_ref, post):
    planes, number, band, extent = d_ref.shape
    post[...] = post_matrix(s)
    flat = d_ref[...].reshape(planes * number * band, extent).astype(BF16)
    for b in row_blocks(extent):
        place(s, out_ref, 0, b, dot(post[b : b + 128, :], flat).astype(BF16))
        place(s, out_ref, 1, b, dot(post[b : b + 128, :], flat, ((1,), (1,))).astype(BF16))


def part_rows(s, got_ref, part, devices, lanes=slice(None)):
    pieces = [
        got_ref[(d * 2 + part) * s.local : (d * 2 + part + 1) * s.local, lanes] for d in devices
    ]
    return jnp.concatenate(pieces, axis=0)


def even_take_kernel(s, got_ref, row_lanes, column_lanes, right_rows, left_rows, s_ref, t_ref, message):
    everyone = range(s.devices)
    for b in row_blocks(s.extent):
        s_ref[b : b + 128, :] = dot(
            part_rows(s, got_ref, 0, everyone, slice(b, b + 128)), row_lanes[...], ((0,), (0,))
        ).astype(BF16)
    for q in range(s.rows):
        owners = [g * s.rows + q for g in range(s.groups)]
        pieces = [
            part_rows(s, got_ref, 1, owners, slice(v * s.band, (v + 1) * s.band))
            for v in range(s.extent // s.band)
        ]
        t_ref[q * s.band : (q + 1) * s.band, :] = dot(
            jnp.concatenate(pieces, axis=0), column_lanes[...], ((0,), (0,))
        ).astype(BF16)
    write_messages(s, right_rows, left_rows, s_ref, t_ref, [message])


def even_last_kernel(s, weight, ks_ref, total_in, t_ref, left, unit, row_lanes, column_lanes, out_ref, grown, turned):
    for th in range(s.tiles):
        lanes = slice(th * s.tile, (th + 1) * s.tile)
        turned[:, lanes] = dot(t_ref[:, lanes], unit[...]).astype(BF16)
    for b in row_blocks(s.extent):
        rows = slice(b, b + 128)
        grown[rows, :] = (total_in[rows, :] + weight * ks_ref[rows, :]).astype(BF16)
    for b in row_blocks(s.extent):
        place(s, out_ref, 0, b, dot(row_lanes[b : b + 128, :], grown[...], ((1,), (1,))).astype(BF16))
    for b in row_blocks(s.extent):
        rows = slice(b, b + 128)
        grown[rows, :] = (weight * dot(left[rows, :], turned[...])).astype(BF16)
    for q in range(s.rows):
        value = dot(column_lanes[...], grown[q * s.band : (q + 1) * s.band, :], ((1,), (1,))).astype(BF16)
        for v in range(s.extent // s.band):
            for g in range(s.groups):
                at = (v * s.groups + g) * s.local
                start = ((g * s.rows + q) * 2 + 1) * s.local
                out_ref[start : start + s.local, v * s.band : (v + 1) * s.band] = value[at : at + s.local, :]


def even_finish_kernel(s, got_ref, d_ref, out_ref, post, moved):
    planes, number, band, extent = d_ref.shape
    post[...] = post_matrix(s)
    everyone = range(s.devices)
    for d in everyone:
        moved[d * s.local : (d + 1) * s.local, :] = got_ref[d * 2 * s.local : (d * 2 + 1) * s.local, :]
    for z in range(planes):
        for n in range(number):
            at = (z * number + n) * band
            lanes = slice(at, at + band)
            change = dot(post[:, lanes], moved[...], ((0,), (0,)))
            change = change + dot(part_rows(s, got_ref, 1, everyone, lanes), post[...], ((0,), (0,)))
            out_ref[z, n] = d_ref[z, n] + change


def hamiltonian_kernel(s, own_ref, outer_ref, where_ref, left, right, left_rows, right_rows, post):
    blocks, block = own_ref.shape[0], own_ref.shape[1]
    post[...] = post_matrix(s)
    row, column = iotas(block, s.extent)
    for b in range(blocks):
        spread = column - row
        to_own = (spread == b * block).astype(F32).astype(BF16)
        to_far = (spread == where_ref[b] * block).astype(F32).astype(BF16)
        left[b * block : (b + 1) * block, :] = (dot(own_ref[b], to_own) + dot(outer_ref[b], to_far)).astype(BF16)
    row, column = iotas(s.extent, s.extent)
    same = (row == column).astype(F32).astype(BF16)
    for b in row_blocks(s.extent):
        rows = slice(b, b + 128)
        right[rows, :] = dot(same[rows, :], left[...], ((1,), (1,))).astype(BF16)
        left_rows[rows, :] = dot(post[rows, :], left[...]).astype(BF16)
        right_rows[rows, :] = dot(post[rows, :], left[...], ((1,), (1,))).astype(BF16)


def weights_kernel(s, table, local_q, wa_s, wb_s, wa_t, wb_t):
    depth, wide = 2 * s.tile, MODES * s.tile
    row, column = iotas(depth, wide)
    same = row // s.za % s.fold == column // s.za % s.fold
    source, kind = (row % s.auxes).astype(F32), (row // s.tile).astype(F32)
    from_imag, to_imag = row // s.auxes % 2, column // s.auxes % 2
    up = same & (table[0:1, :] == source) & (table[2:3, :] == kind)
    down = same & (table[1:2, :] == source) & (table[3:4, :] == kind)
    along = jnp.where(up, 1.0, 0.0) + jnp.where(down, table[4:5, :], 0.0)
    cross = jnp.where(down, table[5:6, :], 0.0)
    along = jnp.where(from_imag == 1, along, -along)
    flip = jnp.where((from_imag == 1) & (row // s.tile == 1), -1.0, 1.0)
    by_row = flip * jnp.where(from_imag == to_imag, cross, along)
    by_column = flip * jnp.where(from_imag == to_imag, cross, -along)

    def pieces(value):
        high = value.astype(BF16)
        return high, (value - high.astype(F32)).astype(BF16)

    for near, far, wa, wb in ((by_row, by_column, wa_s, wb_s), (by_column, by_row, wa_t, wb_t)):
        wb[:depth, :], wb[depth:, :] = pieces(far)
        for th in range(s.tiles):
            lanes = slice(th * s.tile, (th + 1) * s.tile)
            total = local_q[0:1, lanes] * near[:, : s.tile]
            for k in range(1, MODES):
                total = total + local_q[k : k + 1, lanes] * near[:, k * s.tile : (k + 1) * s.tile]
            wa[th, :depth, :], wa[th, depth:, :] = pieces(total)


def even_body(
    s,
    density,
    couplings,
    weight_real,
    weight_imag,
    mode_rates,
    tier_counts,
    link_index,
    link_mirror,
    block_diagonal,
    block_outer,
    block_column,
):
    planes, per_device, band, extent = density.shape
    group, row = lax.axis_index("aux"), lax.axis_index("row")
    device = group * s.rows + row
    cube = 2 * extent * extent * s.lanes
    state = shape(extent, s.lanes, dtype=BF16)
    full = shape(extent, s.lanes)
    pair = shape(2 * extent, s.lanes, dtype=BF16)
    held = pltpu.VMEM((extent, s.lanes), F32)
    held_b = pltpu.VMEM((extent, s.lanes), BF16)

    def exchange(message):
        sent = message.reshape(s.devices, -1, s.lanes)
        got = lax.all_to_all(sent, BOTH, split_axis=0, concat_axis=0, tiled=True)
        return got.reshape(-1, s.lanes)

    counts = counts_of_all(s, tier_counts, group)
    message = run(functools.partial(even_start_kernel, s), [pair], [density], scratch=[held_b], flops=2 * cube)[0]
    got = exchange(message)

    left, right, left_rows, right_rows = run(
        functools.partial(hamiltonian_kernel, s),
        [state] * 4,
        [block_diagonal, block_outer, block_column],
        scratch=[held_b],
        flops=4 * cube,
        scalars=(2,),
    )

    def in_lanes(by_mode):
        spread = jnp.broadcast_to(by_mode[:, None, :], (MODES, 2 * s.fold, s.auxes))
        return spread.reshape(1, MODES * s.tile)

    index = link_index.T.astype(F32)
    mirror = link_mirror.T.astype(F32)
    table = jnp.concatenate(
        [
            in_lanes(index[:MODES]),
            in_lanes(index[MODES:]),
            in_lanes(mirror[:MODES]),
            in_lanes(mirror[MODES:]),
            in_lanes((counts * weight_real[None, :]).T),
            in_lanes((counts * weight_imag[None, :]).T),
        ]
    )
    mine = lax.dynamic_slice_in_dim(couplings.reshape(MODES, s.local, s.devices), device, 1, 2)
    local_q = jnp.broadcast_to(mine, (MODES, s.local, s.za)).reshape(MODES, s.lanes)
    wa = shape(s.tiles, 4 * s.tile, s.tile, dtype=BF16)
    wb = shape(4 * s.tile, MODES * s.tile, dtype=BF16)
    wa_s, wb_s, wa_t, wb_t = run(
        functools.partial(weights_kernel, s), [wa, wb, wa, wb], [table, local_q]
    )
    damping = jnp.sum(counts * mode_rates[None, :], axis=1)
    damp = jnp.tile(damping, (planes * s.local,))[None, :]
    q_first = couplings.T

    k, n = iotas(s.lanes, s.lanes)
    parts = band // s.devices
    row_lanes = (
        n
        == (k // s.local % s.rows * parts + k % parts) * s.za
        + k // (parts * per_device) % planes * s.auxes
        + k // (s.local * s.rows) * per_device
        + k // parts % per_device
    ).astype(BF16)
    column_lanes = (
        n
        == k % s.local * s.za
        + k // (s.local * s.groups * per_device) * s.auxes
        + k // s.local % s.groups * per_device
        + k // (s.local * s.groups) % per_device
    ).astype(BF16)

    k, n = iotas(s.tile, s.tile)
    sign = jnp.where(n // s.auxes % 2 == 0, 1.0, -1.0)
    unit = jnp.where(k // s.za * s.za + (k + s.auxes) % s.za == n, sign, 0.0).astype(BF16)
    k, n = iotas(s.fold * s.tile, s.fold * s.tile)
    sign = jnp.where(n // s.auxes % 2 == 0, 1.0, -1.0)
    there = (k // s.za % s.fold * s.fold + k // s.tile) * s.za + (k + s.auxes) % s.za
    swap = jnp.where(there == n, sign, 0.0).astype(BF16)
    size = max(256, 16 * s.local)
    span = size // s.local
    k, n = iotas(size, size)
    order = (n == k % span * s.local + k // span).astype(BF16)

    s_now, t_now, message = run(
        functools.partial(even_take_kernel, s),
        [state, state, pair],
        [got, row_lanes, column_lanes, right_rows, left_rows],
        flops=4 * cube,
    )
    start_s, start_t = s_now, t_now
    ys, yt = s_now, t_now
    total = None
    shares = [STEP / 6.0, STEP / 3.0, STEP / 3.0, STEP / 6.0]
    steps = [0.25, 0.25, 0.5]
    for section in range(4):
        columns = section < 3
        if columns:
            got = exchange(message)
        slopes = run(
            functools.partial(slope_kernel, s, columns),
            [full, full] if columns else [full],
            [s_now, t_now, ys, yt, damp, q_first, right, left, unit, wa_s, wb_s, wa_t, wb_t],
            scratch=[held_b],
            flops=(12 if columns else 6) * cube,
        )
        if columns:
            args = [got, order, swap, right_rows, left_rows, *slopes, start_s, start_t]
            if total is not None:
                args.append(total)
            outs = [state, state, full, full, full]
            more = section < 2
            if more:
                outs.append(pair)
            s_now, t_now, ys, yt, total, *message = run(
                functools.partial(next_kernel, s, shares[section], steps[section], total is not None, more, 1),
                outs,
                args,
                scratch=[held],
                flops=6 * cube,
            )
            message = message[0] if more else None
    message = run(
        functools.partial(even_last_kernel, s, shares[3]),
        [pair],
        [slopes[0], total, t_now, left, unit, row_lanes, column_lanes],
        scratch=[held_b, held_b],
        flops=3 * cube,
    )[0]
    got = exchange(message)
    return run(
        functools.partial(even_finish_kernel, s),
        [shape(planes, per_device, band, extent)],
        [got, density],
        scratch=[held_b, held_b],
        flops=2 * cube,
    )[0]


def body(density, *others):
    planes, per_device, band, extent = density.shape
    s = Sizes(lax.axis_size("aux"), lax.axis_size("row"), per_device, band, extent)
    even = band % s.devices == 0 and s.local % 16 == 0 and LANES % s.za == 0
    if even and s.lanes == extent and planes * per_device * band == extent:
        return even_body(s, density, *others)
    return general_body(density, *others)


def solution(mesh):
    return jax.shard_map(
        body,
        mesh=mesh,
        in_specs=(
            P(None, "aux", "row", None),
            P(),
            P(),
            P(),
            P(),
            P("aux", None),
            P(),
            P(),
            P(),
            P(),
            P(),
        ),
        out_specs=P(None, "aux", "row", None),
        check_vma=False,
    )
```

profile of v0, /device:TPU:0, one launch (start us, length us, event | category | flops | bytes accessed | tf_op | source)
XLA Modules:
  0.0 231.6 jit_solution(12385992042305932594)
XLA Ops:
  1.2 2.9 %collective-permute-start = (f32[16,4]{1,0:T(8,128)}, f32[16,4]{1,0:T(8,128)}, u32[]{:S(2)}, u32[]{:S(2)}) collective-permute-start(f32[16,4]{1,0:T(8,128)} %convert_dynamic-update-slice_fusion), channel_id=1, source_target_pairs={{0,4},{4,0},{8,12},{12,8},{16,20},{20,16},{24,28},{28,24},{1,5},{5... | collective-permute-start | bytes 776 | tf_op jit(solution)/shard_map/ppermute | solution.py:475
  4.2 1.2 copy-done
  5.4 2.1 shard_map.109
  7.5 5.1 %all-to-all-start = ((bf16[32,32,512]{2,1,0:T(8,128)(2,1)}), bf16[32,32,512]{2,1,0:T(8,128)(2,1)}, u32[]{:S(2)}, u32[]{:S(2)}) async-start(bf16[32,32,512]{2,1,0:T(8,128)(2,1)} %bitcast), calls=%async_computation | async-start | bytes 2097152 | tf_op jit(solution)/shard_map/all_to_all | solution.py:641
  13.5 2.6 %shard_map.110 = (bf16[512,512]{1,0:T(8,128)(2,1)S(1)}, bf16[512,512]{1,0:T(8,128)(2,1)S(1)}, bf16[512,512]{1,0:T(8,128)(2,1)S(1)}, bf16[512,512]{1,0:T(8,128)(2,1)S(1)}) custom-call(bf16[8,64,64]{2,1,0:T(8,128)(2,1)S(1)} %copy-done.68, bf16[8,64,64]{2,1,0:T(8,128)(2,1)S(1)} %copy-done.69, s32[8]{0:T(128)S(1)} %copy-done.70), custom_call_target="tpu_custom_call" | custom-call | flops 1073741824 | bytes 2228256 | tf_op jit(solution)/shard_map/pallas_call | solution.py:44
  19.0 1.2 fusion.24.column_lanes
  20.2 1.4 fusion.25.row_lanes
  21.7 17.1 %all-to-all-done = bf16[32,32,512]{2,1,0:T(8,128)(2,1)} async-done(((bf16[32,32,512]{2,1,0:T(8,128)(2,1)}), bf16[32,32,512]{2,1,0:T(8,128)(2,1)}, u32[]{:S(2)}, u32[]{:S(2)}) %all-to-all-start) | async-done | bytes 1048608 | tf_op jit(solution)/shard_map/all_to_all | solution.py:641
  38.8 2.6 %shard_map.111 = (bf16[512,512]{1,0:T(8,128)(2,1)S(1)}, bf16[512,512]{1,0:T(8,128)(2,1)S(1)}, bf16[1024,512]{1,0:T(8,128)(2,1)S(1)}) custom-call(bf16[1024,512]{1,0:T(8,128)(2,1)} %bitcast.1.got_ref, bf16[512,512]{1,0:T(8,128)(2,1)S(1)} %fusion.25.row_lanes, bf16[512,512]{1,0:T(8,128)(2,1)S(1)} %fusion.24.column_lanes, ...), custom_call_target="tpu_custom_call" | custom-call | flops 1073741824 | bytes 5242880 | tf_op jit(solution)/shard_map/pallas_call | solution.py:44
  44.0 3.9 %all-to-all-start.1 = ((bf16[32,32,512]{2,1,0:T(8,128)(2,1)}), bf16[32,32,512]{2,1,0:T(8,128)(2,1)}, u32[]{:S(2)}, u32[]{:S(2)}) async-start(bf16[32,32,512]{2,1,0:T(8,128)(2,1)} %bitcast.28), calls=%async_computation.1 | async-start | bytes 2097152 | tf_op jit(solution)/shard_map/all_to_all | solution.py:641
  52.7 1.3 add_dynamic-update-slice_fusion
  54.0 1.5 collective-permute-start.1
  57.5 8.0 %collective-permute-done.1 = f32[16,4]{1,0:T(8,128)} collective-permute-done((f32[16,4]{1,0:T(8,128)}, f32[16,4]{1,0:T(8,128)}, u32[]{:S(2)}, u32[]{:S(2)}) %collective-permute-start.1) | collective-permute-done | bytes 288 | tf_op jit(solution)/shard_map/ppermute | solution.py:475
  65.5 1.3 add.264
  66.8 4.6 %collective-permute-start.2 = (f32[16,4]{1,0:T(8,128)}, f32[16,4]{1,0:T(8,128)}, u32[]{:S(2)}, u32[]{:S(2)}) collective-permute-start(f32[16,4]{1,0:T(8,128)} %add.264), channel_id=1, source_target_pairs={{0,16},{4,20},{8,24},{12,28},{16,0},{20,4},{24,8},{28,12},{1,17},{... | collective-permute-start | bytes 776 | tf_op jit(solution)/shard_map/ppermute | solution.py:475
  73.6 1.4 reshape.75.local_q
  75.0 1.4 multiply_bitcast_fusion
  84.6 1.0 copy-done.9
  85.6 1.0 copy-done.14
  86.7 1.0 copy-done.34
  87.7 4.6 %shard_map.113 = (f32[512,512]{1,0:T(8,128)S(1)}, f32[512,512]{1,0:T(8,128)S(1)}) custom-call(bf16[512,512]{1,0:T(8,128)(2,1)S(1)} %copy-done.9, bf16[512,512]{1,0:T(8,128)(2,1)S(1)} %copy-done.14, bf16[512,512]{1,0:T(8,128)(2,1)S(1)} %copy-done.9, bf16[512,512]{1,0:T(8,128)(2,1)S(1)} %copy-done.14, f32[1,512]{1,0:T(1,128)S(1)} %copy-done.59, ...), custom_call_target="tpu_custom_call" | custom-call | flops 3221225472 | bytes 7383040 | tf_op jit(solution)/shard_map/pallas_call | solution.py:44
  98.6 1.0 copy-done.15
  99.6 1.2 copy-done.76
  100.9 1.2 copy-done.78
  102.1 3.5 %shard_map.114 = (bf16[512,512]{1,0:T(8,128)(2,1)S(1)}, bf16[512,512]{1,0:T(8,128)(2,1)S(1)}, f32[512,512]{1,0:T(8,128)S(1)}, f32[512,512]{1,0:T(8,128)S(1)}, f3...) custom-call(bf16[1024,512]{1,0:T(8,128)(2,1)} %bitcast.3.refs_0_, bf16[256,256]{1,0:T(8,128)(2,1)S(1)} %fusion.26.refs_1_, ...), custom_call_target="tpu_custom_call" | custom-call | flops 1610612736 | bytes 11141120 | tf_op jit(solution)/shard_map/pallas_call | solution.py:44
  111.1 3.7 %all-to-all-start.2 = ((bf16[32,32,512]{2,1,0:T(8,128)(2,1)}), bf16[32,32,512]{2,1,0:T(8,128)(2,1)S(1)}, u32[]{:S(2)}, u32[]{:S(2)}) async-start(bf16[32,32,512]{2,1,0:T(8,128)(2,1)} %bitcast.30), calls=%async_computation.2 | async-start | bytes 2097152 | tf_op jit(solution)/shard_map/all_to_all | solution.py:641
  115.8 1.0 copy-done.39
  116.8 1.0 copy-done.43
  117.9 1.0 copy-done.47
  118.9 1.0 copy-done.51
  120.7 1.2 copy-done.72
  121.9 1.2 copy-done.74
  123.2 1.0 copy-done.80
  124.2 1.0 copy-done.82
  125.2 4.6 %shard_map.115 = (f32[512,512]{1,0:T(8,128)S(1)}, f32[512,512]{1,0:T(8,128)S(1)}) custom-call(bf16[512,512]{1,0:T(8,128)(2,1)S(1)} %copy-done.80, bf16[512,512]{1,0:T(8,128)(2,1)S(1)} %copy-done.82, f32[512,512]{1,0:T(8,128)S(1)} %copy-done.72, f32[512,512]{1,0:T(8,128)S(1)} %copy-done.74, f32[1,512]{1,0:T(1,128)S(1)} %copy-done.59, f32[512,4]{1,0:T(8,128)S(1)} %bitcast.25, ...), custom_call_target="tpu_custom_call" | custom-call | flops 3221225472 | bytes 8431616 | tf_op jit(solution)/shard_map/pallas_call | solution.py:44
  131.8 9.0 %all-to-all-done.2 = bf16[32,32,512]{2,1,0:T(8,128)(2,1)S(1)} async-done(((bf16[32,32,512]{2,1,0:T(8,128)(2,1)}), bf16[32,32,512]{2,1,0:T(8,128)(2,1)S(1)}, u32[]{:S(2)}, u32[]{:S(2)}) %all-to-all-start.2) | async-done | bytes 1048608 | tf_op jit(solution)/shard_map/all_to_all | solution.py:641
  140.8 1.0 copy-done.3
  141.8 1.0 copy-done.6
  142.8 1.0 copy-done.11
  143.9 1.0 copy-done.16
  144.9 1.2 copy-done.24
  146.2 1.2 copy-done.30
  147.4 1.2 copy-done.32
  148.6 2.4 %shard_map.116 = (bf16[512,512]{1,0:T(8,128)(2,1)S(1)}, bf16[512,512]{1,0:T(8,128)(2,1)S(1)}, f32[512,512]{1,0:T(8,128)S(1)}, f32[512,512]{1,0:T(8,128)S(1)}, f3...) custom-call(bf16[1024,512]{1,0:T(8,128)(2,1)S(1)} %bitcast.23, bf16[256,256]{1,0:T(8,128)(2,1)S(1)} %fusion.26.refs_1_, ...), custom_call_target="tpu_custom_call" | custom-call | flops 1610612736 | bytes 12189696 | tf_op jit(solution)/shard_map/pallas_call | solution.py:44
  156.5 3.9 %all-to-all-start.3 = ((bf16[32,32,512]{2,1,0:T(8,128)(2,1)}), bf16[32,32,512]{2,1,0:T(8,128)(2,1)S(1)}, u32[]{:S(2)}, u32[]{:S(2)}) async-start(bf16[32,32,512]{2,1,0:T(8,128)(2,1)} %bitcast.29), calls=%async_computation.3 | async-start | bytes 2097152 | tf_op jit(solution)/shard_map/all_to_all | solution.py:641
  161.4 1.0 copy-done.40
  162.5 1.0 copy-done.44
  163.5 1.0 copy-done.48
  166.3 1.2 copy-done.61
  167.6 1.2 copy-done.63
  168.8 1.0 copy-done.65
  170.9 4.6 %shard_map.117 = (f32[512,512]{1,0:T(8,128)S(1)}, f32[512,512]{1,0:T(8,128)S(1)}) custom-call(bf16[512,512]{1,0:T(8,128)(2,1)S(1)} %copy-done.65, bf16[512,512]{1,0:T(8,128)(2,1)S(1)} %copy-done.67, f32[512,512]{1,0:T(8,128)S(1)} %copy-done.61, f32[512,512]{1,0:T(8,128)S(1)} %copy-done.63, f32[1,512]{1,0:T(1,128)S(1)} %copy-done.59, f32[512,4]{1,0:T(8,128)S(1)} %bitcast.26, ...), custom_call_target="tpu_custom_call" | custom-call | flops 3221225472 | bytes 8431616 | tf_op jit(solution)/shard_map/pallas_call | solution.py:44
  177.4 8.9 %all-to-all-done.3 = bf16[32,32,512]{2,1,0:T(8,128)(2,1)S(1)} async-done(((bf16[32,32,512]{2,1,0:T(8,128)(2,1)}), bf16[32,32,512]{2,1,0:T(8,128)(2,1)S(1)}, u32[]{:S(2)}, u32[]{:S(2)}) %all-to-all-start.3) | async-done | bytes 1048608 | tf_op jit(solution)/shard_map/all_to_all | solution.py:641
  186.4 1.0 copy-done.4
  187.4 1.0 copy-done.7
  188.4 1.0 copy-done.12
  190.5 1.2 copy-done.22
  191.7 1.2 copy-done.26
  193.0 1.2 copy-done.28
  194.2 1.7 shard_map.118
  195.9 2.4 %shard_map.119.ks_ref = f32[512,512]{1,0:T(8,128)S(1)} custom-call(bf16[512,512]{1,0:T(8,128)(2,1)S(1)} %get-tuple-element.68.s_ref, bf16[512,512]{1,0:T(8,128)(2,1)S(1)} %get-tuple-element.69.t_ref, f32[512,512]{1,0:T(8,128)S(1)} %get-tuple-element.70.ys_ref, f32[512,512]{1,0:T(8,128)S(1)} %get-tuple-element.71.yt_ref, f32[1,512]{1,0:T(1,128)S(1)} %copy-done.59, ...), custom_call_target="tpu_custom_call" | custom-call | flops 1610612736 | bytes 7383040 | tf_op jit(solution)/shard_map/pallas_call | solution.py:44
  198.3 1.8 shard_map.120
  200.1 29.7 %all_to_all.25 = bf16[32,32,512]{2,1,0:T(8,128)(2,1)S(1)} all-to-all(bf16[32,32,512]{2,1,0:T(8,128)(2,1)S(1)} %bitcast.20), channel_id=1, replica_groups=mesh['aux'=8,'row'=4] {'aux','row'}, dimensions={0} | all-to-all | bytes 2097152 | tf_op jit(solution)/shard_map/all_to_all | solution.py:641
  229.8 1.8 shard_map.121
  (204 shorter events, 52.6 us)
Async XLA Ops:
  1.2 51.5 %collective-permute-start = (f32[16,4]{1,0:T(8,128)}, f32[16,4]{1,0:T(8,128)}, u32[]{:S(2)}, u32[]{:S(2)}) collective-permute-start(f32[16,4]{1,0:T(8,128)} %convert_dynamic-update-slice_fusion), channel_id=1, source_target_pairs={{0,4},{4,0},{8,12},{12,8},{16,20},{20,16},{24,28},{28,24},{1,5},{5... | collective-permute-start | bytes 776 | tf_op jit(solution)/shard_map/ppermute | solution.py:475
  4.2 1.2 copy-start
  7.5 5.3 %copy-start.68 = (bf16[8,64,64]{2,1,0:T(8,128)(2,1)S(1)}, bf16[8,64,64]{2,1,0:T(8,128)(2,1)}, u32[]{:S(2)}) copy-start(bf16[8,64,64]{2,1,0:T(8,128)(2,1)} %own_ref.1) | copy-start | bytes 196612
  7.5 5.3 %copy-start.69 = (bf16[8,64,64]{2,1,0:T(8,128)(2,1)S(1)}, bf16[8,64,64]{2,1,0:T(8,128)(2,1)}, u32[]{:S(2)}) copy-start(bf16[8,64,64]{2,1,0:T(8,128)(2,1)} %outer_ref.1) | copy-start | bytes 196612
  7.5 31.3 %all-to-all-start = ((bf16[32,32,512]{2,1,0:T(8,128)(2,1)}), bf16[32,32,512]{2,1,0:T(8,128)(2,1)}, u32[]{:S(2)}, u32[]{:S(2)}) async-start(bf16[32,32,512]{2,1,0:T(8,128)(2,1)} %bitcast), calls=%async_computation | async-start | bytes 2097152 | tf_op jit(solution)/shard_map/all_to_all | solution.py:641
  16.9 80.7 %copy-start.2 = (bf16[512,512]{1,0:T(8,128)(2,1)}, bf16[512,512]{1,0:T(8,128)(2,1)S(1)}, u32[]{:S(2)}) copy-start(bf16[512,512]{1,0:T(8,128)(2,1)S(1)} %get-tuple-element.40.left_rows.refs_4_) | copy-start | bytes 1572868
  16.9 80.7 %copy-start.5 = (bf16[512,512]{1,0:T(8,128)(2,1)}, bf16[512,512]{1,0:T(8,128)(2,1)S(1)}, u32[]{:S(2)}) copy-start(bf16[512,512]{1,0:T(8,128)(2,1)S(1)} %get-tuple-element.39.right_rows.refs_3_) | copy-start | bytes 1572868
  44.0 53.5 %all-to-all-start.1 = ((bf16[32,32,512]{2,1,0:T(8,128)(2,1)}), bf16[32,32,512]{2,1,0:T(8,128)(2,1)}, u32[]{:S(2)}, u32[]{:S(2)}) async-start(bf16[32,32,512]{2,1,0:T(8,128)(2,1)} %bitcast.28), calls=%async_computation.1 | async-start | bytes 2097152 | tf_op jit(solution)/shard_map/all_to_all | solution.py:641
  52.7 2.8 %copy-start.85 = (f32[4,16]{1,0:T(4,128)S(1)}, f32[4,16]{1,0:T(4,128)}, u32[]{:S(2)}) copy-start(f32[4,16]{1,0:T(4,128)} %get-tuple-element.78) | copy-start | bytes 772
  54.0 11.5 %collective-permute-start.1 = (f32[16,4]{1,0:T(8,128)}, f32[16,4]{1,0:T(8,128)}, u32[]{:S(2)}, u32[]{:S(2)}) collective-permute-start(f32[16,4]{1,0:T(8,128)} %add_dynamic-update-slice_fusion), channel_id=1, source_target_pairs={{0,8},{4,12},{8,0},{12,4},{16,24},{20,28},{24,16},{28,20},{1,9},{5... | collective-permute-start | bytes 776 | tf_op jit(solution)/shard_map/ppermute | solution.py:475
  65.5 5.9 %copy-start.84 = (f32[4,16]{1,0:T(4,128)S(1)}, f32[4,16]{1,0:T(4,128)}, u32[]{:S(2)}) copy-start(f32[4,16]{1,0:T(4,128)} %get-tuple-element.79) | copy-start | bytes 772
  66.8 8.2 %collective-permute-start.2 = (f32[16,4]{1,0:T(8,128)}, f32[16,4]{1,0:T(8,128)}, u32[]{:S(2)}, u32[]{:S(2)}) collective-permute-start(f32[16,4]{1,0:T(8,128)} %add.264), channel_id=1, source_target_pairs={{0,16},{4,20},{8,24},{12,28},{16,0},{20,4},{24,8},{28,12},{1,17},{... | collective-permute-start | bytes 776 | tf_op jit(solution)/shard_map/ppermute | solution.py:475
  84.6 1.0 copy-start.9
  85.6 1.0 copy-start.14
  86.7 1.0 copy-start.34
  97.5 1.0 copy-start.10
  98.6 1.0 copy-start.15
  99.6 1.2 copy-start.76
  100.9 1.2 copy-start.78
  106.5 1.0 copy-start.23
  111.1 29.7 %all-to-all-start.2 = ((bf16[32,32,512]{2,1,0:T(8,128)(2,1)}), bf16[32,32,512]{2,1,0:T(8,128)(2,1)S(1)}, u32[]{:S(2)}, u32[]{:S(2)}) async-start(bf16[32,32,512]{2,1,0:T(8,128)(2,1)} %bitcast.30), calls=%async_computation.2 | async-start | bytes 2097152 | tf_op jit(solution)/shard_map/all_to_all | solution.py:641
  114.7 1.0 copy-start.35
  115.8 1.0 copy-start.39
  116.8 1.0 copy-start.43
  117.9 1.0 copy-start.47
  118.9 1.0 copy-start.51
  120.7 1.2 copy-start.72
  121.9 1.2 copy-start.74
  123.2 1.0 copy-start.80
  124.2 1.0 copy-start.82
  129.8 1.0 copy-start.29
  140.8 1.0 copy-start.3
  141.8 1.0 copy-start.6
  142.8 1.0 copy-start.11
  143.9 1.0 copy-start.16
  144.9 1.2 copy-start.24
  146.2 1.2 copy-start.30
  147.4 1.2 copy-start.32
  151.9 1.0 copy-start.21
  156.5 29.9 %all-to-all-start.3 = ((bf16[32,32,512]{2,1,0:T(8,128)(2,1)}), bf16[32,32,512]{2,1,0:T(8,128)(2,1)S(1)}, u32[]{:S(2)}, u32[]{:S(2)}) async-start(bf16[32,32,512]{2,1,0:T(8,128)(2,1)} %bitcast.29), calls=%async_computation.3 | async-start | bytes 2097152 | tf_op jit(solution)/shard_map/all_to_all | solution.py:641
  160.4 1.0 copy-start.36
  161.4 1.0 copy-start.40
  162.5 1.0 copy-start.44
  163.5 1.0 copy-start.48
  164.5 1.0 copy-start.52
  166.3 1.2 copy-start.61
  167.6 1.2 copy-start.63
  168.8 1.0 copy-start.65
  169.8 1.0 copy-start.67
  175.4 1.0 copy-start.25
  186.3 1.0 copy-start.4
  187.4 1.0 copy-start.7
  188.4 1.0 copy-start.12
  189.5 1.0 copy-start.17
  190.5 1.2 copy-start.22
  191.7 1.2 copy-start.26
  193.0 1.2 copy-start.28
  194.2 1.7 copy-start.37
  194.2 1.7 copy-start.41
  194.2 1.7 copy-start.45
  194.2 1.7 copy-start.49
  194.2 1.7 copy-start.53
  194.2 1.7 copy-start.57
  200.1 29.7 %copy-start.1 = (f32[2,2,128,512]{3,2,1,0:T(8,128)S(1)}, f32[2,2,128,512]{3,2,1,0:T(8,128)}, u32[]{:S(2)}) copy-start(f32[2,2,128,512]{3,2,1,0:T(8,128)} %d_ref.3) | copy-start | bytes 3145732
  (33 other events, 27.4 us)
where the time goes:
time: 235 us; the launch traced here: 232 us
  local copies, waits for them, and re-layouts  88.1 us (37%)
  waiting for transfers between devices  43.1 us (18%)
  Pallas kernels  35.2 us (15%)
  blocking collectives  29.7 us (13%)
  starting transfers between devices  25.6 us (11%)
  other arithmetic  9.32 us (4%)
    unnamed x182, local copies, waits for them, and re-layouts  74.2 us
    pallas_call x13, Pallas kernels, run(): pl.pallas_call(kernel, out_shape=list(outs), in_specs=[flat if n in scala...  35.2 us
    all_to_all x4, waiting for transfers between devices, exchange(): got = lax.all_to_all(sent, BOTH, split_axis=0, concat_axis=0, tiled=True)  35.1 us
    all_to_all x1, blocking collectives, exchange(): got = lax.all_to_all(sent, BOTH, split_axis=0, concat_axis=0, tiled=True)  29.7 us
    all_to_all x4, starting transfers between devices, exchange(): got = lax.all_to_all(sent, BOTH, split_axis=0, concat_axis=0, tiled=True)  16.6 us
    ppermute x3, starting transfers between devices, counts_of_all(): lax.ppermute(whole, 'aux', [(i, i ^ step) for i in range(s.groups)])  9.01 us
    ppermute x3, waiting for transfers between devices, counts_of_all(): lax.ppermute(whole, 'aux', [(i, i ^ step) for i in range(s.groups)])  7.98 us
  transfers between devices with their start and end apart: 7, of which 4 were waited for; matrix products, arithmetic and copies ran while one was open for 10% of the time, Pallas kernels for 9%

commit v1 on v0

--- a/solution.py
+++ b/solution.py
@@ -464,19 +464,6 @@
     )[0]
 
 
-def counts_of_all(s, tier_counts, group):
-    if s.groups & (s.groups - 1):
-        return lax.all_gather(tier_counts, "aux", axis=0, tiled=True).astype(F32)
-    whole = lax.dynamic_update_slice_in_dim(
-        jnp.zeros((s.auxes, MODES), F32), tier_counts.astype(F32), group * s.per_device, 0
-    )
-    step = 1
-    while step < s.groups:
-        whole = whole + lax.ppermute(whole, "aux", [(i, i ^ step) for i in range(s.groups)])
-        step *= 2
-    return whole
-
-
 def iotas(rows, columns):
     return (
         lax.broadcasted_iota(jnp.int32, (rows, columns), 0),
@@ -484,85 +471,313 @@
     )
 
 
+def mask_to(value):
+    return value.astype(F32).astype(BF16)
+
+
 def post_matrix(s):
     row, column = iotas(s.extent, s.extent)
-    return (column == row % s.local * s.devices + row // s.local).astype(F32).astype(BF16)
-
-
-def place(s, message, part, first, value, lanes=slice(None)):
-    for k in range(value.shape[0] // s.local):
-        start = ((first // s.local + k) * 2 + part) * s.local
-        message[start : start + s.local, lanes] = value[k * s.local : (k + 1) * s.local, :]
-
-
-def even_start_kernel(s, d_ref, out_ref, post):
-    planes, number, band, extent = d_ref.shape
+    return mask_to(column == row % s.local * s.devices + row // s.local)
+
+
+class Stage:
+    def __init__(self, sources, buffers, targets, results, semaphores):
+        self.buffers, self.results, self.targets = buffers, results, targets
+        self.semaphores, self.next = semaphores, 0
+        self.coming = [self.copy(a, b) for a, b in zip(sources, buffers)]
+        self.going = []
+
+    def copy(self, source, target):
+        made = pltpu.make_async_copy(source, target, self.semaphores.at[self.next])
+        self.next += 1
+        made.start()
+        return made
+
+    def need(self, index):
+        if self.coming[index] is not None:
+            self.coming[index].wait()
+            self.coming[index] = None
+        return self.buffers[index]
+
+    def send(self, index):
+        self.going.append(self.copy(self.results[index], self.targets[index]))
+
+    def finish(self):
+        for made in self.going:
+            made.wait()
+
+
+def run_staged(body, outs, args, temporaries=(), scalars=(), flops=0):
+    arrays, views = [], []
+    for arg in args:
+        array, part = arg if isinstance(arg, tuple) else (arg, None)
+        if not any(array is a for a in arrays):
+            arrays.append(array)
+        views.append(([array is a for a in arrays].index(True), part))
+    shapes, places = [], []
+    for out in outs:
+        if isinstance(out, tuple):
+            for part in range(out[1]):
+                places.append((len(shapes), part))
+            shapes.append(out[0])
+        else:
+            places.append((len(shapes), None))
+            shapes.append(out)
+    tall = lambda x, part: x.shape if part is None else x.shape[:1] + x.shape[2:]
+    buffers = [pltpu.VMEM(tall(arrays[k], part), arrays[k].dtype) for k, part in views]
+    results = [pltpu.VMEM(tall(shapes[k], part), shapes[k].dtype) for k, part in places]
+    count = len(buffers) + len(results)
+
+    def kernel(*refs):
+        small, refs = refs[: len(scalars)], refs[len(scalars) :]
+        source, refs = refs[: len(arrays)], refs[len(arrays) :]
+        target, refs = refs[: len(shapes)], refs[len(shapes) :]
+        own, refs = refs[: len(buffers)], refs[len(buffers) :]
+        made, refs = refs[: len(results)], refs[len(results) :]
+        pick = lambda ref, part: ref if part is None else ref.at[:, part]
+        stage = Stage(
+            [pick(source[k], part) for k, part in views],
+            own,
+            [pick(target[k], part) for k, part in places],
+            made,
+            refs[-1],
+        )
+        body(stage, small, refs[:-1])
+        stage.finish()
+
+    moved = sum(a.size * a.dtype.itemsize for a in arrays)
+    moved += sum(o.size * o.dtype.itemsize for o in shapes)
+    far = pl.BlockSpec(memory_space=pltpu.HBM)
+    return pl.pallas_call(
+        kernel,
+        out_shape=shapes,
+        in_specs=[pl.BlockSpec(memory_space=pltpu.SMEM)] * len(scalars) + [far] * len(arrays),
+        out_specs=[far] * len(shapes),
+        scratch_shapes=buffers + results + list(temporaries) + [pltpu.SemaphoreType.DMA((count,))],
+        compiler_params=pltpu.CompilerParams(vmem_limit_bytes=48 << 20),
+        cost_estimate=pl.CostEstimate(flops=flops, bytes_accessed=moved, transcendentals=0),
+    )(*scalars, *arrays)
+
+
+def fill(s, result, first, value, lanes=slice(None)):
+    count = value.shape[0] // s.local
+    device = first // s.local
+    result[device : device + count, :, lanes] = value.reshape(count, s.local, value.shape[1])
+
+
+def flat_rows(ref, rows, lanes=slice(None)):
+    piece = ref[rows, :, lanes]
+    return piece.reshape(piece.shape[0] * piece.shape[1], piece.shape[2])
+
+
+def even_start(s, stage, small, temporaries):
+    (counts,) = small
+    (post,) = temporaries
     post[...] = post_matrix(s)
-    flat = d_ref[...].reshape(planes * number * band, extent).astype(BF16)
-    for b in row_blocks(extent):
-        place(s, out_ref, 0, b, dot(post[b : b + 128, :], flat).astype(BF16))
-        place(s, out_ref, 1, b, dot(post[b : b + 128, :], flat, ((1,), (1,))).astype(BF16))
-
-
-def part_rows(s, got_ref, part, devices, lanes=slice(None)):
-    pieces = [
-        got_ref[(d * 2 + part) * s.local : (d * 2 + part + 1) * s.local, lanes] for d in devices
-    ]
-    return jnp.concatenate(pieces, axis=0)
-
-
-def even_take_kernel(s, got_ref, row_lanes, column_lanes, right_rows, left_rows, s_ref, t_ref, message):
-    everyone = range(s.devices)
+    blocks = s.extent // s.band
+    which = lax.axis_index("row") % s.per_device
+    flats = [stage.need(v)[...].reshape(s.band, s.extent).astype(BF16) for v in range(blocks)]
+    row, lane = iotas(128, s.band)
+    for v in range(blocks):
+        count = counts[which, v].astype(F32)
+        for b in row_blocks(s.extent):
+            value = dot(post[b : b + 128, :], flats[v], ((1,), (1,)))
+            own = (row % s.local == 0) & (lane == (row + b) // s.local)
+            value = jnp.where(own, count, value).astype(BF16)
+            fill(s, stage.results[1], b, value, slice(v * s.band, (v + 1) * s.band))
+    stage.send(1)
+    flat = jnp.concatenate(flats, axis=0)
+    for b in row_blocks(s.extent):
+        fill(s, stage.results[0], b, dot(post[b : b + 128, :], flat).astype(BF16))
+    stage.send(0)
+
+
+def send_products(s, stage, matrix, state_ref, index):
+    for b in row_blocks(s.extent):
+        fill(s, stage.results[index], b, dot(matrix[b : b + 128, :], state_ref[...]).astype(BF16))
+    stage.send(index)
+
+
+def even_take(s, stage, small, temporaries):
+    s_ref, t_ref, counts_ref = stage.results[2], stage.results[3], stage.results[4]
+    me = lax.axis_index("aux") * s.rows + lax.axis_index("row")
+    everyone = slice(0, s.devices)
+    rows_in, row_lanes = stage.need(0), stage.need(1)
     for b in row_blocks(s.extent):
         s_ref[b : b + 128, :] = dot(
-            part_rows(s, got_ref, 0, everyone, slice(b, b + 128)), row_lanes[...], ((0,), (0,))
+            flat_rows(rows_in, everyone, slice(b, b + 128)), row_lanes[...], ((0,), (0,))
         ).astype(BF16)
+    stage.send(2)
+    send_products(s, stage, stage.need(2), s_ref, 1)
+    columns_in, column_lanes = stage.need(3), stage.need(4)
+    blocks = s.extent // s.band
+    parts = s.band // s.devices
+    row, lane = iotas(s.devices, s.tile)
+    mine = (row == me) & (lane < s.za)
     for q in range(s.rows):
-        owners = [g * s.rows + q for g in range(s.groups)]
-        pieces = [
-            part_rows(s, got_ref, 1, owners, slice(v * s.band, (v + 1) * s.band))
-            for v in range(s.extent // s.band)
-        ]
+        pieces = []
+        for v in range(blocks):
+            for g in range(s.groups):
+                pieces.append(columns_in[g * s.rows + q, :, v * s.band : (v + 1) * s.band])
         t_ref[q * s.band : (q + 1) * s.band, :] = dot(
             jnp.concatenate(pieces, axis=0), column_lanes[...], ((0,), (0,))
         ).astype(BF16)
-    write_messages(s, right_rows, left_rows, s_ref, t_ref, [message])
-
-
-def even_last_kernel(s, weight, ks_ref, total_in, t_ref, left, unit, row_lanes, column_lanes, out_ref, grown, turned):
+        rows = slice(q * s.band, q * s.band + s.devices)
+        first = q * parts * s.za
+        kept = s_ref[: s.devices, first : first + s.tile].astype(F32)
+        t_ref[rows, : s.tile] = jnp.where(mine, kept, t_ref[rows, : s.tile].astype(F32)).astype(BF16)
+    stage.send(3)
+    send_products(s, stage, stage.need(5), t_ref, 0)
+    row, lane = iotas(s.extent, MODES)
+    gather = mask_to(row == lane * s.band + me)
+    row, lane = iotas(s.auxes, s.per_device * s.groups * s.local)
+    wanted = mask_to(lane == row * s.local)
+    pieces = [columns_in[a // s.per_device * s.rows + a % s.per_device] for a in range(s.auxes)]
+    counts_ref[...] = dot(wanted, dot(jnp.concatenate(pieces, axis=0), gather).astype(BF16))
+    stage.send(4)
+
+
+def even_turn(s, got_ref, order, swap, arrived):
+    def load(start, size):
+        return flat_rows(got_ref, slice(start // s.local, (start + size) // s.local))
+
+    def put(rows, lanes, value):
+        arrived[rows, lanes] = value
+
+    turn(s, load, order, swap, put)
+
+
+def even_next(s, weight, step, has_total, stage, small, temporaries):
+    (arrived,) = temporaries
+    s_ref, t_ref, ys_ref, yt_ref, total_ref = stage.results[2:7]
+    got_s, order, swap = stage.need(0), stage.need(1), stage.need(2)
+    even_turn(s, got_s, order, swap, arrived)
+    ks_ref, ds_ref = stage.need(3), stage.need(4)
+    total_in = stage.need(10) if has_total else None
+    for b in row_blocks(s.extent, 64):
+        rows = slice(b, b + 64)
+        slope = ks_ref[rows, :] + arrived[rows, :]
+        grown = weight * slope
+        total_ref[rows, :] = total_in[rows, :] + grown if has_total else grown
+        state = ds_ref[rows, :].astype(F32) + step * slope
+        ys_ref[rows, :] = state
+        s_ref[rows, :] = state.astype(BF16)
+    for index in (2, 4, 6):
+        stage.send(index)
+    send_products(s, stage, stage.need(5), s_ref, 1)
+    even_turn(s, stage.need(6), order, swap, arrived)
+    kt_ref, dt_ref = stage.need(7), stage.need(8)
+    for b in row_blocks(s.extent, 64):
+        rows = slice(b, b + 64)
+        slope = kt_ref[rows, :] - arrived[rows, :]
+        state = dt_ref[rows, :].astype(F32) + step * slope
+        yt_ref[rows, :] = state
+        t_ref[rows, :] = state.astype(BF16)
+    stage.send(3)
+    stage.send(5)
+    send_products(s, stage, stage.need(9), t_ref, 0)
+
+
+def even_slope_part(s, direct, mirror, y_ref, h, unit, damp, q_ref, wa, wb, turned, sign, put):
+    for th in range(s.tiles):
+        lanes = slice(th * s.tile, (th + 1) * s.tile)
+        turned[:, lanes] = dot(direct[:, lanes], unit[...]).astype(BF16)
+    for b in row_blocks(s.extent):
+        rows = slice(b, b + 128)
+        whole = dot(h[rows, :], turned[...])
+        for th in range(s.tiles):
+            lanes = slice(th * s.tile, (th + 1) * s.tile)
+            source = jnp.concatenate([direct[rows, lanes], mirror[rows, lanes]], axis=1)
+            source = jnp.concatenate([source, source], axis=1)
+            total = dot(source, wa[th]) - damp[:, lanes] * y_ref[rows, lanes].astype(F32)
+            total = total + sign * whole[:, lanes]
+            fields = dot(source, wb[...])
+            for k in range(MODES):
+                total = total + q_ref[rows, k : k + 1] * fields[:, k * s.tile : (k + 1) * s.tile]
+            put(rows, lanes, total)
+
+
+def even_slope(s, stage, small, temporaries):
+    (turned,) = temporaries
+
+    def put_in(index):
+        def put(rows, lanes, value):
+            stage.results[index][rows, lanes] = value
+
+        return put
+
+    need = stage.need
+    unit, damp, q_ref = need(4), need(5), need(6)
+    even_slope_part(
+        s, need(0), need(1), need(2), need(7), unit, damp, q_ref, need(8), need(9), turned, -1.0, put_in(0)
+    )
+    stage.send(0)
+    even_slope_part(
+        s, need(1), need(0), need(3), need(10), unit, damp, q_ref, need(11), need(12), turned, 1.0, put_in(1)
+    )
+    stage.send(1)
+
+
+def even_last(s, step, weight_three, weight_four, stage, small, temporaries):
+    arrived, s_ref, t_ref, grown, turned, base = temporaries
+    need = stage.need
+    order, swap = need(1), need(2)
+    even_turn(s, need(0), order, swap, arrived)
+    kt_ref, dt_ref = need(3), need(4)
+    for b in row_blocks(s.extent, 64):
+        rows = slice(b, b + 64)
+        slope = kt_ref[rows, :] - arrived[rows, :]
+        t_ref[rows, :] = (dt_ref[rows, :].astype(F32) + step * slope).astype(BF16)
+    unit, left, column_lanes = need(5), need(6), need(7)
     for th in range(s.tiles):
         lanes = slice(th * s.tile, (th + 1) * s.tile)
         turned[:, lanes] = dot(t_ref[:, lanes], unit[...]).astype(BF16)
     for b in row_blocks(s.extent):
         rows = slice(b, b + 128)
-        grown[rows, :] = (total_in[rows, :] + weight * ks_ref[rows, :]).astype(BF16)
-    for b in row_blocks(s.extent):
-        place(s, out_ref, 0, b, dot(row_lanes[b : b + 128, :], grown[...], ((1,), (1,))).astype(BF16))
-    for b in row_blocks(s.extent):
-        rows = slice(b, b + 128)
-        grown[rows, :] = (weight * dot(left[rows, :], turned[...])).astype(BF16)
+        grown[rows, :] = (weight_four * dot(left[rows, :], turned[...])).astype(BF16)
+    out = stage.results[1]
     for q in range(s.rows):
         value = dot(column_lanes[...], grown[q * s.band : (q + 1) * s.band, :], ((1,), (1,))).astype(BF16)
         for v in range(s.extent // s.band):
             for g in range(s.groups):
                 at = (v * s.groups + g) * s.local
-                start = ((g * s.rows + q) * 2 + 1) * s.local
-                out_ref[start : start + s.local, v * s.band : (v + 1) * s.band] = value[at : at + s.local, :]
-
-
-def even_finish_kernel(s, got_ref, d_ref, out_ref, post, moved):
-    planes, number, band, extent = d_ref.shape
+                out[g * s.rows + q, :, v * s.band : (v + 1) * s.band] = value[at : at + s.local, :]
+    stage.send(1)
+    even_turn(s, need(8), order, swap, arrived)
+    ks_ref, ds_ref, total_in = need(9), need(10), need(11)
+    for b in row_blocks(s.extent, 64):
+        rows = slice(b, b + 64)
+        slope = ks_ref[rows, :] + arrived[rows, :]
+        base[rows, :] = total_in[rows, :] + weight_three * slope
+        state = ds_ref[rows, :].astype(F32) + step * slope
+        arrived[rows, :] = state
+        s_ref[rows, :] = state.astype(BF16)
+
+    def put(rows, lanes, value):
+        grown[rows, lanes] = (base[rows, lanes] + weight_four * value).astype(BF16)
+
+    even_slope_part(
+        s, s_ref, t_ref, arrived, need(14), unit, need(12), need(13), need(15), need(16), turned, -1.0, put
+    )
+    row_lanes = need(17)
+    for b in row_blocks(s.extent):
+        fill(s, stage.results[0], b, dot(row_lanes[b : b + 128, :], grown[...], ((1,), (1,))).astype(BF16))
+    stage.send(0)
+
+
+def even_finish(s, stage, small, temporaries):
+    (post,) = temporaries
     post[...] = post_matrix(s)
-    everyone = range(s.devices)
-    for d in everyone:
-        moved[d * s.local : (d + 1) * s.local, :] = got_ref[d * 2 * s.local : (d * 2 + 1) * s.local, :]
-    for z in range(planes):
-        for n in range(number):
-            at = (z * number + n) * band
-            lanes = slice(at, at + band)
-            change = dot(post[:, lanes], moved[...], ((0,), (0,)))
-            change = change + dot(part_rows(s, got_ref, 1, everyone, lanes), post[...], ((0,), (0,)))
-            out_ref[z, n] = d_ref[z, n] + change
+    everyone = slice(0, s.devices)
+    rows_in, columns_in = stage.need(0), stage.need(1)
+    for v in range(s.extent // s.band):
+        lanes = slice(v * s.band, (v + 1) * s.band)
+        change = dot(post[:, lanes], flat_rows(rows_in, everyone), ((0,), (0,)))
+        change = change + dot(flat_rows(columns_in, everyone, lanes), post[...], ((0,), (0,)))
+        stage.results[v][...] = (stage.need(2 + v)[...].reshape(s.band, s.extent) + change).reshape(
+            stage.results[v].shape
+        )
+        stage.send(v)
 
 
 def hamiltonian_kernel(s, own_ref, outer_ref, where_ref, left, right, left_rows, right_rows, post):
@@ -571,11 +786,11 @@
     row, column = iotas(block, s.extent)
     for b in range(blocks):
         spread = column - row
-        to_own = (spread == b * block).astype(F32).astype(BF16)
-        to_far = (spread == where_ref[b] * block).astype(F32).astype(BF16)
+        to_own = mask_to(spread == b * block)
+        to_far = mask_to(spread == where_ref[b] * block)
         left[b * block : (b + 1) * block, :] = (dot(own_ref[b], to_own) + dot(outer_ref[b], to_far)).astype(BF16)
     row, column = iotas(s.extent, s.extent)
-    same = (row == column).astype(F32).astype(BF16)
+    same = mask_to(row == column)
     for b in row_blocks(s.extent):
         rows = slice(b, b + 128)
         right[rows, :] = dot(same[rows, :], left[...], ((1,), (1,))).astype(BF16)
@@ -583,16 +798,55 @@
         right_rows[rows, :] = dot(post[rows, :], left[...], ((1,), (1,))).astype(BF16)
 
 
-def weights_kernel(s, table, local_q, wa_s, wb_s, wa_t, wb_t):
+def weights_kernel(
+    s, real_ref, imag_ref, rate_ref, counts_ref, index_ref, mirror_ref, couplings_ref, wa_s, wb_s, wa_t, wb_t, damp
+):
+    me = lax.axis_index("aux") * s.rows + lax.axis_index("row")
     depth, wide = 2 * s.tile, MODES * s.tile
+    row, column = iotas(s.auxes, wide)
+    by_lane = mask_to(column % s.auxes == row)
+
+    def spread(table):
+        return dot(table.astype(F32).astype(BF16), by_lane, ((0,), (0,)))
+
+    counts = spread(counts_ref[...])
+    index, mirror = spread(index_ref[...]), spread(mirror_ref[...])
+    lane_mode = lax.broadcasted_iota(jnp.int32, (1, wide), 1) // s.tile
+
+    def of_mode(values):
+        out = values[0]
+        for k in range(1, MODES):
+            out = jnp.where(lane_mode == k, values[k], out)
+        return out
+
+    take = lambda table, first: of_mode([table[first + k : first + k + 1, :] for k in range(MODES)])
+    ups, downs = take(index, 0), take(index, MODES)
+    up_kinds, down_kinds = take(mirror, 0), take(mirror, MODES)
+    real = of_mode([counts[k : k + 1, :] * real_ref[k] for k in range(MODES)])
+    imag = of_mode([counts[k : k + 1, :] * imag_ref[k] for k in range(MODES)])
+    rates = counts[0:1, :] * rate_ref[0]
+    for k in range(1, MODES):
+        rates = rates + counts[k : k + 1, :] * rate_ref[k]
+    damp[...] = rates
+
+    row, column = iotas(s.extent, s.lanes)
+    pick = (row % s.devices == me) & (row // s.devices == column // s.za)
+    local_q = lax.dot_general(
+        couplings_ref[...],
+        pick.astype(F32),
+        (((1,), (0,)), ((), ())),
+        precision=lax.Precision.HIGHEST,
+        preferred_element_type=F32,
+    )
+
     row, column = iotas(depth, wide)
     same = row // s.za % s.fold == column // s.za % s.fold
     source, kind = (row % s.auxes).astype(F32), (row // s.tile).astype(F32)
     from_imag, to_imag = row // s.auxes % 2, column // s.auxes % 2
-    up = same & (table[0:1, :] == source) & (table[2:3, :] == kind)
-    down = same & (table[1:2, :] == source) & (table[3:4, :] == kind)
-    along = jnp.where(up, 1.0, 0.0) + jnp.where(down, table[4:5, :], 0.0)
-    cross = jnp.where(down, table[5:6, :], 0.0)
+    up = same & (ups == source) & (up_kinds == kind)
+    down = same & (downs == source) & (down_kinds == kind)
+    along = jnp.where(up, 1.0, 0.0) + jnp.where(down, real, 0.0)
+    cross = jnp.where(down, imag, 0.0)
     along = jnp.where(from_imag == 1, along, -along)
     flip = jnp.where((from_imag == 1) & (row // s.tile == 1), -1.0, 1.0)
     by_row = flip * jnp.where(from_imag == to_imag, cross, along)
@@ -627,22 +881,25 @@
     block_column,
 ):
     planes, per_device, band, extent = density.shape
-    group, row = lax.axis_index("aux"), lax.axis_index("row")
-    device = group * s.rows + row
     cube = 2 * extent * extent * s.lanes
     state = shape(extent, s.lanes, dtype=BF16)
     full = shape(extent, s.lanes)
-    pair = shape(2 * extent, s.lanes, dtype=BF16)
+    pair = (shape(s.devices, 2, s.local, s.lanes, dtype=BF16), 2)
     held = pltpu.VMEM((extent, s.lanes), F32)
     held_b = pltpu.VMEM((extent, s.lanes), BF16)
 
     def exchange(message):
-        sent = message.reshape(s.devices, -1, s.lanes)
-        got = lax.all_to_all(sent, BOTH, split_axis=0, concat_axis=0, tiled=True)
-        return got.reshape(-1, s.lanes)
-
-    counts = counts_of_all(s, tier_counts, group)
-    message = run(functools.partial(even_start_kernel, s), [pair], [density], scratch=[held_b], flops=2 * cube)[0]
+        return lax.all_to_all(message, BOTH, split_axis=0, concat_axis=0, tiled=True)
+
+    blocks = density.reshape(1, planes * per_device, band, extent)
+    message = run_staged(
+        functools.partial(even_start, s),
+        [pair],
+        [(blocks, v) for v in range(planes * per_device)],
+        temporaries=[held_b],
+        scalars=[tier_counts],
+        flops=2 * cube,
+    )[0]
     got = exchange(message)
 
     left, right, left_rows, right_rows = run(
@@ -653,32 +910,6 @@
         flops=4 * cube,
         scalars=(2,),
     )
-
-    def in_lanes(by_mode):
-        spread = jnp.broadcast_to(by_mode[:, None, :], (MODES, 2 * s.fold, s.auxes))
-        return spread.reshape(1, MODES * s.tile)
-
-    index = link_index.T.astype(F32)
-    mirror = link_mirror.T.astype(F32)
-    table = jnp.concatenate(
-        [
-            in_lanes(index[:MODES]),
-            in_lanes(index[MODES:]),
-            in_lanes(mirror[:MODES]),
-            in_lanes(mirror[MODES:]),
-            in_lanes((counts * weight_real[None, :]).T),
-            in_lanes((counts * weight_imag[None, :]).T),
-        ]
-    )
-    mine = lax.dynamic_slice_in_dim(couplings.reshape(MODES, s.local, s.devices), device, 1, 2)
-    local_q = jnp.broadcast_to(mine, (MODES, s.local, s.za)).reshape(MODES, s.lanes)
-    wa = shape(s.tiles, 4 * s.tile, s.tile, dtype=BF16)
-    wb = shape(4 * s.tile, MODES * s.tile, dtype=BF16)
-    wa_s, wb_s, wa_t, wb_t = run(
-        functools.partial(weights_kernel, s), [wa, wb, wa, wb], [table, local_q]
-    )
-    damping = jnp.sum(counts * mode_rates[None, :], axis=1)
-    damp = jnp.tile(damping, (planes * s.local,))[None, :]
     q_first = couplings.T
 
     k, n = iotas(s.lanes, s.lanes)
@@ -710,66 +941,72 @@
     k, n = iotas(size, size)
     order = (n == k % span * s.local + k // span).astype(BF16)
 
-    s_now, t_now, message = run(
-        functools.partial(even_take_kernel, s),
-        [state, state, pair],
-        [got, row_lanes, column_lanes, right_rows, left_rows],
+    message, s_now, t_now, counts = run_staged(
+        functools.partial(even_take, s),
+        [pair, state, state, shape(s.auxes, MODES)],
+        [(got, 0), row_lanes, right_rows, (got, 1), column_lanes, left_rows],
         flops=4 * cube,
+    )
+    wa = shape(s.tiles, 4 * s.tile, s.tile, dtype=BF16)
+    wb = shape(4 * s.tile, MODES * s.tile, dtype=BF16)
+    wa_s, wb_s, wa_t, wb_t, damp = run(
+        functools.partial(weights_kernel, s),
+        [wa, wb, wa, wb, shape(1, s.lanes)],
+        [weight_real, weight_imag, mode_rates, counts, link_index, link_mirror, couplings],
+        scalars=(0, 1, 2),
+        flops=cube,
     )
     start_s, start_t = s_now, t_now
     ys, yt = s_now, t_now
     total = None
     shares = [STEP / 6.0, STEP / 3.0, STEP / 3.0, STEP / 6.0]
     steps = [0.25, 0.25, 0.5]
-    for section in range(4):
-        columns = section < 3
-        if columns:
-            got = exchange(message)
-        slopes = run(
-            functools.partial(slope_kernel, s, columns),
-            [full, full] if columns else [full],
-            [s_now, t_now, ys, yt, damp, q_first, right, left, unit, wa_s, wb_s, wa_t, wb_t],
-            scratch=[held_b],
-            flops=(12 if columns else 6) * cube,
+    for section in range(3):
+        got = exchange(message)
+        ks, kt = run_staged(
+            functools.partial(even_slope, s),
+            [full, full],
+            [s_now, t_now, ys, yt, unit, damp, q_first, right, wa_s, wb_s, left, wa_t, wb_t],
+            temporaries=[held_b],
+            flops=12 * cube,
         )
-        if columns:
-            args = [got, order, swap, right_rows, left_rows, *slopes, start_s, start_t]
+        if section < 2:
+            args = [(got, 0), order, swap, ks, start_s, right_rows, (got, 1), kt, start_t, left_rows]
             if total is not None:
                 args.append(total)
-            outs = [state, state, full, full, full]
-            more = section < 2
-            if more:
-                outs.append(pair)
-            s_now, t_now, ys, yt, total, *message = run(
-                functools.partial(next_kernel, s, shares[section], steps[section], total is not None, more, 1),
-                outs,
+            message, s_now, t_now, ys, yt, total = run_staged(
+                functools.partial(even_next, s, shares[section], steps[section], total is not None),
+                [pair, state, state, full, full, full],
                 args,
-                scratch=[held],
+                temporaries=[held],
                 flops=6 * cube,
             )
-            message = message[0] if more else None
-    message = run(
-        functools.partial(even_last_kernel, s, shares[3]),
+    message = run_staged(
+        functools.partial(even_last, s, steps[2], shares[2], shares[3]),
         [pair],
-        [slopes[0], total, t_now, left, unit, row_lanes, column_lanes],
-        scratch=[held_b, held_b],
-        flops=3 * cube,
+        [(got, 1), order, swap, kt, start_t, unit, left, column_lanes, (got, 0), ks, start_s, total]
+        + [damp, q_first, right, wa_s, wb_s, row_lanes],
+        temporaries=[held, held_b, held_b, held_b, held_b, held],
+        flops=12 * cube,
     )[0]
     got = exchange(message)
-    return run(
-        functools.partial(even_finish_kernel, s),
-        [shape(planes, per_device, band, extent)],
-        [got, density],
-        scratch=[held_b, held_b],
+    evolved = run_staged(
+        functools.partial(even_finish, s),
+        [(shape(1, planes * per_device, band, extent), planes * per_device)],
+        [(got, 0), (got, 1)] + [(blocks, v) for v in range(planes * per_device)],
+        temporaries=[held_b],
         flops=2 * cube,
     )[0]
+    return evolved.reshape(density.shape)
 
 
 def body(density, *others):
     planes, per_device, band, extent = density.shape
     s = Sizes(lax.axis_size("aux"), lax.axis_size("row"), per_device, band, extent)
     even = band % s.devices == 0 and s.local % 16 == 0 and LANES % s.za == 0
-    if even and s.lanes == extent and planes * per_device * band == extent:
+    even = even and s.lanes == extent and planes * per_device * band == extent
+    even = even and planes * per_device == MODES and per_device <= s.rows and s.devices <= s.band
+    if even:
         return even_body(s, density, *others)
     return general_body(density, *others)
 

time: 235 us -> 198 us (0.84)
  local copies, waits for them, and re-layouts: 88.1 us -> 45.7 us
  Pallas kernels: 35.2 us -> 51.5 us
  starting transfers between devices: 25.6 us -> 19.2 us
  other arithmetic: 9.32 us -> 4.24 us
    pallas_call x0 -> x9, Pallas kernels: none -> 46.8 us  [run_staged(): pl.pallas_call(kernel, out_shape=shapes, in_specs=[pl.BlockSpec(memory_sp...]
    pallas_call x13 -> x2, Pallas kernels: 35.2 us -> 4.63 us  [run(): pl.pallas_call(kernel, out_shape=list(outs), in_specs=[flat if n in scala...]
    unnamed x182 -> x121, local copies, waits for them, and re-layouts: 74.2 us -> 45.7 us
    all_to_all x4, waiting for transfers between devices: 35.1 us -> 45.4 us  [exchange(): lax.all_to_all(message, BOTH, split_axis=0, concat_axis=0, tiled=True)]
    ppermute x3 -> x0, starting transfers between devices: 9.01 us -> none  [counts_of_all(): lax.ppermute(whole, 'aux', [(i, i ^ step) for i in range(s.groups)])]
    ppermute x3 -> x0, waiting for transfers between devices: 7.98 us -> none  [counts_of_all(): lax.ppermute(whole, 'aux', [(i, i ^ step) for i in range(s.groups)])]
    reshape x8 -> x0, local copies, waits for them, and re-layouts: 5.41 us -> none  [the longest x6 3.9 us: in_lanes(): return spread.reshape(1, MODES * s.tile)]
    broadcast_in_dim x8 -> x0, local copies, waits for them, and re-layouts: 3.94 us -> none  [the longest x6 2.66 us: in_lanes(): spread = jnp.broadcast_to(by_mode[:, None, :], (MODES, 2 * s.fold, s.auxes))]
  transfers between devices with their start and end apart: 7 -> 4, of which waited for: 4 -> 4; matrix products, arithmetic and copies ran while one was open for 10% -> 2% of each run, Pallas kernels for 9% -> 13%
where the time goes in v1:
time: 198 us; the launch traced here: 197 us
  Pallas kernels  51.5 us (26%)
  local copies, waits for them, and re-layouts  45.7 us (23%)
  waiting for transfers between devices  45.4 us (23%)
  blocking collectives  29.7 us (15%)
  starting transfers between devices  19.2 us (10%)
  other arithmetic  4.24 us (2%)
    pallas_call x9, Pallas kernels, run_staged(): pl.pallas_call(kernel, out_shape=shapes, in_specs=[pl.BlockSpec(memory_sp...  46.8 us
    unnamed x121, local copies, waits for them, and re-layouts  45.7 us
    all_to_all x4, waiting for transfers between devices, exchange(): lax.all_to_all(message, BOTH, split_axis=0, concat_axis=0, tiled=True)  45.4 us
    all_to_all x1, blocking collectives, exchange(): lax.all_to_all(message, BOTH, split_axis=0, concat_axis=0, tiled=True)  29.7 us
    all_to_all x4, starting transfers between devices, exchange(): lax.all_to_all(message, BOTH, split_axis=0, concat_axis=0, tiled=True)  19.2 us
    pallas_call x2, Pallas kernels, run(): pl.pallas_call(kernel, out_shape=list(outs), in_specs=[flat if n in scala...  4.63 us
  transfers between devices with their start and end apart: 4, of which 4 were waited for; matrix products, arithmetic and copies ran while one was open for 2% of the time, Pallas kernels for 13%

profile of v1, /device:TPU:0, one launch (start us, length us, event | category | flops | bytes accessed | tf_op | source)
XLA Modules:
  0.0 196.5 jit_solution(10620232737415500716)
XLA Ops:
  0.7 1.2 copy-done
  1.9 2.7 %shard_map.109 = bf16[32,2,16,512]{3,2,1,0:T(8,128)(2,1)} custom-call(s32[2,4]{1,0:T(2,128)S(1)} %copy-done.14, f32[1,4,128,512]{3,2,1,0:T(8,128)S(1)} %bitcast.3), custom_call_target="tpu_custom_call" | custom-call | flops 536870912 | bytes 2097152 | tf_op jit(solution)/shard_map/pallas_call | solution.py:551
  4.6 7.3 %all-to-all-start = ((bf16[32,2,16,512]{3,2,1,0:T(8,128)(2,1)}), bf16[32,2,16,512]{3,2,1,0:T(8,128)(2,1)S(1)}, u32[]{:S(2)}, u32[]{:S(2)}) async-start(bf16[32,2,16,512]{3,2,1,0:T(8,128)(2,1)} %shard_map.109), calls=%async_computation | async-start | bytes 2097152 | tf_op jit(solution)/shard_map/all_to_all | solution.py:892
  12.6 2.6 %shard_map.110 = (bf16[512,512]{1,0:T(8,128)(2,1)S(1)}, bf16[512,512]{1,0:T(8,128)(2,1)S(1)}, bf16[512,512]{1,0:T(8,128)(2,1)S(1)}, bf16[512,512]{1,0:T(8,128)(2,1)S(1)}) custom-call(bf16[8,64,64]{2,1,0:T(8,128)(2,1)S(1)} %copy-done.20, bf16[8,64,64]{2,1,0:T(8,128)(2,1)S(1)} %copy-done.21, s32[8]{0:T(128)S(1)} %copy-done.22), custom_call_target="tpu_custom_call" | custom-call | flops 1073741824 | bytes 2228256 | tf_op jit(solution)/shard_map/pallas_call | solution.py:44
  15.2 0.8 copy-done.47
  16.0 0.8 copy-done.52
  18.5 1.2 fusion.24.refs_3_.refs_7_
  19.7 1.4 fusion.25.refs_1_.refs_16_
  21.2 17.0 %all-to-all-done.refs_0_ = bf16[32,2,16,512]{3,2,1,0:T(8,128)(2,1)S(1)} async-done(((bf16[32,2,16,512]{3,2,1,0:T(8,128)(2,1)}), bf16[32,2,16,512]{3,2,1,0:T(8,128)(2,1)S(1)}, u32[]{:S(2)}, u32[]{:S(2)}) %all-to-all-start) | async-done | bytes 1048608 | tf_op jit(solution)/shard_map/all_to_all | solution.py:892
  38.1 3.0 %shard_map.111 = (bf16[32,2,16,512]{3,2,1,0:T(8,128)(2,1)}, bf16[512,512]{1,0:T(8,128)(2,1)S(1)}, bf16[512,512]{1,0:T(8,128)(2,1)S(1)}, f32[16,4]{1,0:T(8,128)S(1)}) custom-call(bf16[32,2,16,512]{3,2,1,0:T(8,128)(2,1)S(1)} %all-to-all-done.refs_0_, bf16[512,512]{1,0:T(8,128)(2,1)S(1)} %fusion.25.refs_1_.refs_16_, ...), custom_call_target="tpu_custom_call" | custom-call | flops 1073741824 | bytes 5243136 | tf_op jit(solution)/shard_map/pallas_call | solution.py:551
  41.2 0.9 copy-done.3
  42.1 0.8 copy-done.8
  42.9 3.9 %all-to-all-start.1 = ((bf16[32,2,16,512]{3,2,1,0:T(8,128)(2,1)}), bf16[32,2,16,512]{3,2,1,0:T(8,128)(2,1)}, u32[]{:S(2)}, u32[]{:S(2)}) async-start(bf16[32,2,16,512]{3,2,1,0:T(8,128)(2,1)} %get-tuple-element.38), calls=%async_computation.1 | async-start | bytes 2097152 | tf_op jit(solution)/shard_map/all_to_all | solution.py:892
  47.4 1.0 select_convert_fusion.refs_2_
  48.4 2.1 %shard_map.112 = (bf16[4,512,128]{2,1,0:T(8,128)(2,1)S(1)}, bf16[512,512]{1,0:T(8,128)(2,1)S(1)}, bf16[4,512,128]{2,1,0:T(8,128)(2,1)S(1)}, bf16[512,512]{1,0:T(8,128)(2,1)S(1)}, f32[1,512]{1,0:T(1,128)S(1)}) custom-call(f32[4]{0:T(128)S(1)} %copy-done.23, f32[4]{0:T(128)S(1)} %copy-done.24, f32[4]{0:T(128)S(1)} %copy-done.25, ...), custom_call_target="tpu_custom_call" | custom-call | flops 268435456 | bytes 2108720 | tf_op jit(solution)/shard_map/pallas_call | solution.py:44
  50.6 1.0 copy-done.48
  51.6 1.0 copy-done.53
  52.6 6.3 %shard_map.113 = (f32[512,512]{1,0:T(8,128)S(1)}, f32[512,512]{1,0:T(8,128)}) custom-call(bf16[512,512]{1,0:T(8,128)(2,1)S(1)} %copy-done.4, bf16[512,512]{1,0:T(8,128)(2,1)S(1)} %copy-done.9, bf16[128,128]{1,0:T(8,128)(2,1)S(1)} %select_convert_fusion.1.refs_2_.refs_4_.refs_5_, f32[1,512]{1,0:T(1,128)S(1)} %get-tuple-element.42.refs_3_.refs_5_.refs_11_, ...), custom_call_target="tpu_custom_call" | custom-call | flops 3221225472 | bytes 6334464 | tf_op jit(solution)/shard_map/pallas_call | solution.py:551
  59.0 1.0 copy-done.27
  60.8 0.8 copy-done.36
  61.6 0.8 copy-done.40
  63.2 9.7 %all-to-all-done.1.refs_0_ = bf16[32,2,16,512]{3,2,1,0:T(8,128)(2,1)} async-done(((bf16[32,2,16,512]{3,2,1,0:T(8,128)(2,1)}), bf16[32,2,16,512]{3,2,1,0:T(8,128)(2,1)}, u32[]{:S(2)}, u32[]{:S(2)}) %all-to-all-start.1) | async-done | bytes 1048608 | tf_op jit(solution)/shard_map/all_to_all | solution.py:892
  72.8 1.0 copy-done.5
  73.9 1.0 copy-done.10
  74.9 4.9 %shard_map.114 = (bf16[32,2,16,512]{3,2,1,0:T(8,128)(2,1)}, bf16[512,512]{1,0:T(8,128)(2,1)S(1)}, bf16[512,512]{1,0:T(8,128)(2,1)S(1)}, f32[512,512]{1,0:T(8,128...) custom-call(bf16[32,2,16,512]{3,2,1,0:T(8,128)(2,1)} %all-to-all-done.1.refs_0_, bf16[256,256]{1,0:T(8,128)(2,1)S(1)} %fusion.26.refs_1_, ...), custom_call_target="tpu_custom_call" | custom-call | flops 1610612736 | bytes 11141120 | tf_op jit(solution)/shard_map/pallas_call | solution.py:551
  79.8 1.0 copy-done.26
  80.8 0.8 copy-done.28
  82.4 4.0 %all-to-all-start.2 = ((bf16[32,2,16,512]{3,2,1,0:T(8,128)(2,1)}), bf16[32,2,16,512]{3,2,1,0:T(8,128)(2,1)}, u32[]{:S(2)}, u32[]{:S(2)}) async-start(bf16[32,2,16,512]{3,2,1,0:T(8,128)(2,1)} %get-tuple-element.51), calls=%async_computation.2 | async-start | bytes 2097152 | tf_op jit(solution)/shard_map/all_to_all | solution.py:892
  86.4 1.0 copy-done.29
  87.4 1.0 copy-done.31
  88.5 1.0 copy-done.33
  89.5 1.0 copy-done.37
  90.5 1.0 copy-done.41
  91.6 1.0 copy-done.44
  92.6 1.0 copy-done.49
  93.7 1.0 copy-done.54
  94.7 7.2 %shard_map.115 = (f32[512,512]{1,0:T(8,128)S(1)}, f32[512,512]{1,0:T(8,128)}) custom-call(bf16[512,512]{1,0:T(8,128)(2,1)S(1)} %copy-done.29, bf16[512,512]{1,0:T(8,128)(2,1)S(1)} %copy-done.31, f32[512,512]{1,0:T(8,128)} %copy-done.26, f32[512,512]{1,0:T(8,128)} %get-tuple-element.55.refs_3_, ...), custom_call_target="tpu_custom_call" | custom-call | flops 3221225472 | bytes 8431616 | tf_op jit(solution)/shard_map/pallas_call | solution.py:551
  101.9 1.0 copy-done.2
  102.9 9.5 %all-to-all-done.2.refs_0_ = bf16[32,2,16,512]{3,2,1,0:T(8,128)(2,1)} async-done(((bf16[32,2,16,512]{3,2,1,0:T(8,128)(2,1)}), bf16[32,2,16,512]{3,2,1,0:T(8,128)(2,1)}, u32[]{:S(2)}, u32[]{:S(2)}) %all-to-all-start.2) | async-done | bytes 1048608 | tf_op jit(solution)/shard_map/all_to_all | solution.py:892
  112.4 1.0 copy-done.6
  113.4 1.0 copy-done.11
  114.4 5.4 %shard_map.116 = (bf16[32,2,16,512]{3,2,1,0:T(8,128)(2,1)}, bf16[512,512]{1,0:T(8,128)(2,1)S(1)}, bf16[512,512]{1,0:T(8,128)(2,1)S(1)}, f32[512,512]{1,0:T(8,128...) custom-call(bf16[32,2,16,512]{3,2,1,0:T(8,128)(2,1)} %all-to-all-done.2.refs_0_, bf16[256,256]{1,0:T(8,128)(2,1)S(1)} %fusion.26.refs_1_, ...), custom_call_target="tpu_custom_call" | custom-call | flops 1610612736 | bytes 12189696 | tf_op jit(solution)/shard_map/pallas_call | solution.py:551
  119.9 1.0 copy-done.15
  120.8 0.8 copy-done.16
  121.7 0.8 copy-done.18
  122.5 4.0 %all-to-all-start.3 = ((bf16[32,2,16,512]{3,2,1,0:T(8,128)(2,1)}), bf16[32,2,16,512]{3,2,1,0:T(8,128)(2,1)}, u32[]{:S(2)}, u32[]{:S(2)}) async-start(bf16[32,2,16,512]{3,2,1,0:T(8,128)(2,1)} %get-tuple-element.59), calls=%async_computation.3 | async-start | bytes 2097152 | tf_op jit(solution)/shard_map/all_to_all | solution.py:892
  126.5 1.0 copy-done.17
  127.5 1.0 copy-done.19
  128.6 1.0 copy-done.34
  129.6 1.0 copy-done.38
  130.6 1.0 copy-done.42
  131.7 1.0 copy-done.45
  132.7 1.0 copy-done.50
  133.8 1.0 copy-done.55
  134.8 7.3 %shard_map.117 = (f32[512,512]{1,0:T(8,128)S(1)}, f32[512,512]{1,0:T(8,128)}) custom-call(bf16[512,512]{1,0:T(8,128)(2,1)S(1)} %copy-done.17, bf16[512,512]{1,0:T(8,128)(2,1)S(1)} %copy-done.19, f32[512,512]{1,0:T(8,128)} %copy-done.15, f32[512,512]{1,0:T(8,128)} %get-tuple-element.63.refs_3_, ...), custom_call_target="tpu_custom_call" | custom-call | flops 3221225472 | bytes 8431616 | tf_op jit(solution)/shard_map/pallas_call | solution.py:551
  142.1 1.0 copy-done.46
  143.1 9.3 %all-to-all-done.3.refs_0_ = bf16[32,2,16,512]{3,2,1,0:T(8,128)(2,1)} async-done(((bf16[32,2,16,512]{3,2,1,0:T(8,128)(2,1)}), bf16[32,2,16,512]{3,2,1,0:T(8,128)(2,1)}, u32[]{:S(2)}, u32[]{:S(2)}) %all-to-all-start.3) | async-done | bytes 1048608 | tf_op jit(solution)/shard_map/all_to_all | solution.py:892
  152.4 1.0 copy-done.35
  153.5 1.0 copy-done.39
  154.5 1.0 copy-done.51
  155.6 1.0 copy-done.56
  156.6 7.6 %shard_map.118 = bf16[32,2,16,512]{3,2,1,0:T(8,128)(2,1)S(1)} custom-call(bf16[32,2,16,512]{3,2,1,0:T(8,128)(2,1)} %all-to-all-done.3.refs_0_, bf16[256,256]{1,0:T(8,128)(2,1)S(1)} %fusion.26.refs_1_, bf16[512,512]{1,0:T(8,128)(2,1)S(1)} %select_convert_fusion.refs_2_, f32[512,512]{1,0:T(8,128)} %get-tuple-element.64.refs_3_, ...), custom_call_target="tpu_custom_call" | custom-call | flops 3221225472 | bytes 10135552 | tf_op jit(solution)/shard_map/pallas_call | solution.py:551
  164.2 29.7 %all_to_all.25.refs_0_ = bf16[32,2,16,512]{3,2,1,0:T(8,128)(2,1)S(1)} all-to-all(bf16[32,2,16,512]{3,2,1,0:T(8,128)(2,1)S(1)} %shard_map.118), channel_id=1, replica_groups=mesh['aux'=8,'row'=4] {'aux','row'}, dimensions={0} | all-to-all | bytes 2097152 | tf_op jit(solution)/shard_map/all_to_all | solution.py:892
  193.9 2.4 %shard_map.119 = f32[1,4,128,512]{3,2,1,0:T(8,128)} custom-call(bf16[32,2,16,512]{3,2,1,0:T(8,128)(2,1)S(1)} %all_to_all.25.refs_0_, f32[1,4,128,512]{3,2,1,0:T(8,128)S(1)} %bitcast.4), custom_call_target="tpu_custom_call" | custom-call | flops 536870912 | bytes 3145728 | tf_op jit(solution)/shard_map/pallas_call | solution.py:551
  (105 shorter events, 5.9 us)
Async XLA Ops:
  0.0 0.7 copy-start.14
  0.7 1.2 copy-start
  4.6 7.4 %copy-start.20 = (bf16[8,64,64]{2,1,0:T(8,128)(2,1)S(1)}, bf16[8,64,64]{2,1,0:T(8,128)(2,1)}, u32[]{:S(2)}) copy-start(bf16[8,64,64]{2,1,0:T(8,128)(2,1)} %own_ref.1) | copy-start | bytes 196612
  4.6 7.4 %copy-start.21 = (bf16[8,64,64]{2,1,0:T(8,128)(2,1)S(1)}, bf16[8,64,64]{2,1,0:T(8,128)(2,1)}, u32[]{:S(2)}) copy-start(bf16[8,64,64]{2,1,0:T(8,128)(2,1)} %outer_ref.1) | copy-start | bytes 196612
  4.6 33.5 %all-to-all-start = ((bf16[32,2,16,512]{3,2,1,0:T(8,128)(2,1)}), bf16[32,2,16,512]{3,2,1,0:T(8,128)(2,1)S(1)}, u32[]{:S(2)}, u32[]{:S(2)}) async-start(bf16[32,2,16,512]{3,2,1,0:T(8,128)(2,1)} %shard_map.109), calls=%async_computation | async-start | bytes 2097152 | tf_op jit(solution)/shard_map/all_to_all | solution.py:892
  11.9 0.7 copy-start.22
  12.6 4.2 %copy-start.57 = (s32[16,8]{0,1:T(8,128)S(1)}, s32[16,8]{0,1:T(8,128)}, u32[]{:S(2)}) copy-start(s32[16,8]{0,1:T(8,128)} %param.17) | copy-start | bytes 1540
  15.2 0.8 copy-start.47
  16.0 0.8 copy-start.52
  16.8 0.7 copy-start.58
  17.5 0.7 copy-start.13
  41.2 0.9 copy-start.3
  42.0 0.8 copy-start.8
  42.9 30.0 %all-to-all-start.1 = ((bf16[32,2,16,512]{3,2,1,0:T(8,128)(2,1)}), bf16[32,2,16,512]{3,2,1,0:T(8,128)(2,1)}, u32[]{:S(2)}, u32[]{:S(2)}) async-start(bf16[32,2,16,512]{3,2,1,0:T(8,128)(2,1)} %get-tuple-element.38), calls=%async_computation.1 | async-start | bytes 2097152 | tf_op jit(solution)/shard_map/all_to_all | solution.py:892
  47.4 1.1 copy-start.23
  47.4 1.1 copy-start.24
  47.4 1.1 copy-start.25
  47.4 3.1 %copy-start.9 = (bf16[512,512]{1,0:T(8,128)(2,1)S(1)}, bf16[512,512]{1,0:T(8,128)(2,1)}, u32[]{:S(2)}) copy-start(bf16[512,512]{1,0:T(8,128)(2,1)} %copy-done.8) | copy-start | bytes 1572868
  48.4 2.1 %copy-start.4 = (bf16[512,512]{1,0:T(8,128)(2,1)S(1)}, bf16[512,512]{1,0:T(8,128)(2,1)}, u32[]{:S(2)}) copy-start(bf16[512,512]{1,0:T(8,128)(2,1)} %copy-done.3) | copy-start | bytes 1572868
  50.5 1.0 copy-start.48
  51.6 1.0 copy-start.53
  59.0 1.0 copy-start.27
  60.0 0.8 copy-start.32
  60.8 0.8 copy-start.36
  61.6 0.8 copy-start.40
  62.4 0.8 copy-start.43
  72.8 1.0 copy-start.5
  73.9 1.0 copy-start.10
  79.8 1.0 copy-start.26
  80.8 0.8 copy-start.28
  81.6 0.8 copy-start.30
  82.4 30.0 %all-to-all-start.2 = ((bf16[32,2,16,512]{3,2,1,0:T(8,128)(2,1)}), bf16[32,2,16,512]{3,2,1,0:T(8,128)(2,1)}, u32[]{:S(2)}, u32[]{:S(2)}) async-start(bf16[32,2,16,512]{3,2,1,0:T(8,128)(2,1)} %get-tuple-element.51), calls=%async_computation.2 | async-start | bytes 2097152 | tf_op jit(solution)/shard_map/all_to_all | solution.py:892
  86.4 1.0 copy-start.29
  87.4 1.0 copy-start.31
  88.5 1.0 copy-start.33
  89.5 1.0 copy-start.37
  90.5 1.0 copy-start.41
  91.6 1.0 copy-start.44
  92.6 1.0 copy-start.49
  93.7 1.0 copy-start.54
  101.9 1.0 copy-start.2
  112.4 1.0 copy-start.6
  113.4 1.0 copy-start.11
  119.8 1.0 copy-start.15
  120.8 0.8 copy-start.16
  121.6 0.8 copy-start.18
  122.5 30.0 %all-to-all-start.3 = ((bf16[32,2,16,512]{3,2,1,0:T(8,128)(2,1)}), bf16[32,2,16,512]{3,2,1,0:T(8,128)(2,1)}, u32[]{:S(2)}, u32[]{:S(2)}) async-start(bf16[32,2,16,512]{3,2,1,0:T(8,128)(2,1)} %get-tuple-element.59), calls=%async_computation.3 | async-start | bytes 2097152 | tf_op jit(solution)/shard_map/all_to_all | solution.py:892
  126.5 1.0 copy-start.17
  127.5 1.0 copy-start.19
  128.6 1.0 copy-start.34
  129.6 1.0 copy-start.38
  130.6 1.0 copy-start.42
  131.7 1.0 copy-start.45
  132.7 1.0 copy-start.50
  133.8 1.0 copy-start.55
  134.8 17.6 %copy-start.7 = (bf16[512,512]{1,0:T(8,128)(2,1)S(1)}, bf16[512,512]{1,0:T(8,128)(2,1)}, u32[]{:S(2)}) copy-start(bf16[512,512]{1,0:T(8,128)(2,1)} %copy-done.3) | copy-start | bytes 1572868
  134.8 17.6 %copy-start.12 = (bf16[512,512]{1,0:T(8,128)(2,1)S(1)}, bf16[512,512]{1,0:T(8,128)(2,1)}, u32[]{:S(2)}) copy-start(bf16[512,512]{1,0:T(8,128)(2,1)} %copy-done.8) | copy-start | bytes 1572868
  142.1 1.0 copy-start.46
  152.4 1.0 copy-start.35
  153.5 1.0 copy-start.39
  154.5 1.0 copy-start.51
  155.6 1.0 copy-start.56
  164.2 29.7 %copy-start.1 = (f32[2,2,128,512]{3,2,1,0:T(8,128)S(1)}, f32[2,2,128,512]{3,2,1,0:T(8,128)}, u32[]{:S(2)}) copy-start(f32[2,2,128,512]{3,2,1,0:T(8,128)} %param.11) | copy-start | bytes 3145732

commit v2 on v1

--- a/solution.py
+++ b/solution.py
@@ -12,6 +12,7 @@
 LANES = 128
 STEP = 0.5
 BOTH = ("aux", "row")
+GRANT = 59 * (1 << 20) + (384 << 10)
 
 F32 = jnp.float32
 BF16 = jnp.bfloat16
@@ -554,7 +555,7 @@
         in_specs=[pl.BlockSpec(memory_space=pltpu.SMEM)] * len(scalars) + [far] * len(arrays),
         out_specs=[far] * len(shapes),
         scratch_shapes=buffers + results + list(temporaries) + [pltpu.SemaphoreType.DMA((count,))],
-        compiler_params=pltpu.CompilerParams(vmem_limit_bytes=48 << 20),
+        compiler_params=pltpu.CompilerParams(vmem_limit_bytes=GRANT),
         cost_estimate=pl.CostEstimate(flops=flops, bytes_accessed=moved, transcendentals=0),
     )(*scalars, *arrays)
 

time: 198 us -> 189 us (0.955)
  local copies, waits for them, and re-layouts: 45.7 us -> 14.5 us
  waiting for transfers between devices: 45.4 us -> 56.1 us
  Pallas kernels: 51.5 us -> 59.6 us
  other arithmetic: 4.24 us -> 8.37 us
    unnamed x121 -> x49, local copies, waits for them, and re-layouts: 45.7 us -> 14.5 us
    all_to_all x4, waiting for transfers between devices: 45.4 us -> 56.1 us  [exchange(): lax.all_to_all(message, BOTH, split_axis=0, concat_axis=0, tiled=True)]
    pallas_call x9, Pallas kernels: 46.8 us -> 55 us  [run_staged(): pl.pallas_call(kernel, out_shape=shapes, in_specs=[pl.BlockSpec(memory_sp...]
  transfers between devices with their start and end apart: 4 -> 4, of which waited for: 4 -> 4; matrix products, arithmetic and copies ran while one was open for 2% -> 5% of each run, Pallas kernels for 13% -> 15%
where the time goes in v2:
time: 189 us; the launch traced here: 188 us
  Pallas kernels  59.6 us (32%)
  waiting for transfers between devices  56.1 us (30%)
  blocking collectives  30 us (16%)
  starting transfers between devices  18.9 us (10%)
  local copies, waits for them, and re-layouts  14.5 us (8%)
  other arithmetic  8.37 us (4%)
    all_to_all x4, waiting for transfers between devices, exchange(): lax.all_to_all(message, BOTH, split_axis=0, concat_axis=0, tiled=True)  56.1 us
    pallas_call x9, Pallas kernels, run_staged(): pl.pallas_call(kernel, out_shape=shapes, in_specs=[pl.BlockSpec(memory_sp...  55 us
    all_to_all x1, blocking collectives, exchange(): lax.all_to_all(message, BOTH, split_axis=0, concat_axis=0, tiled=True)  30 us
    all_to_all x4, starting transfers between devices, exchange(): lax.all_to_all(message, BOTH, split_axis=0, concat_axis=0, tiled=True)  18.9 us
    unnamed x49, local copies, waits for them, and re-layouts  14.5 us
    pallas_call x2, Pallas kernels, run(): pl.pallas_call(kernel, out_shape=list(outs), in_specs=[flat if n in scala...  4.63 us
  transfers between devices with their start and end apart: 4, of which 4 were waited for; matrix products, arithmetic and copies ran while one was open for 5% of the time, Pallas kernels for 15%

profile of v2, /device:TPU:0, one launch (start us, length us, event | category | flops | bytes accessed | tf_op | source)
XLA Modules:
  0.0 188.0 jit_solution(12061740052380569829)
XLA Ops:
  0.0 3.7 %shard_map.109 = bf16[32,2,16,512]{3,2,1,0:T(8,128)(2,1)} custom-call(s32[2,4]{1,0:T(2,128)} %refs_0_.1, f32[1,4,128,512]{3,2,1,0:T(8,128)} %bitcast.3), custom_call_target="tpu_custom_call" | custom-call | flops 536870912 | bytes 2097152 | tf_op jit(solution)/shard_map/pallas_call | solution.py:552
  3.7 0.0 copy-start.3
  3.7 0.0 copy-start.4
  3.7 7.3 %all-to-all-start = ((bf16[32,2,16,512]{3,2,1,0:T(8,128)(2,1)}), bf16[32,2,16,512]{3,2,1,0:T(8,128)(2,1)S(1)}, u32[]{:S(2)}, u32[]{:S(2)}) async-start(bf16[32,2,16,512]{3,2,1,0:T(8,128)(2,1)} %shard_map.109), calls=%async_computation | async-start | bytes 2097152 | tf_op jit(solution)/shard_map/all_to_all | solution.py:893
  11.1 0.0 copy-start.5
  11.1 0.0 copy-done.3
  11.1 0.0 copy-done.4
  11.1 0.6 copy-done.5
  11.7 0.0 copy-start.21
  11.7 2.6 %shard_map.110 = (bf16[512,512]{1,0:T(8,128)(2,1)S(1)}, bf16[512,512]{1,0:T(8,128)(2,1)S(1)}, bf16[512,512]{1,0:T(8,128)(2,1)S(1)}, bf16[512,512]{1,0:T(8,128)(2,1)S(1)}) custom-call(bf16[8,64,64]{2,1,0:T(8,128)(2,1)S(1)} %copy-done.3, bf16[8,64,64]{2,1,0:T(8,128)(2,1)S(1)} %copy-done.4, s32[8]{0:T(128)S(1)} %copy-done.5), custom_call_target="tpu_custom_call" | custom-call | flops 1073741824 | bytes 2228256 | tf_op jit(solution)/shard_map/pallas_call | solution.py:45
  14.3 0.0 copy-start
  14.3 0.8 copy-done
  15.1 0.0 copy-start.1
  15.1 0.9 copy-done.1
  15.9 0.0 copy-start.13
  15.9 0.8 copy-done.13
  16.7 0.0 copy-start.14
  16.7 0.8 copy-done.14
  17.5 0.0 copy-done.21
  17.5 0.0 copy-start.22
  17.5 0.1 copy.12.index_ref
  17.6 0.6 copy-done.22
  18.2 0.1 copy.13.mirror_ref
  18.3 0.6 copy-done.2
  18.9 0.9 copy.14
  19.9 2.2 %fusion.24.refs_3_.refs_7_ = bf16[512,512]{1,0:T(8,128)(2,1)} fusion(s32[512]{0:T(512)S(1)} %get-tuple-element.82, s32[512]{0:T(512)S(1)} %get-tuple-element.89, s32[512]{0:T(512)S(1)} %get-tuple-element.83, s32[512]{0:T(512)S(1)} %get-tuple-element.90, s32[512]{0:T(512)S(1)} %get-tuple-element.81, s32[512]{0:T(512)S(1)} %get-tuple-element.84, ...), kind=kLoop, calls=%fused_computation.58 | loop fusion | flops 8912896 | bytes 542720 | tf_op jit(solution)/shard_map/convert_element_type | solution.py:931
  22.1 2.3 %fusion.25.refs_1_.refs_16_ = bf16[512,512]{1,0:T(8,128)(2,1)} fusion(s32[512]{0:T(512)S(1)} %get-tuple-element.67, s32[512]{0:T(512)S(1)} %get-tuple-element.77, s32[512]{0:T(512)S(1)} %get-tuple-element.68, s32[512]{0:T(512)S(1)} %get-tuple-element.78, s32[512]{0:T(512)S(1)} %get-tuple-element.69, s32[512]{0:T(512)S(1)} %get-tuple-element.79, ...), kind=kLoop, calls=%fused_computation.59 | loop fusion | flops 12582912 | bytes 547328 | tf_op jit(solution)/shard_map/convert_element_type | solution.py:924
  24.5 12.8 %all-to-all-done.refs_0_ = bf16[32,2,16,512]{3,2,1,0:T(8,128)(2,1)S(1)} async-done(((bf16[32,2,16,512]{3,2,1,0:T(8,128)(2,1)}), bf16[32,2,16,512]{3,2,1,0:T(8,128)(2,1)S(1)}, u32[]{:S(2)}, u32[]{:S(2)}) %all-to-all-start) | async-done | bytes 1048608 | tf_op jit(solution)/shard_map/all_to_all | solution.py:893
  37.2 0.0 copy-start.18
  37.2 1.0 copy-done.18
  38.2 4.0 %shard_map.111 = (bf16[32,2,16,512]{3,2,1,0:T(8,128)(2,1)}, bf16[512,512]{1,0:T(8,128)(2,1)}, bf16[512,512]{1,0:T(8,128)(2,1)}, f32[16,4]{1,0:T(8,128)}) custom-call(bf16[32,2,16,512]{3,2,1,0:T(8,128)(2,1)} %copy-done.18, bf16[512,512]{1,0:T(8,128)(2,1)} %fusion.25.refs_1_.refs_16_, bf16[512,512]{1,0:T(8,128)(2,1)} %copy-done.1, ...), custom_call_target="tpu_custom_call" | custom-call | flops 1073741824 | bytes 5243136 | tf_op jit(solution)/shard_map/pallas_call | solution.py:552
  42.2 3.8 %all-to-all-start.1 = ((bf16[32,2,16,512]{3,2,1,0:T(8,128)(2,1)}), bf16[32,2,16,512]{3,2,1,0:T(8,128)(2,1)S(1)}, u32[]{:S(2)}, u32[]{:S(2)}) async-start(bf16[32,2,16,512]{3,2,1,0:T(8,128)(2,1)} %get-tuple-element.38), calls=%async_computation.1 | async-start | bytes 2097152 | tf_op jit(solution)/shard_map/all_to_all | solution.py:893
  46.1 0.8 select_convert_fusion.1.refs_2_.refs_4_.refs_5_
  46.9 0.9 fusion.26.refs_1_
  47.8 0.0 copy-start.15
  47.8 2.0 %select_convert_fusion.refs_2_ = bf16[512,512]{1,0:T(8,128)(2,1)} fusion(s32[512]{0:T(512)S(1)} %get-tuple-element.71, s32[512]{0:T(512)S(1)} %get-tuple-element.80, s32[512]{0:T(512)S(1)} %get-tuple-element.98, s32[512]{0:T(512)S(1)} %get-tuple-element.101, s32[512]{0:T(512)S(1)} %get-tuple-element.97, s32[512]{0:T(512)S(1)} %get-tuple-element.102, ...), kind=kLoop, calls=%fused_computation.57 | loop fusion | flops 9175040 | bytes 542720 | tf_op jit(solution)/shard_map/convert_element_type | solution.py:939
  49.8 0.0 copy-start.6
  49.8 0.0 copy-done.15
  49.8 0.6 copy-done.6
  50.5 0.0 copy-done.7
  50.5 0.0 copy-done.8
  50.5 2.1 %shard_map.112 = (bf16[4,512,128]{2,1,0:T(8,128)(2,1)S(1)}, bf16[512,512]{1,0:T(8,128)(2,1)S(1)}, bf16[4,512,128]{2,1,0:T(8,128)(2,1)S(1)}, bf16[512,512]{1,0:T(8,128)(2,1)S(1)}, f32[1,512]{1,0:T(1,128)S(1)}) custom-call(f32[4]{0:T(128)S(1)} %copy-done.6, f32[4]{0:T(128)S(1)} %copy-done.7, f32[4]{0:T(128)S(1)} %copy-done.8, f32[16,4]{1,0:T(8,128)S(1)} %copy-done.15, ...), custom_call_target="tpu_custom_call" | custom-call | flops 268435456 | bytes 2108720 | tf_op jit(solution)/shard_map/pallas_call | solution.py:45
  52.6 0.0 copy-start.9
  52.6 0.8 copy-done.9
  53.4 0.8 copy-done.10
  54.2 0.8 copy-done.11
  55.0 0.8 copy-done.12
  55.8 0.6 copy-done.16
  56.4 7.9 %shard_map.113 = (f32[512,512]{1,0:T(8,128)}, f32[512,512]{1,0:T(8,128)}) custom-call(bf16[512,512]{1,0:T(8,128)(2,1)} %get-tuple-element.39.refs_0_.refs_4_.refs_9_, bf16[512,512]{1,0:T(8,128)(2,1)} %get-tuple-element.40.refs_1_.refs_7_.refs_4_, bf16[128,128]{1,0:T(8,128)(2,1)} %select_convert_fusion.1.refs_2_.refs_4_.refs_5_, f32[1,512]{1,0:T(1,128)} %copy-done.16, ...), custom_call_target="tpu_custom_call" | custom-call | flops 3221225472 | bytes 6334464 | tf_op jit(solution)/shard_map/pallas_call | solution.py:552
  64.3 7.8 %all-to-all-done.1.refs_0_ = bf16[32,2,16,512]{3,2,1,0:T(8,128)(2,1)S(1)} async-done(((bf16[32,2,16,512]{3,2,1,0:T(8,128)(2,1)}), bf16[32,2,16,512]{3,2,1,0:T(8,128)(2,1)S(1)}, u32[]{:S(2)}, u32[]{:S(2)}) %all-to-all-start.1) | async-done | bytes 1048608 | tf_op jit(solution)/shard_map/all_to_all | solution.py:893
  72.1 1.0 copy-done.19
  73.0 5.1 %shard_map.114 = (bf16[32,2,16,512]{3,2,1,0:T(8,128)(2,1)}, bf16[512,512]{1,0:T(8,128)(2,1)}, bf16[512,512]{1,0:T(8,128)(2,1)}, f32[512,512]{1,0:T(8,128)}, f32[512,512]{1,0:T(8,128)}, /*index=5*/f32[512,512]{1,0:T(8,128)}) custom-call(bf16[32,2,16,512]{3,2,1,0:T(8,128)(2,1)} %copy-done.19, bf16[256,256]{1,0:T(8,128)(2,1)} %fusion.26.refs_1_, ...), custom_call_target="tpu_custom_call" | custom-call | flops 1610612736 | bytes 11141120 | tf_op jit(solution)/shard_map/pallas_call | solution.py:552
  78.2 3.9 %all-to-all-start.2 = ((bf16[32,2,16,512]{3,2,1,0:T(8,128)(2,1)}), bf16[32,2,16,512]{3,2,1,0:T(8,128)(2,1)S(1)}, u32[]{:S(2)}, u32[]{:S(2)}) async-start(bf16[32,2,16,512]{3,2,1,0:T(8,128)(2,1)} %get-tuple-element.51), calls=%async_computation.2 | async-start | bytes 2097152 | tf_op jit(solution)/shard_map/all_to_all | solution.py:893
  82.0 8.2 %shard_map.115 = (f32[512,512]{1,0:T(8,128)}, f32[512,512]{1,0:T(8,128)}) custom-call(bf16[512,512]{1,0:T(8,128)(2,1)} %get-tuple-element.52.refs_0_, bf16[512,512]{1,0:T(8,128)(2,1)} %get-tuple-element.53.refs_1_, f32[512,512]{1,0:T(8,128)} %get-tuple-element.54.refs_2_, f32[512,512]{1,0:T(8,128)} %get-tuple-element.55.refs_3_, ...), custom_call_target="tpu_custom_call" | custom-call | flops 3221225472 | bytes 8431616 | tf_op jit(solution)/shard_map/pallas_call | solution.py:552
  90.2 17.8 %all-to-all-done.2.refs_0_ = bf16[32,2,16,512]{3,2,1,0:T(8,128)(2,1)S(1)} async-done(((bf16[32,2,16,512]{3,2,1,0:T(8,128)(2,1)}), bf16[32,2,16,512]{3,2,1,0:T(8,128)(2,1)S(1)}, u32[]{:S(2)}, u32[]{:S(2)}) %all-to-all-start.2) | async-done | bytes 1048608 | tf_op jit(solution)/shard_map/all_to_all | solution.py:893
  108.1 1.0 copy-done.17
  109.0 6.1 %shard_map.116 = (bf16[32,2,16,512]{3,2,1,0:T(8,128)(2,1)}, bf16[512,512]{1,0:T(8,128)(2,1)}, bf16[512,512]{1,0:T(8,128)(2,1)}, f32[512,512]{1,0:T(8,128)}, f32[512,512]{1,0:T(8,128)}, /*index=5*/f32[512,512]{1,0:T(8,128)}) custom-call(bf16[32,2,16,512]{3,2,1,0:T(8,128)(2,1)} %copy-done.17, bf16[256,256]{1,0:T(8,128)(2,1)} %fusion.26.refs_1_, ...), custom_call_target="tpu_custom_call" | custom-call | flops 1610612736 | bytes 12189696 | tf_op jit(solution)/shard_map/pallas_call | solution.py:552
  115.1 3.9 %all-to-all-start.3 = ((bf16[32,2,16,512]{3,2,1,0:T(8,128)(2,1)}), bf16[32,2,16,512]{3,2,1,0:T(8,128)(2,1)S(1)}, u32[]{:S(2)}, u32[]{:S(2)}) async-start(bf16[32,2,16,512]{3,2,1,0:T(8,128)(2,1)} %get-tuple-element.59), calls=%async_computation.3 | async-start | bytes 2097152 | tf_op jit(solution)/shard_map/all_to_all | solution.py:893
  119.0 8.2 %shard_map.117 = (f32[512,512]{1,0:T(8,128)}, f32[512,512]{1,0:T(8,128)}) custom-call(bf16[512,512]{1,0:T(8,128)(2,1)} %get-tuple-element.60.refs_0_, bf16[512,512]{1,0:T(8,128)(2,1)} %get-tuple-element.61.refs_1_, f32[512,512]{1,0:T(8,128)} %get-tuple-element.62.refs_2_, f32[512,512]{1,0:T(8,128)} %get-tuple-element.63.refs_3_, ...), custom_call_target="tpu_custom_call" | custom-call | flops 3221225472 | bytes 8431616 | tf_op jit(solution)/shard_map/pallas_call | solution.py:552
  127.2 17.8 %all-to-all-done.3.refs_0_ = bf16[32,2,16,512]{3,2,1,0:T(8,128)(2,1)S(1)} async-done(((bf16[32,2,16,512]{3,2,1,0:T(8,128)(2,1)}), bf16[32,2,16,512]{3,2,1,0:T(8,128)(2,1)S(1)}, u32[]{:S(2)}, u32[]{:S(2)}) %all-to-all-start.3) | async-done | bytes 1048608 | tf_op jit(solution)/shard_map/all_to_all | solution.py:893
  145.0 1.0 copy-done.20
  146.0 8.5 %shard_map.118 = bf16[32,2,16,512]{3,2,1,0:T(8,128)(2,1)} custom-call(bf16[32,2,16,512]{3,2,1,0:T(8,128)(2,1)} %copy-done.20, bf16[256,256]{1,0:T(8,128)(2,1)} %fusion.26.refs_1_, bf16[512,512]{1,0:T(8,128)(2,1)} %select_convert_fusion.refs_2_, f32[512,512]{1,0:T(8,128)} %get-tuple-element.64.refs_3_, ...), custom_call_target="tpu_custom_call" | custom-call | flops 3221225472 | bytes 10135552 | tf_op jit(solution)/shard_map/pallas_call | solution.py:552
  154.5 30.0 %all_to_all.25.refs_0_ = bf16[32,2,16,512]{3,2,1,0:T(8,128)(2,1)} all-to-all(bf16[32,2,16,512]{3,2,1,0:T(8,128)(2,1)} %shard_map.118), channel_id=1, replica_groups=mesh['aux'=8,'row'=4] {'aux','row'}, dimensions={0} | all-to-all | bytes 2097152 | tf_op jit(solution)/shard_map/all_to_all | solution.py:893
  184.5 3.3 %shard_map.119 = f32[1,4,128,512]{3,2,1,0:T(8,128)} custom-call(bf16[32,2,16,512]{3,2,1,0:T(8,128)(2,1)} %all_to_all.25.refs_0_, f32[1,4,128,512]{3,2,1,0:T(8,128)} %bitcast.4), custom_call_target="tpu_custom_call" | custom-call | flops 536870912 | bytes 3145728 | tf_op jit(solution)/shard_map/pallas_call | solution.py:552
  (33 shorter events, 0.1 us)
Async XLA Ops:
  3.7 7.4 %copy-start.3 = (bf16[8,64,64]{2,1,0:T(8,128)(2,1)S(1)}, bf16[8,64,64]{2,1,0:T(8,128)(2,1)}, u32[]{:S(2)}) copy-start(bf16[8,64,64]{2,1,0:T(8,128)(2,1)} %own_ref.1) | copy-start | bytes 196612
  3.7 7.4 %copy-start.4 = (bf16[8,64,64]{2,1,0:T(8,128)(2,1)S(1)}, bf16[8,64,64]{2,1,0:T(8,128)(2,1)}, u32[]{:S(2)}) copy-start(bf16[8,64,64]{2,1,0:T(8,128)(2,1)} %outer_ref.1) | copy-start | bytes 196612
  3.7 33.5 %all-to-all-start = ((bf16[32,2,16,512]{3,2,1,0:T(8,128)(2,1)}), bf16[32,2,16,512]{3,2,1,0:T(8,128)(2,1)S(1)}, u32[]{:S(2)}, u32[]{:S(2)}) async-start(bf16[32,2,16,512]{3,2,1,0:T(8,128)(2,1)} %shard_map.109), calls=%async_computation | async-start | bytes 2097152 | tf_op jit(solution)/shard_map/all_to_all | solution.py:893
  11.1 0.7 copy-start.5
  11.7 5.8 %copy-start.21 = (s32[16,8]{0,1:T(8,128)S(1)}, s32[16,8]{0,1:T(8,128)}, u32[]{:S(2)}) copy-start(s32[16,8]{0,1:T(8,128)} %param.17) | copy-start | bytes 1540
  14.3 0.8 copy-start
  15.1 0.9 copy-start.1
  15.9 0.8 copy-start.13
  16.7 0.8 copy-start.14
  17.5 0.7 copy-start.22
  18.2 0.7 copy-start.2
  37.2 1.0 copy-start.18
  42.2 29.9 %all-to-all-start.1 = ((bf16[32,2,16,512]{3,2,1,0:T(8,128)(2,1)}), bf16[32,2,16,512]{3,2,1,0:T(8,128)(2,1)S(1)}, u32[]{:S(2)}, u32[]{:S(2)}) async-start(bf16[32,2,16,512]{3,2,1,0:T(8,128)(2,1)} %get-tuple-element.38), calls=%async_computation.1 | async-start | bytes 2097152 | tf_op jit(solution)/shard_map/all_to_all | solution.py:893
  47.8 2.0 %copy-start.15 = (f32[16,4]{1,0:T(8,128)S(1)}, f32[16,4]{1,0:T(8,128)}, u32[]{:S(2)}) copy-start(f32[16,4]{1,0:T(8,128)} %get-tuple-element.41.counts_ref) | copy-start | bytes 772
  49.8 0.7 copy-start.6
  49.8 0.7 copy-start.7
  49.8 0.7 copy-start.8
  52.6 0.8 copy-start.9
  53.4 0.8 copy-start.10
  54.2 0.8 copy-start.11
  55.0 0.8 copy-start.12
  55.8 0.6 copy-start.16
  72.1 1.0 copy-start.19
  78.2 29.9 %all-to-all-start.2 = ((bf16[32,2,16,512]{3,2,1,0:T(8,128)(2,1)}), bf16[32,2,16,512]{3,2,1,0:T(8,128)(2,1)S(1)}, u32[]{:S(2)}, u32[]{:S(2)}) async-start(bf16[32,2,16,512]{3,2,1,0:T(8,128)(2,1)} %get-tuple-element.51), calls=%async_computation.2 | async-start | bytes 2097152 | tf_op jit(solution)/shard_map/all_to_all | solution.py:893
  108.0 1.0 copy-start.17
  115.1 29.9 %all-to-all-start.3 = ((bf16[32,2,16,512]{3,2,1,0:T(8,128)(2,1)}), bf16[32,2,16,512]{3,2,1,0:T(8,128)(2,1)S(1)}, u32[]{:S(2)}, u32[]{:S(2)}) async-start(bf16[32,2,16,512]{3,2,1,0:T(8,128)(2,1)} %get-tuple-element.59), calls=%async_computation.3 | async-start | bytes 2097152 | tf_op jit(solution)/shard_map/all_to_all | solution.py:893
  145.0 1.0 copy-start.20

commit v3 on v2

--- a/solution.py
+++ b/solution.py
@@ -12,7 +12,7 @@
 LANES = 128
 STEP = 0.5
 BOTH = ("aux", "row")
-GRANT = 59 * (1 << 20) + (384 << 10)
+GRANT = 52 << 20
 
 F32 = jnp.float32
 BF16 = jnp.bfloat16
@@ -482,10 +482,11 @@
 
 
 class Stage:
-    def __init__(self, sources, buffers, targets, results, semaphores):
+    def __init__(self, sources, buffers, targets, results, semaphores, offset, lead):
         self.buffers, self.results, self.targets = buffers, results, targets
-        self.semaphores, self.next = semaphores, 0
-        self.coming = [self.copy(a, b) for a, b in zip(sources, buffers)]
+        self.semaphores, self.next, self.offset = semaphores, 0, offset
+        self.sources, self.lead = sources, lead
+        self.coming = [self.copy(a, b) for a, b in zip(sources[:lead], buffers)]
         self.going = []
 
     def copy(self, source, target):
@@ -494,12 +495,22 @@
         made.start()
         return made
 
+    def front(self, index):
+        return self.need(index - self.offset)
+
     def need(self, index):
+        index += self.offset
+        if index >= len(self.coming):
+            self.start_rest()
         if self.coming[index] is not None:
             self.coming[index].wait()
             self.coming[index] = None
         return self.buffers[index]
 
+    def start_rest(self):
+        known = len(self.coming)
+        self.coming += [self.copy(a, b) for a, b in zip(self.sources[known:], self.buffers[known:])]
+
     def send(self, index):
         self.going.append(self.copy(self.results[index], self.targets[index]))
 
@@ -508,9 +519,9 @@
             made.wait()
 
 
-def run_staged(body, outs, args, temporaries=(), scalars=(), flops=0):
+def run_staged(body, outs, args, temporaries=(), scalars=(), front=(), lead=None, flops=0):
     arrays, views = [], []
-    for arg in args:
+    for arg in [*front, *args]:
         array, part = arg if isinstance(arg, tuple) else (arg, None)
         if not any(array is a for a in arrays):
             arrays.append(array)
@@ -542,6 +553,8 @@
             [pick(target[k], part) for k, part in places],
             made,
             refs[-1],
+            len(front),
+            len(views) if lead is None else lead,
         )
         body(stage, small, refs[:-1])
         stage.finish()
@@ -572,15 +585,18 @@
 
 
 def even_start(s, stage, small, temporaries):
-    (counts,) = small
     (post,) = temporaries
     post[...] = post_matrix(s)
     blocks = s.extent // s.band
     which = lax.axis_index("row") % s.per_device
     flats = [stage.need(v)[...].reshape(s.band, s.extent).astype(BF16) for v in range(blocks)]
     row, lane = iotas(128, s.band)
+    counts = stage.need(blocks)[...].astype(F32)
+    mine = counts[0:1, :]
+    for n in range(1, s.per_device):
+        mine = jnp.where(which == n, counts[n : n + 1, :], mine)
     for v in range(blocks):
-        count = counts[which, v].astype(F32)
+        count = mine[:, v : v + 1]
         for b in row_blocks(s.extent):
             value = dot(post[b : b + 128, :], flats[v], ((1,), (1,)))
             own = (row % s.local == 0) & (lane == (row + b) // s.local)
@@ -600,17 +616,17 @@
 
 
 def even_take(s, stage, small, temporaries):
-    s_ref, t_ref, counts_ref = stage.results[2], stage.results[3], stage.results[4]
+    s_ref, t_ref = stage.results[2], stage.results[3]
     me = lax.axis_index("aux") * s.rows + lax.axis_index("row")
     everyone = slice(0, s.devices)
-    rows_in, row_lanes = stage.need(0), stage.need(1)
+    rows_in, row_lanes = stage.front(0), stage.need(0)
     for b in row_blocks(s.extent):
         s_ref[b : b + 128, :] = dot(
             flat_rows(rows_in, everyone, slice(b, b + 128)), row_lanes[...], ((0,), (0,))
         ).astype(BF16)
     stage.send(2)
-    send_products(s, stage, stage.need(2), s_ref, 1)
-    columns_in, column_lanes = stage.need(3), stage.need(4)
+    send_products(s, stage, stage.need(1), s_ref, 1)
+    columns_in, column_lanes = stage.front(1), stage.need(2)
     blocks = s.extent // s.band
     parts = s.band // s.devices
     row, lane = iotas(s.devices, s.tile)
@@ -628,55 +644,54 @@
         kept = s_ref[: s.devices, first : first + s.tile].astype(F32)
         t_ref[rows, : s.tile] = jnp.where(mine, kept, t_ref[rows, : s.tile].astype(F32)).astype(BF16)
     stage.send(3)
-    send_products(s, stage, stage.need(5), t_ref, 0)
-    row, lane = iotas(s.extent, MODES)
-    gather = mask_to(row == lane * s.band + me)
-    row, lane = iotas(s.auxes, s.per_device * s.groups * s.local)
-    wanted = mask_to(lane == row * s.local)
-    pieces = [columns_in[a // s.per_device * s.rows + a % s.per_device] for a in range(s.auxes)]
-    counts_ref[...] = dot(wanted, dot(jnp.concatenate(pieces, axis=0), gather).astype(BF16))
-    stage.send(4)
-
-
-def even_turn(s, got_ref, order, swap, arrived):
+    send_products(s, stage, stage.need(3), t_ref, 0)
+
+
+def turn_matrices(s, order, swap):
+    size = order.shape[0]
+    span = size // s.local
+    k, n = lax.broadcasted_iota(jnp.int32, (size, 1), 0), lax.broadcasted_iota(jnp.int32, (1, size), 1)
+    order[...] = mask_to(n == k % span * s.local + k // span)
+    wide = s.fold * s.tile
+    k, n = lax.broadcasted_iota(jnp.int32, (wide, 1), 0), lax.broadcasted_iota(jnp.int32, (1, wide), 1)
+    sign = jnp.where(n // s.auxes % 2 == 0, 1.0, -1.0)
+    there = (k // s.za % s.fold * s.fold + k // s.tile) * s.za + (k + s.auxes) % s.za
+    swap[...] = jnp.where(there == n, sign, 0.0).astype(BF16)
+
+
+def even_turn(s, got, order, swap, put):
     def load(start, size):
-        return flat_rows(got_ref, slice(start // s.local, (start + size) // s.local))
-
+        return flat_rows(got, slice(start // s.local, (start + size) // s.local))
+
+    turn(s, load, order, swap, put)
+
+
+def updates(s, step, sign, k_ref, d_ref, keep):
     def put(rows, lanes, value):
-        arrived[rows, lanes] = value
-
-    turn(s, load, order, swap, put)
-
-
-def even_next(s, weight, step, has_total, stage, small, temporaries):
-    (arrived,) = temporaries
-    s_ref, t_ref, ys_ref, yt_ref, total_ref = stage.results[2:7]
-    got_s, order, swap = stage.need(0), stage.need(1), stage.need(2)
-    even_turn(s, got_s, order, swap, arrived)
-    ks_ref, ds_ref = stage.need(3), stage.need(4)
-    total_in = stage.need(10) if has_total else None
-    for b in row_blocks(s.extent, 64):
-        rows = slice(b, b + 64)
-        slope = ks_ref[rows, :] + arrived[rows, :]
-        grown = weight * slope
-        total_ref[rows, :] = total_in[rows, :] + grown if has_total else grown
-        state = ds_ref[rows, :].astype(F32) + step * slope
-        ys_ref[rows, :] = state
-        s_ref[rows, :] = state.astype(BF16)
-    for index in (2, 4, 6):
-        stage.send(index)
-    send_products(s, stage, stage.need(5), s_ref, 1)
-    even_turn(s, stage.need(6), order, swap, arrived)
-    kt_ref, dt_ref = stage.need(7), stage.need(8)
-    for b in row_blocks(s.extent, 64):
-        rows = slice(b, b + 64)
-        slope = kt_ref[rows, :] - arrived[rows, :]
-        state = dt_ref[rows, :].astype(F32) + step * slope
-        yt_ref[rows, :] = state
-        t_ref[rows, :] = state.astype(BF16)
-    stage.send(3)
-    stage.send(5)
-    send_products(s, stage, stage.need(9), t_ref, 0)
+        own = k_ref[rows, lanes]
+        slope = own + value if sign > 0 else own - value
+        keep(rows, lanes, d_ref[rows, lanes].astype(F32) + step * slope)
+
+    return put
+
+
+def even_next(s, step, stage, small, temporaries):
+    s_ref, t_ref, order, swap = temporaries
+    turn_matrices(s, order, swap)
+
+    def keep_in(ref):
+        def keep(rows, lanes, value):
+            ref[rows, lanes] = value.astype(BF16)
+
+        return keep
+
+    got = stage.front(0)
+    stage.start_rest()
+    even_turn(s, got, order, swap, updates(s, step, 1, stage.need(0), stage.need(1), keep_in(s_ref)))
+    send_products(s, stage, stage.need(2), s_ref, 1)
+    got = stage.need(3)
+    even_turn(s, got, order, swap, updates(s, step, -1, stage.need(4), stage.need(5), keep_in(t_ref)))
+    send_products(s, stage, stage.need(6), t_ref, 0)
 
 
 def even_slope_part(s, direct, mirror, y_ref, h, unit, damp, q_ref, wa, wb, turned, sign, put):
@@ -698,44 +713,92 @@
             put(rows, lanes, total)
 
 
-def even_slope(s, stage, small, temporaries):
+def put_in(ref):
+    def put(rows, lanes, value):
+        ref[rows, lanes] = value
+
+    return put
+
+
+def even_first_slope(s, stage, small, temporaries):
     (turned,) = temporaries
-
-    def put_in(index):
-        def put(rows, lanes, value):
-            stage.results[index][rows, lanes] = value
-
-        return put
-
     need = stage.need
+    first, second = stage.results
+    s_ref, t_ref, unit, damp, q_ref = need(0), need(1), need(2), need(3), need(4)
+    even_slope_part(
+        s, s_ref, t_ref, s_ref, need(5), unit, damp, q_ref, need(6), need(7), turned, -1.0, put_in(first)
+    )
+    stage.send(0)
+    even_slope_part(
+        s, t_ref, s_ref, t_ref, need(8), unit, damp, q_ref, need(9), need(10), turned, 1.0, put_in(second)
+    )
+    stage.send(1)
+
+
+def even_slope(s, step, ratio, has_total, stage, small, temporaries):
+    turned, s_ref, t_ref, ys_ref, yt_ref, order, swap = temporaries
+    turn_matrices(s, order, swap)
+    need = stage.need
+    first, second, total_ref = stage.results
+
+    def keep_in(ref, exact):
+        def keep(rows, lanes, value):
+            exact[rows, lanes] = value
+            ref[rows, lanes] = value.astype(BF16)
+
+        return keep
+
+    ds_ref = need(1)
+    even_turn(
+        s,
+        stage.front(0),
+        order,
+        swap,
+        updates(s, step, 1, need(0), ds_ref, keep_in(s_ref, ys_ref)),
+    )
+    even_turn(
+        s,
+        stage.front(1),
+        order,
+        swap,
+        updates(s, step, -1, need(2), need(3), keep_in(t_ref, yt_ref)),
+    )
+    total_in = need(13) if has_total else None
+    for b in row_blocks(s.extent, 64):
+        rows = slice(b, b + 64)
+        grown = ratio * (ys_ref[rows, :] - ds_ref[rows, :].astype(F32))
+        total_ref[rows, :] = total_in[rows, :] + grown if has_total else grown
+    stage.send(2)
     unit, damp, q_ref = need(4), need(5), need(6)
     even_slope_part(
-        s, need(0), need(1), need(2), need(7), unit, damp, q_ref, need(8), need(9), turned, -1.0, put_in(0)
+        s, s_ref, t_ref, ys_ref, need(7), unit, damp, q_ref, need(8), need(9), turned, -1.0, put_in(first)
     )
     stage.send(0)
     even_slope_part(
-        s, need(1), need(0), need(3), need(10), unit, damp, q_ref, need(11), need(12), turned, 1.0, put_in(1)
+        s, t_ref, s_ref, yt_ref, need(10), unit, damp, q_ref, need(11), need(12), turned, 1.0, put_in(second)
     )
     stage.send(1)
 
 
-def even_last(s, step, weight_three, weight_four, stage, small, temporaries):
-    arrived, s_ref, t_ref, grown, turned, base = temporaries
+def even_last(s, step, ratio, weight, stage, small, temporaries):
+    ys_ref, s_ref, t_ref, grown, turned, order, swap = temporaries
+    turn_matrices(s, order, swap)
     need = stage.need
-    order, swap = need(1), need(2)
-    even_turn(s, need(0), order, swap, arrived)
-    kt_ref, dt_ref = need(3), need(4)
-    for b in row_blocks(s.extent, 64):
-        rows = slice(b, b + 64)
-        slope = kt_ref[rows, :] - arrived[rows, :]
-        t_ref[rows, :] = (dt_ref[rows, :].astype(F32) + step * slope).astype(BF16)
-    unit, left, column_lanes = need(5), need(6), need(7)
+
+    def keep_columns(rows, lanes, value):
+        t_ref[rows, lanes] = value.astype(BF16)
+
+    put = updates(s, step, -1, need(0), need(1), keep_columns)
+    got = stage.front(0)
+    stage.start_rest()
+    even_turn(s, got, order, swap, put)
+    unit, left, column_lanes = need(2), need(3), need(4)
     for th in range(s.tiles):
         lanes = slice(th * s.tile, (th + 1) * s.tile)
         turned[:, lanes] = dot(t_ref[:, lanes], unit[...]).astype(BF16)
     for b in row_blocks(s.extent):
         rows = slice(b, b + 128)
-        grown[rows, :] = (weight_four * dot(left[rows, :], turned[...])).astype(BF16)
+        grown[rows, :] = (weight * dot(left[rows, :], turned[...])).astype(BF16)
     out = stage.results[1]
     for q in range(s.rows):
         value = dot(column_lanes[...], grown[q * s.band : (q + 1) * s.band, :], ((1,), (1,))).astype(BF16)
@@ -744,23 +807,24 @@
                 at = (v * s.groups + g) * s.local
                 out[g * s.rows + q, :, v * s.band : (v + 1) * s.band] = value[at : at + s.local, :]
     stage.send(1)
-    even_turn(s, need(8), order, swap, arrived)
-    ks_ref, ds_ref, total_in = need(9), need(10), need(11)
-    for b in row_blocks(s.extent, 64):
-        rows = slice(b, b + 64)
-        slope = ks_ref[rows, :] + arrived[rows, :]
-        base[rows, :] = total_in[rows, :] + weight_three * slope
-        state = ds_ref[rows, :].astype(F32) + step * slope
-        arrived[rows, :] = state
-        s_ref[rows, :] = state.astype(BF16)
-
-    def put(rows, lanes, value):
-        grown[rows, lanes] = (base[rows, lanes] + weight_four * value).astype(BF16)
+
+    def keep_rows(rows, lanes, value):
+        ys_ref[rows, lanes] = value
+        s_ref[rows, lanes] = value.astype(BF16)
+
+    ds_ref = need(6)
+    put = updates(s, step, 1, need(5), ds_ref, keep_rows)
+    even_turn(s, stage.front(1), order, swap, put)
+    total_in = need(7)
+
+    def put_change(rows, lanes, value):
+        change = total_in[rows, lanes] + ratio * (ys_ref[rows, lanes] - ds_ref[rows, lanes].astype(F32))
+        grown[rows, lanes] = (change + weight * value).astype(BF16)
 
     even_slope_part(
-        s, s_ref, t_ref, arrived, need(14), unit, need(12), need(13), need(15), need(16), turned, -1.0, put
-    )
-    row_lanes = need(17)
+        s, s_ref, t_ref, ys_ref, need(10), unit, need(8), need(9), need(11), need(12), turned, -1.0, put_change
+    )
+    row_lanes = need(13)
     for b in row_blocks(s.extent):
         fill(s, stage.results[0], b, dot(row_lanes[b : b + 128, :], grown[...], ((1,), (1,))).astype(BF16))
     stage.send(0)
@@ -770,18 +834,21 @@
     (post,) = temporaries
     post[...] = post_matrix(s)
     everyone = slice(0, s.devices)
-    rows_in, columns_in = stage.need(0), stage.need(1)
     for v in range(s.extent // s.band):
         lanes = slice(v * s.band, (v + 1) * s.band)
-        change = dot(post[:, lanes], flat_rows(rows_in, everyone), ((0,), (0,)))
-        change = change + dot(flat_rows(columns_in, everyone, lanes), post[...], ((0,), (0,)))
-        stage.results[v][...] = (stage.need(2 + v)[...].reshape(s.band, s.extent) + change).reshape(
+        change = dot(post[:, lanes], flat_rows(stage.front(0), everyone), ((0,), (0,)))
+        change = change + dot(flat_rows(stage.front(1), everyone, lanes), post[...], ((0,), (0,)))
+        stage.results[v][...] = (stage.need(v)[...].reshape(s.band, s.extent) + change).reshape(
             stage.results[v].shape
         )
         stage.send(v)
 
 
-def hamiltonian_kernel(s, own_ref, outer_ref, where_ref, left, right, left_rows, right_rows, post):
+def even_hamiltonian(s, stage, small, temporaries):
+    (where_ref,) = small
+    (post,) = temporaries
+    left, right, left_rows, right_rows = stage.results
+    own_ref, outer_ref = stage.need(0), stage.need(1)
     blocks, block = own_ref.shape[0], own_ref.shape[1]
     post[...] = post_matrix(s)
     row, column = iotas(block, s.extent)
@@ -797,11 +864,14 @@
         right[rows, :] = dot(same[rows, :], left[...], ((1,), (1,))).astype(BF16)
         left_rows[rows, :] = dot(post[rows, :], left[...]).astype(BF16)
         right_rows[rows, :] = dot(post[rows, :], left[...], ((1,), (1,))).astype(BF16)
-
-
-def weights_kernel(
-    s, real_ref, imag_ref, rate_ref, counts_ref, index_ref, mirror_ref, couplings_ref, wa_s, wb_s, wa_t, wb_t, damp
-):
+    for index in range(4):
+        stage.send(index)
+
+
+def even_weights(s, stage, small, temporaries):
+    real_ref, imag_ref, rate_ref = small
+    wa_s, wb_s, wa_t, wb_t, damp = stage.results
+    columns_in, index_ref, mirror_ref, couplings_ref = [stage.need(k) for k in range(4)]
     me = lax.axis_index("aux") * s.rows + lax.axis_index("row")
     depth, wide = 2 * s.tile, MODES * s.tile
     row, column = iotas(s.auxes, wide)
@@ -810,7 +880,12 @@
     def spread(table):
         return dot(table.astype(F32).astype(BF16), by_lane, ((0,), (0,)))
 
-    counts = spread(counts_ref[...])
+    row, lane = iotas(s.extent, MODES)
+    gather = mask_to(row == lane * s.band + me)
+    row, lane = iotas(s.auxes, s.auxes * s.local)
+    wanted = mask_to(lane == row * s.local)
+    pieces = [columns_in[a // s.per_device * s.rows + a % s.per_device] for a in range(s.auxes)]
+    counts = spread(dot(wanted, dot(jnp.concatenate(pieces, axis=0), gather).astype(BF16)))
     index, mirror = spread(index_ref[...]), spread(mirror_ref[...])
     lane_mode = lax.broadcasted_iota(jnp.int32, (1, wide), 1) // s.tile
 
@@ -865,6 +940,8 @@
             for k in range(1, MODES):
                 total = total + local_q[k : k + 1, lanes] * near[:, k * s.tile : (k + 1) * s.tile]
             wa[th, :depth, :], wa[th, depth:, :] = pieces(total)
+    for index in range(5):
+        stage.send(index)
 
 
 def even_body(
@@ -896,20 +973,19 @@
     message = run_staged(
         functools.partial(even_start, s),
         [pair],
-        [(blocks, v) for v in range(planes * per_device)],
+        [(blocks, v) for v in range(planes * per_device)] + [tier_counts],
         temporaries=[held_b],
-        scalars=[tier_counts],
         flops=2 * cube,
     )[0]
     got = exchange(message)
 
-    left, right, left_rows, right_rows = run(
-        functools.partial(hamiltonian_kernel, s),
+    left, right, left_rows, right_rows = run_staged(
+        functools.partial(even_hamiltonian, s),
         [state] * 4,
-        [block_diagonal, block_outer, block_column],
-        scratch=[held_b],
+        [block_diagonal, block_outer],
+        temporaries=[held_b],
+        scalars=[block_column],
         flops=4 * cube,
-        scalars=(2,),
     )
     q_first = couplings.T
 
@@ -933,69 +1009,74 @@
     k, n = iotas(s.tile, s.tile)
     sign = jnp.where(n // s.auxes % 2 == 0, 1.0, -1.0)
     unit = jnp.where(k // s.za * s.za + (k + s.auxes) % s.za == n, sign, 0.0).astype(BF16)
-    k, n = iotas(s.fold * s.tile, s.fold * s.tile)
-    sign = jnp.where(n // s.auxes % 2 == 0, 1.0, -1.0)
-    there = (k // s.za % s.fold * s.fold + k // s.tile) * s.za + (k + s.auxes) % s.za
-    swap = jnp.where(there == n, sign, 0.0).astype(BF16)
-    size = max(256, 16 * s.local)
-    span = size // s.local
-    k, n = iotas(size, size)
-    order = (n == k % span * s.local + k // span).astype(BF16)
-
-    message, s_now, t_now, counts = run_staged(
+    wide, size = s.fold * s.tile, max(256, 16 * s.local)
+    swap, order = pltpu.VMEM((wide, wide), BF16), pltpu.VMEM((size, size), BF16)
+
+    message, s_now, t_now = run_staged(
         functools.partial(even_take, s),
-        [pair, state, state, shape(s.auxes, MODES)],
-        [(got, 0), row_lanes, right_rows, (got, 1), column_lanes, left_rows],
+        [pair, state, state],
+        [row_lanes, right_rows, column_lanes, left_rows],
+        front=[(got, 0), (got, 1)],
         flops=4 * cube,
     )
     wa = shape(s.tiles, 4 * s.tile, s.tile, dtype=BF16)
     wb = shape(4 * s.tile, MODES * s.tile, dtype=BF16)
-    wa_s, wb_s, wa_t, wb_t, damp = run(
-        functools.partial(weights_kernel, s),
+    wa_s, wb_s, wa_t, wb_t, damp = run_staged(
+        functools.partial(even_weights, s),
         [wa, wb, wa, wb, shape(1, s.lanes)],
-        [weight_real, weight_imag, mode_rates, counts, link_index, link_mirror, couplings],
-        scalars=(0, 1, 2),
+        [(got, 1), link_index, link_mirror, couplings],
+        scalars=[weight_real, weight_imag, mode_rates],
         flops=cube,
     )
-    start_s, start_t = s_now, t_now
-    ys, yt = s_now, t_now
-    total = None
+    tables = [unit, damp, q_first, right, wa_s, wb_s, left, wa_t, wb_t]
     shares = [STEP / 6.0, STEP / 3.0, STEP / 3.0, STEP / 6.0]
     steps = [0.25, 0.25, 0.5]
-    for section in range(3):
-        got = exchange(message)
-        ks, kt = run_staged(
-            functools.partial(even_slope, s),
-            [full, full],
-            [s_now, t_now, ys, yt, unit, damp, q_first, right, wa_s, wb_s, left, wa_t, wb_t],
-            temporaries=[held_b],
-            flops=12 * cube,
+    got = exchange(message)
+    ks, kt = run_staged(
+        functools.partial(even_first_slope, s),
+        [full, full],
+        [s_now, t_now] + tables,
+        temporaries=[held_b],
+        flops=12 * cube,
+    )
+    total = None
+    for section in range(2):
+        step = steps[section]
+        message = run_staged(
+            functools.partial(even_next, s, step),
+            [pair],
+            [ks, s_now, right_rows, (got, 1), kt, t_now, left_rows],
+            temporaries=[held_b, held_b, order, swap],
+            front=[(got, 0)],
+            lead=3,
+            flops=5 * cube,
+        )[0]
+        arrived, got = got, exchange(message)
+        ks, kt, total = run_staged(
+            functools.partial(even_slope, s, step, shares[section] / step, total is not None),
+            [full, full, full],
+            [ks, s_now, kt, t_now] + tables + ([] if total is None else [total]),
+            temporaries=[held_b, held_b, held_b, held, held, order, swap],
+            front=[(arrived, 0), (arrived, 1)],
+            flops=15 * cube,
         )
-        if section < 2:
-            args = [(got, 0), order, swap, ks, start_s, right_rows, (got, 1), kt, start_t, left_rows]
-            if total is not None:
-                args.append(total)
-            message, s_now, t_now, ys, yt, total = run_staged(
-                functools.partial(even_next, s, shares[section], steps[section], total is not None),
-                [pair, state, state, full, full, full],
-                args,
-                temporaries=[held],
-                flops=6 * cube,
-            )
     message = run_staged(
-        functools.partial(even_last, s, steps[2], shares[2], shares[3]),
+        functools.partial(even_last, s, steps[2], shares[2] / steps[2], shares[3]),
         [pair],
-        [(got, 1), order, swap, kt, start_t, unit, left, column_lanes, (got, 0), ks, start_s, total]
+        [kt, t_now, unit, left, column_lanes, ks, s_now, total]
         + [damp, q_first, right, wa_s, wb_s, row_lanes],
-        temporaries=[held, held_b, held_b, held_b, held_b, held],
+        temporaries=[held, held_b, held_b, held_b, held_b, order, swap],
+        front=[(got, 1), (got, 0)],
+        lead=4,
         flops=12 * cube,
     )[0]
     got = exchange(message)
     evolved = run_staged(
         functools.partial(even_finish, s),
         [(shape(1, planes * per_device, band, extent), planes * per_device)],
-        [(got, 0), (got, 1)] + [(blocks, v) for v in range(planes * per_device)],
+        [(blocks, v) for v in range(planes * per_device)],
         temporaries=[held_b],
+        front=[(got, 0), (got, 1)],
         flops=2 * cube,
     )[0]
     return evolved.reshape(density.shape)

time: 189 us -> 184 us (0.974)
  local copies, waits for them, and re-layouts: 14.5 us -> 7.5 us
  other arithmetic: 8.37 us -> 3.85 us
  waiting for transfers between devices: 56.1 us -> 60.5 us
    unnamed x49 -> x47, local copies, waits for them, and re-layouts: 14.5 us -> 7.5 us
    pallas_call x9 -> x11, Pallas kernels: 55 us -> 61.4 us  [run_staged(): pl.pallas_call(kernel, out_shape=shapes, in_specs=[pl.BlockSpec(memory_sp...]
    pallas_call x2 -> x0, Pallas kernels: 4.63 us -> none  [run(): pl.pallas_call(kernel, out_shape=list(outs), in_specs=[flat if n in scala...]
    all_to_all x4, waiting for transfers between devices: 56.1 us -> 60.5 us  [exchange(): lax.all_to_all(message, BOTH, split_axis=0, concat_axis=0, tiled=True)]
    convert_element_type x2 -> x0, other arithmetic: 2.91 us -> none  [the longest x1 1.99 us: even_body(): swap = jnp.where(there == n, sign, 0.0).astype(BF16)]
  transfers between devices with their start and end apart: 4 -> 4, of which waited for: 4 -> 4; matrix products, arithmetic and copies ran while one was open for 5% -> 2% of each run, Pallas kernels for 15% -> 18%
where the time goes in v3:
time: 184 us; the launch traced here: 183 us
  Pallas kernels  61.4 us (33%)
  waiting for transfers between devices  60.5 us (33%)
  blocking collectives  29.9 us (16%)
  starting transfers between devices  19.2 us (10%)
  local copies, waits for them, and re-layouts  7.5 us (4%)
  other arithmetic  3.85 us (2%)
    pallas_call x11, Pallas kernels, run_staged(): pl.pallas_call(kernel, out_shape=shapes, in_specs=[pl.BlockSpec(memory_sp...  61.4 us
    all_to_all x4, waiting for transfers between devices, exchange(): lax.all_to_all(message, BOTH, split_axis=0, concat_axis=0, tiled=True)  60.5 us
    all_to_all x1, blocking collectives, exchange(): lax.all_to_all(message, BOTH, split_axis=0, concat_axis=0, tiled=True)  29.9 us
    all_to_all x4, starting transfers between devices, exchange(): lax.all_to_all(message, BOTH, split_axis=0, concat_axis=0, tiled=True)  19.2 us
    unnamed x47, local copies, waits for them, and re-layouts  7.5 us
  transfers between devices with their start and end apart: 4, of which 4 were waited for; matrix products, arithmetic and copies ran while one was open for 2% of the time, Pallas kernels for 18%

profile of v3, /device:TPU:0, one launch (start us, length us, event | category | flops | bytes accessed | tf_op | source)
XLA Modules:
  0.0 183.0 jit_solution(11936324782912941556)
XLA Ops:
  0.0 0.0 copy-start.6
  0.0 0.7 copy-done.6
  0.7 3.1 %shard_map.109 = bf16[32,2,16,512]{3,2,1,0:T(8,128)(2,1)} custom-call(f32[1,4,128,512]{3,2,1,0:T(8,128)} %bitcast.7, s32[2,4]{1,0:T(2,128)S(1)} %copy-done.6), custom_call_target="tpu_custom_call" | custom-call | flops 536870912 | bytes 2097184 | tf_op jit(solution)/shard_map/pallas_call | solution.py:565
  3.8 0.0 copy-start.13
  3.8 0.0 copy-start.14
  3.8 7.3 %all-to-all-start = ((bf16[32,2,16,512]{3,2,1,0:T(8,128)(2,1)}), bf16[32,2,16,512]{3,2,1,0:T(8,128)(2,1)S(1)}, u32[]{:S(2)}, u32[]{:S(2)}) async-start(bf16[32,2,16,512]{3,2,1,0:T(8,128)(2,1)} %shard_map.109), calls=%async_computation | async-start | bytes 2097152 | tf_op jit(solution)/shard_map/all_to_all | solution.py:970
  11.1 0.0 copy-start.15
  11.1 0.0 copy-done.13
  11.1 0.0 copy-done.14
  11.2 0.6 copy-done.15
  11.8 3.9 %shard_map.110 = (bf16[512,512]{1,0:T(8,128)(2,1)S(1)}, bf16[512,512]{1,0:T(8,128)(2,1)S(1)}, bf16[512,512]{1,0:T(8,128)(2,1)S(1)}, bf16[512,512]{1,0:T(8,128)(2,1)}) custom-call(s32[8]{0:T(128)S(1)} %copy-done.15, bf16[8,64,64]{2,1,0:T(8,128)(2,1)S(1)} %copy-done.13, bf16[8,64,64]{2,1,0:T(8,128)(2,1)S(1)} %copy-done.14), custom_call_target="tpu_custom_call" | custom-call | flops 1073741824 | bytes 2228224 | tf_op jit(solution)/shard_map/pallas_call | solution.py:565
  15.6 0.0 copy-start
  15.6 0.8 copy-done
  16.4 0.0 copy-start.16
  16.5 2.2 %fusion.17.refs_3_.refs_5_ = bf16[512,512]{1,0:T(8,128)(2,1)} fusion(s32[512]{0:T(512)S(1)} %get-tuple-element.60, s32[512]{0:T(512)S(1)} %get-tuple-element.67, s32[512]{0:T(512)S(1)} %get-tuple-element.61, s32[512]{0:T(512)S(1)} %get-tuple-element.68, s32[512]{0:T(512)S(1)} %get-tuple-element.59, s32[512]{0:T(512)S(1)} %get-tuple-element.62, ...), kind=kLoop, calls=%fused_computation.39 | loop fusion | flops 8912896 | bytes 542720 | tf_op jit(solution)/shard_map/convert_element_type | solution.py:1007
  18.7 0.0 copy-done.16
  18.7 1.4 fusion.18.refs_1_.refs_14_
  20.1 0.0 copy-start.3
  20.1 17.2 %all-to-all-done.refs_0_.refs_3_ = bf16[32,2,16,512]{3,2,1,0:T(8,128)(2,1)S(1)} async-done(((bf16[32,2,16,512]{3,2,1,0:T(8,128)(2,1)}), bf16[32,2,16,512]{3,2,1,0:T(8,128)(2,1)S(1)}, u32[]{:S(2)}, u32[]{:S(2)}) %all-to-all-start) | async-done | bytes 1048608 | tf_op jit(solution)/shard_map/all_to_all | solution.py:970
  37.3 1.0 copy-done.19
  38.3 3.9 %shard_map.111 = (bf16[32,2,16,512]{3,2,1,0:T(8,128)(2,1)}, bf16[512,512]{1,0:T(8,128)(2,1)S(1)}, bf16[512,512]{1,0:T(8,128)(2,1)S(1)}) custom-call(bf16[32,2,16,512]{3,2,1,0:T(8,128)(2,1)} %copy-done.19, bf16[512,512]{1,0:T(8,128)(2,1)S(1)} %fusion.18.refs_1_.refs_14_, bf16[512,512]{1,0:T(8,128)(2,1)} %get-tuple-element.25.refs_2_.refs_3_, ...), custom_call_target="tpu_custom_call" | custom-call | flops 1073741824 | bytes 5242880 | tf_op jit(solution)/shard_map/pallas_call | solution.py:565
  42.2 0.0 copy-done.3
  42.2 0.0 copy-start.2
  42.2 0.0 copy-start.20
  42.2 4.0 %all-to-all-start.1 = ((bf16[32,2,16,512]{3,2,1,0:T(8,128)(2,1)}), bf16[32,2,16,512]{3,2,1,0:T(8,128)(2,1)}, u32[]{:S(2)}, u32[]{:S(2)}) async-start(bf16[32,2,16,512]{3,2,1,0:T(8,128)(2,1)} %get-tuple-element.27), calls=%async_computation.1 | async-start | bytes 2097152 | tf_op jit(solution)/shard_map/all_to_all | solution.py:970
  46.2 0.0 copy-done.20
  46.2 0.0 copy-start.21
  46.2 0.1 copy.12.refs_4_
  46.2 0.6 copy-done.21
  46.9 0.1 copy.13.refs_5_
  46.9 0.6 copy-done.5
  47.5 0.1 copy.14
  47.8 0.0 copy-start.7
  47.8 0.0 copy-start.8
  47.8 0.0 copy-start.9
  47.8 0.2 select_convert_fusion.refs_2_.refs_5_.refs_3_
  48.0 0.4 copy-done.7
  48.4 0.0 copy-done.8
  48.4 0.0 copy-done.9
  48.5 4.5 %shard_map.112 = (bf16[4,512,128]{2,1,0:T(8,128)(2,1)S(1)}, bf16[512,512]{1,0:T(8,128)(2,1)S(1)}, bf16[4,512,128]{2,1,0:T(8,128)(2,1)S(1)}, bf16[512,512]{1,0:T(8,128)(2,1)}, f32[1,512]{1,0:T(1,128)S(1)}) custom-call(f32[4]{0:T(128)S(1)} %copy-done.7, f32[4]{0:T(128)S(1)} %copy-done.8, f32[4]{0:T(128)S(1)} %copy-done.9, bf16[32,2,16,512]{3,2,1,0:T(8,128)(2,1)} %copy-done.19, ...), custom_call_target="tpu_custom_call" | custom-call | flops 268435456 | bytes 3156992 | tf_op jit(solution)/shard_map/pallas_call | solution.py:565
  53.0 0.0 copy-start.10
  53.0 0.8 copy-done.10
  53.8 0.8 copy-done.11
  54.6 0.8 copy-done.12
  55.4 7.2 %shard_map.113 = (f32[512,512]{1,0:T(8,128)}, f32[512,512]{1,0:T(8,128)}) custom-call(bf16[512,512]{1,0:T(8,128)(2,1)S(1)} %get-tuple-element.28.refs_0_.refs_2_.refs_7_, bf16[512,512]{1,0:T(8,128)(2,1)S(1)} %get-tuple-element.29.refs_1_.refs_5_.refs_4_.refs_2_, bf16[128,128]{1,0:T(8,128)(2,1)S(1)} %select_convert_fusion.refs_2_.refs_5_.refs_3_, ...), custom_call_target="tpu_custom_call" | custom-call | flops 3221225472 | bytes 6334464 | tf_op jit(solution)/shard_map/pallas_call | solution.py:565
  62.6 9.6 %all-to-all-done.1.refs_0_ = bf16[32,2,16,512]{3,2,1,0:T(8,128)(2,1)} async-done(((bf16[32,2,16,512]{3,2,1,0:T(8,128)(2,1)}), bf16[32,2,16,512]{3,2,1,0:T(8,128)(2,1)}, u32[]{:S(2)}, u32[]{:S(2)}) %all-to-all-start.1) | async-done | bytes 1048608 | tf_op jit(solution)/shard_map/all_to_all | solution.py:970
  72.2 0.0 copy-done.1
  72.2 4.7 %shard_map.114 = bf16[32,2,16,512]{3,2,1,0:T(8,128)(2,1)} custom-call(bf16[32,2,16,512]{3,2,1,0:T(8,128)(2,1)} %all-to-all-done.1.refs_0_, f32[512,512]{1,0:T(8,128)} %get-tuple-element.37.refs_1_, bf16[512,512]{1,0:T(8,128)(2,1)S(1)} %get-tuple-element.28.refs_0_.refs_2_.refs_7_, bf16[512,512]{1,0:T(8,128)(2,1)S(1)} %copy-done.1, ...), custom_call_target="tpu_custom_call" | custom-call | flops 1342177280 | bytes 6291456 | tf_op jit(solution)/shard_map/pallas_call | solution.py:565
  76.9 4.0 %all-to-all-start.2 = ((bf16[32,2,16,512]{3,2,1,0:T(8,128)(2,1)}), bf16[32,2,16,512]{3,2,1,0:T(8,128)(2,1)}, u32[]{:S(2)}, u32[]{:S(2)}) async-start(bf16[32,2,16,512]{3,2,1,0:T(8,128)(2,1)} %shard_map.114), calls=%async_computation.2 | async-start | bytes 2097152 | tf_op jit(solution)/shard_map/all_to_all | solution.py:970
  80.9 9.1 %shard_map.115 = (f32[512,512]{1,0:T(8,128)}, f32[512,512]{1,0:T(8,128)}, f32[512,512]{1,0:T(8,128)}) custom-call(bf16[32,2,16,512]{3,2,1,0:T(8,128)(2,1)} %all-to-all-done.1.refs_0_, f32[512,512]{1,0:T(8,128)} %get-tuple-element.37.refs_1_, bf16[512,512]{1,0:T(8,128)(2,1)S(1)} %get-tuple-element.28.refs_0_.refs_2_.refs_7_, ...), custom_call_target="tpu_custom_call" | custom-call | flops 4026531840 | bytes 10528768 | tf_op jit(solution)/shard_map/pallas_call | solution.py:565
  89.9 16.9 %all-to-all-done.2.refs_0_ = bf16[32,2,16,512]{3,2,1,0:T(8,128)(2,1)} async-done(((bf16[32,2,16,512]{3,2,1,0:T(8,128)(2,1)}), bf16[32,2,16,512]{3,2,1,0:T(8,128)(2,1)}, u32[]{:S(2)}, u32[]{:S(2)}) %all-to-all-start.2) | async-done | bytes 1048608 | tf_op jit(solution)/shard_map/all_to_all | solution.py:970
  106.9 4.7 %shard_map.116 = bf16[32,2,16,512]{3,2,1,0:T(8,128)(2,1)} custom-call(bf16[32,2,16,512]{3,2,1,0:T(8,128)(2,1)} %all-to-all-done.2.refs_0_, f32[512,512]{1,0:T(8,128)} %get-tuple-element.39.refs_1_, bf16[512,512]{1,0:T(8,128)(2,1)S(1)} %get-tuple-element.28.refs_0_.refs_2_.refs_7_, bf16[512,512]{1,0:T(8,128)(2,1)S(1)} %copy-done.1, ...), custom_call_target="tpu_custom_call" | custom-call | flops 1342177280 | bytes 6291456 | tf_op jit(solution)/shard_map/pallas_call | solution.py:565
  111.6 4.0 %all-to-all-start.3 = ((bf16[32,2,16,512]{3,2,1,0:T(8,128)(2,1)}), bf16[32,2,16,512]{3,2,1,0:T(8,128)(2,1)}, u32[]{:S(2)}, u32[]{:S(2)}) async-start(bf16[32,2,16,512]{3,2,1,0:T(8,128)(2,1)} %shard_map.116), calls=%async_computation.3 | async-start | bytes 2097152 | tf_op jit(solution)/shard_map/all_to_all | solution.py:970
  115.6 0.0 copy-done.18
  115.6 0.0 copy-done.2
  115.6 0.0 copy-start.4
  115.6 0.0 copy-start.17
  115.6 9.2 %shard_map.117 = (f32[512,512]{1,0:T(8,128)}, f32[512,512]{1,0:T(8,128)}, f32[512,512]{1,0:T(8,128)}) custom-call(bf16[32,2,16,512]{3,2,1,0:T(8,128)(2,1)} %all-to-all-done.2.refs_0_, f32[512,512]{1,0:T(8,128)} %get-tuple-element.39.refs_1_, bf16[512,512]{1,0:T(8,128)(2,1)S(1)} %get-tuple-element.28.refs_0_.refs_2_.refs_7_, ...), custom_call_target="tpu_custom_call" | custom-call | flops 4026531840 | bytes 11577344 | tf_op jit(solution)/shard_map/pallas_call | solution.py:565
  124.8 16.8 %all-to-all-done.3.refs_0_ = bf16[32,2,16,512]{3,2,1,0:T(8,128)(2,1)} async-done(((bf16[32,2,16,512]{3,2,1,0:T(8,128)(2,1)}), bf16[32,2,16,512]{3,2,1,0:T(8,128)(2,1)}, u32[]{:S(2)}, u32[]{:S(2)}) %all-to-all-start.3) | async-done | bytes 1048608 | tf_op jit(solution)/shard_map/all_to_all | solution.py:970
  141.5 0.0 copy-done.4
  141.5 0.0 copy-done.17
  141.5 8.5 %shard_map.118 = bf16[32,2,16,512]{3,2,1,0:T(8,128)(2,1)} custom-call(bf16[32,2,16,512]{3,2,1,0:T(8,128)(2,1)} %all-to-all-done.3.refs_0_, f32[512,512]{1,0:T(8,128)} %get-tuple-element.42.refs_1_, bf16[512,512]{1,0:T(8,128)(2,1)S(1)} %get-tuple-element.29.refs_1_.refs_5_.refs_4_.refs_2_, bf16[128,128]{1,0:T(8,128)(2,1)S(1)} %select_convert_fusion.refs_2_.refs_5_.refs_3_, ...), custom_call_target="tpu_custom_call" | custom-call | flops 3221225472 | bytes 9480192 | tf_op jit(solution)/shard_map/pallas_call | solution.py:565
  150.1 29.9 %all_to_all.25.refs_0_ = bf16[32,2,16,512]{3,2,1,0:T(8,128)(2,1)S(1)} all-to-all(bf16[32,2,16,512]{3,2,1,0:T(8,128)(2,1)} %shard_map.118), channel_id=1, replica_groups=mesh['aux'=8,'row'=4] {'aux','row'}, dimensions={0} | all-to-all | bytes 2097152 | tf_op jit(solution)/shard_map/all_to_all | solution.py:970
  180.0 2.8 %shard_map.119 = f32[1,4,128,512]{3,2,1,0:T(8,128)} custom-call(bf16[32,2,16,512]{3,2,1,0:T(8,128)(2,1)S(1)} %all_to_all.25.refs_0_, f32[1,4,128,512]{3,2,1,0:T(8,128)} %bitcast.8), custom_call_target="tpu_custom_call" | custom-call | flops 536870912 | bytes 3145728 | tf_op jit(solution)/shard_map/pallas_call | solution.py:565
  (23 shorter events, 0.1 us)
Async XLA Ops:
  0.0 0.7 copy-start.6
  3.8 7.4 %copy-start.13 = (bf16[8,64,64]{2,1,0:T(8,128)(2,1)S(1)}, bf16[8,64,64]{2,1,0:T(8,128)(2,1)}, u32[]{:S(2)}) copy-start(bf16[8,64,64]{2,1,0:T(8,128)(2,1)} %refs_1_.4) | copy-start | bytes 196612
  3.8 7.4 %copy-start.14 = (bf16[8,64,64]{2,1,0:T(8,128)(2,1)S(1)}, bf16[8,64,64]{2,1,0:T(8,128)(2,1)}, u32[]{:S(2)}) copy-start(bf16[8,64,64]{2,1,0:T(8,128)(2,1)} %refs_2_.2) | copy-start | bytes 196612
  3.8 33.5 %all-to-all-start = ((bf16[32,2,16,512]{3,2,1,0:T(8,128)(2,1)}), bf16[32,2,16,512]{3,2,1,0:T(8,128)(2,1)S(1)}, u32[]{:S(2)}, u32[]{:S(2)}) async-start(bf16[32,2,16,512]{3,2,1,0:T(8,128)(2,1)} %shard_map.109), calls=%async_computation | async-start | bytes 2097152 | tf_op jit(solution)/shard_map/all_to_all | solution.py:970
  11.1 0.7 copy-start.15
  15.6 0.8 copy-start
  16.4 2.3 %copy-start.16 = (bf16[512,512]{1,0:T(8,128)(2,1)}, bf16[512,512]{1,0:T(8,128)(2,1)S(1)}, u32[]{:S(2)}) copy-start(bf16[512,512]{1,0:T(8,128)(2,1)S(1)} %get-tuple-element.34.refs_8_.refs_11_.refs_4_) | copy-start | bytes 1572868
  16.4 99.2 %copy-start.18 = (bf16[512,512]{1,0:T(8,128)(2,1)}, bf16[512,512]{1,0:T(8,128)(2,1)S(1)}, u32[]{:S(2)}) copy-start(bf16[512,512]{1,0:T(8,128)(2,1)S(1)} %get-tuple-element.31.refs_5_.refs_8_.refs_11_) | copy-start | bytes 1572868
  20.1 22.0 %copy-start.3 = (bf16[512,512]{1,0:T(8,128)(2,1)}, bf16[512,512]{1,0:T(8,128)(2,1)S(1)}, u32[]{:S(2)}) copy-start(bf16[512,512]{1,0:T(8,128)(2,1)S(1)} %fusion.18.refs_1_.refs_14_) | copy-start | bytes 1572868
  37.3 1.0 copy-start.19
  42.2 73.4 %copy-start.2 = (bf16[512,512]{1,0:T(8,128)(2,1)}, bf16[512,512]{1,0:T(8,128)(2,1)S(1)}, u32[]{:S(2)}) copy-start(bf16[512,512]{1,0:T(8,128)(2,1)S(1)} %get-tuple-element.28.refs_0_.refs_2_.refs_7_) | copy-start | bytes 1572868
  42.2 4.0 %copy-start.20 = (s32[16,8]{0,1:T(8,128)S(1)}, s32[16,8]{0,1:T(8,128)}, u32[]{:S(2)}) copy-start(s32[16,8]{0,1:T(8,128)} %param.17) | copy-start | bytes 1540
  42.2 30.0 %all-to-all-start.1 = ((bf16[32,2,16,512]{3,2,1,0:T(8,128)(2,1)}), bf16[32,2,16,512]{3,2,1,0:T(8,128)(2,1)}, u32[]{:S(2)}, u32[]{:S(2)}) async-start(bf16[32,2,16,512]{3,2,1,0:T(8,128)(2,1)} %get-tuple-element.27), calls=%async_computation.1 | async-start | bytes 2097152 | tf_op jit(solution)/shard_map/all_to_all | solution.py:970
  46.2 0.7 copy-start.21
  46.9 0.7 copy-start.5
  47.8 0.7 copy-start.7
  47.8 0.7 copy-start.8
  47.8 0.7 copy-start.9
  53.0 0.8 copy-start.10
  53.8 0.8 copy-start.11
  54.6 0.8 copy-start.12
  55.4 16.8 %copy-start.1 = (bf16[512,512]{1,0:T(8,128)(2,1)S(1)}, bf16[512,512]{1,0:T(8,128)(2,1)}, u32[]{:S(2)}) copy-start(bf16[512,512]{1,0:T(8,128)(2,1)} %get-tuple-element.25.refs_2_.refs_3_) | copy-start | bytes 1572868
  76.9 30.0 %all-to-all-start.2 = ((bf16[32,2,16,512]{3,2,1,0:T(8,128)(2,1)}), bf16[32,2,16,512]{3,2,1,0:T(8,128)(2,1)}, u32[]{:S(2)}, u32[]{:S(2)}) async-start(bf16[32,2,16,512]{3,2,1,0:T(8,128)(2,1)} %shard_map.114), calls=%async_computation.2 | async-start | bytes 2097152 | tf_op jit(solution)/shard_map/all_to_all | solution.py:970
  111.6 30.0 %all-to-all-start.3 = ((bf16[32,2,16,512]{3,2,1,0:T(8,128)(2,1)}), bf16[32,2,16,512]{3,2,1,0:T(8,128)(2,1)}, u32[]{:S(2)}, u32[]{:S(2)}) async-start(bf16[32,2,16,512]{3,2,1,0:T(8,128)(2,1)} %shard_map.116), calls=%async_computation.3 | async-start | bytes 2097152 | tf_op jit(solution)/shard_map/all_to_all | solution.py:970
  115.6 25.9 %copy-start.4 = (bf16[512,512]{1,0:T(8,128)(2,1)S(1)}, bf16[512,512]{1,0:T(8,128)(2,1)}, u32[]{:S(2)}) copy-start(bf16[512,512]{1,0:T(8,128)(2,1)} %fusion.17.refs_3_.refs_5_) | copy-start | bytes 1572868
  115.6 25.9 %copy-start.17 = (bf16[512,512]{1,0:T(8,128)(2,1)S(1)}, bf16[512,512]{1,0:T(8,128)(2,1)}, u32[]{:S(2)}) copy-start(bf16[512,512]{1,0:T(8,128)(2,1)} %copy-done.16) | copy-start | bytes 1572868

commit v4 on v3

--- a/solution.py
+++ b/solution.py
@@ -13,6 +13,8 @@
 STEP = 0.5
 BOTH = ("aux", "row")
 GRANT = 52 << 20
+MOST = 60 << 20
+ROWS = 512
 
 F32 = jnp.float32
 BF16 = jnp.bfloat16
@@ -90,9 +92,10 @@
 def turn(s, load, order, swap, put):
     size = order.shape[0]
     span = size // s.local
-    for block in range(s.extent // size):
+    blocks = s.extent // size
+    parts = []
+    for block in range(blocks):
         moved = dot(order[...], load(block * size, size))
-        parts = []
         for ih in range(s.tiles):
             for jh in range(s.tiles):
                 lanes = slice(jh * s.tile, (jh + 1) * s.tile)
@@ -101,10 +104,11 @@
                     for f in range(s.fold)
                 ]
                 parts.append(jnp.concatenate(pieces, axis=1) if s.fold > 1 else pieces[0])
-        turned = dot(jnp.concatenate(parts, axis=0).astype(BF16), swap[...])
+    turned = dot(jnp.concatenate(parts, axis=0).astype(BF16), swap[...])
+    for block in range(blocks):
         for ih in range(s.tiles):
             for jh in range(s.tiles):
-                start = (ih * s.tiles + jh) * span
+                start = ((block * s.tiles + ih) * s.tiles + jh) * span
                 for f in range(s.fold):
                     first = (jh * s.fold + f) * s.devices + block * span
                     put(
@@ -519,7 +523,7 @@
             made.wait()
 
 
-def run_staged(body, outs, args, temporaries=(), scalars=(), front=(), lead=None, flops=0):
+def run_staged(body, outs, args, temporaries=(), scalars=(), front=(), lead=None, grant=GRANT, flops=0):
     arrays, views = [], []
     for arg in [*front, *args]:
         array, part = arg if isinstance(arg, tuple) else (arg, None)
@@ -568,7 +572,7 @@
         in_specs=[pl.BlockSpec(memory_space=pltpu.SMEM)] * len(scalars) + [far] * len(arrays),
         out_specs=[far] * len(shapes),
         scratch_shapes=buffers + results + list(temporaries) + [pltpu.SemaphoreType.DMA((count,))],
-        compiler_params=pltpu.CompilerParams(vmem_limit_bytes=GRANT),
+        compiler_params=pltpu.CompilerParams(vmem_limit_bytes=grant),
         cost_estimate=pl.CostEstimate(flops=flops, bytes_accessed=moved, transcendentals=0),
     )(*scalars, *arrays)
 
@@ -590,28 +594,28 @@
     blocks = s.extent // s.band
     which = lax.axis_index("row") % s.per_device
     flats = [stage.need(v)[...].reshape(s.band, s.extent).astype(BF16) for v in range(blocks)]
-    row, lane = iotas(128, s.band)
+    row, lane = iotas(ROWS, s.band)
     counts = stage.need(blocks)[...].astype(F32)
     mine = counts[0:1, :]
     for n in range(1, s.per_device):
         mine = jnp.where(which == n, counts[n : n + 1, :], mine)
     for v in range(blocks):
         count = mine[:, v : v + 1]
-        for b in row_blocks(s.extent):
-            value = dot(post[b : b + 128, :], flats[v], ((1,), (1,)))
+        for b in row_blocks(s.extent, ROWS):
+            value = dot(post[b : b + ROWS, :], flats[v], ((1,), (1,)))
             own = (row % s.local == 0) & (lane == (row + b) // s.local)
             value = jnp.where(own, count, value).astype(BF16)
             fill(s, stage.results[1], b, value, slice(v * s.band, (v + 1) * s.band))
     stage.send(1)
     flat = jnp.concatenate(flats, axis=0)
-    for b in row_blocks(s.extent):
-        fill(s, stage.results[0], b, dot(post[b : b + 128, :], flat).astype(BF16))
+    for b in row_blocks(s.extent, ROWS):
+        fill(s, stage.results[0], b, dot(post[b : b + ROWS, :], flat).astype(BF16))
     stage.send(0)
 
 
 def send_products(s, stage, matrix, state_ref, index):
-    for b in row_blocks(s.extent):
-        fill(s, stage.results[index], b, dot(matrix[b : b + 128, :], state_ref[...]).astype(BF16))
+    for b in row_blocks(s.extent, ROWS):
+        fill(s, stage.results[index], b, dot(matrix[b : b + ROWS, :], state_ref[...]).astype(BF16))
     stage.send(index)
 
 
@@ -620,9 +624,9 @@
     me = lax.axis_index("aux") * s.rows + lax.axis_index("row")
     everyone = slice(0, s.devices)
     rows_in, row_lanes = stage.front(0), stage.need(0)
-    for b in row_blocks(s.extent):
-        s_ref[b : b + 128, :] = dot(
-            flat_rows(rows_in, everyone, slice(b, b + 128)), row_lanes[...], ((0,), (0,))
+    for b in row_blocks(s.extent, ROWS):
+        s_ref[b : b + ROWS, :] = dot(
+            flat_rows(rows_in, everyone, slice(b, b + ROWS)), row_lanes[...], ((0,), (0,))
         ).astype(BF16)
     stage.send(2)
     send_products(s, stage, stage.need(1), s_ref, 1)
@@ -666,11 +670,9 @@
     turn(s, load, order, swap, put)
 
 
-def updates(s, step, sign, k_ref, d_ref, keep):
+def updates(scale, base_ref, keep):
     def put(rows, lanes, value):
-        own = k_ref[rows, lanes]
-        slope = own + value if sign > 0 else own - value
-        keep(rows, lanes, d_ref[rows, lanes].astype(F32) + step * slope)
+        keep(rows, lanes, base_ref[rows, lanes] + scale * value)
 
     return put
 
@@ -687,19 +689,19 @@
 
     got = stage.front(0)
     stage.start_rest()
-    even_turn(s, got, order, swap, updates(s, step, 1, stage.need(0), stage.need(1), keep_in(s_ref)))
-    send_products(s, stage, stage.need(2), s_ref, 1)
-    got = stage.need(3)
-    even_turn(s, got, order, swap, updates(s, step, -1, stage.need(4), stage.need(5), keep_in(t_ref)))
-    send_products(s, stage, stage.need(6), t_ref, 0)
+    even_turn(s, got, order, swap, updates(step, stage.need(0), keep_in(s_ref)))
+    send_products(s, stage, stage.need(1), s_ref, 1)
+    got = stage.need(2)
+    even_turn(s, got, order, swap, updates(-step, stage.need(3), keep_in(t_ref)))
+    send_products(s, stage, stage.need(4), t_ref, 0)
 
 
 def even_slope_part(s, direct, mirror, y_ref, h, unit, damp, q_ref, wa, wb, turned, sign, put):
     for th in range(s.tiles):
         lanes = slice(th * s.tile, (th + 1) * s.tile)
         turned[:, lanes] = dot(direct[:, lanes], unit[...]).astype(BF16)
-    for b in row_blocks(s.extent):
-        rows = slice(b, b + 128)
+    for b in row_blocks(s.extent, ROWS):
+        rows = slice(b, b + ROWS)
         whole = dot(h[rows, :], turned[...])
         for th in range(s.tiles):
             lanes = slice(th * s.tile, (th + 1) * s.tile)
@@ -713,29 +715,27 @@
             put(rows, lanes, total)
 
 
-def put_in(ref):
+def put_base(ref, start_ref, step):
     def put(rows, lanes, value):
-        ref[rows, lanes] = value
+        ref[rows, lanes] = start_ref[rows, lanes].astype(F32) + step * value
 
     return put
 
 
-def even_first_slope(s, stage, small, temporaries):
+def even_first_slope(s, step, stage, small, temporaries):
     (turned,) = temporaries
     need = stage.need
     first, second = stage.results
     s_ref, t_ref, unit, damp, q_ref = need(0), need(1), need(2), need(3), need(4)
-    even_slope_part(
-        s, s_ref, t_ref, s_ref, need(5), unit, damp, q_ref, need(6), need(7), turned, -1.0, put_in(first)
-    )
+    put = put_base(first, s_ref, step)
+    even_slope_part(s, s_ref, t_ref, s_ref, need(5), unit, damp, q_ref, need(6), need(7), turned, -1.0, put)
     stage.send(0)
-    even_slope_part(
-        s, t_ref, s_ref, t_ref, need(8), unit, damp, q_ref, need(9), need(10), turned, 1.0, put_in(second)
-    )
+    put = put_base(second, t_ref, step)
+    even_slope_part(s, t_ref, s_ref, t_ref, need(8), unit, damp, q_ref, need(9), need(10), turned, 1.0, put)
     stage.send(1)
 
 
-def even_slope(s, step, ratio, has_total, stage, small, temporaries):
+def even_slope(s, step, next_step, ratio, less, has_total, stage, small, temporaries):
     turned, s_ref, t_ref, ys_ref, yt_ref, order, swap = temporaries
     turn_matrices(s, order, swap)
     need = stage.need
@@ -748,35 +748,21 @@
 
         return keep
 
-    ds_ref = need(1)
-    even_turn(
-        s,
-        stage.front(0),
-        order,
-        swap,
-        updates(s, step, 1, need(0), ds_ref, keep_in(s_ref, ys_ref)),
-    )
-    even_turn(
-        s,
-        stage.front(1),
-        order,
-        swap,
-        updates(s, step, -1, need(2), need(3), keep_in(t_ref, yt_ref)),
-    )
+    even_turn(s, stage.front(0), order, swap, updates(step, need(0), keep_in(s_ref, ys_ref)))
+    even_turn(s, stage.front(1), order, swap, updates(-step, need(1), keep_in(t_ref, yt_ref)))
+    ds_ref, dt_ref = need(2), need(3)
     total_in = need(13) if has_total else None
     for b in row_blocks(s.extent, 64):
         rows = slice(b, b + 64)
-        grown = ratio * (ys_ref[rows, :] - ds_ref[rows, :].astype(F32))
+        grown = ratio * ys_ref[rows, :] - (ratio + less) * ds_ref[rows, :].astype(F32)
         total_ref[rows, :] = total_in[rows, :] + grown if has_total else grown
     stage.send(2)
     unit, damp, q_ref = need(4), need(5), need(6)
-    even_slope_part(
-        s, s_ref, t_ref, ys_ref, need(7), unit, damp, q_ref, need(8), need(9), turned, -1.0, put_in(first)
-    )
+    put = put_base(first, ds_ref, next_step)
+    even_slope_part(s, s_ref, t_ref, ys_ref, need(7), unit, damp, q_ref, need(8), need(9), turned, -1.0, put)
     stage.send(0)
-    even_slope_part(
-        s, t_ref, s_ref, yt_ref, need(10), unit, damp, q_ref, need(11), need(12), turned, 1.0, put_in(second)
-    )
+    put = put_base(second, dt_ref, next_step)
+    even_slope_part(s, t_ref, s_ref, yt_ref, need(10), unit, damp, q_ref, need(11), need(12), turned, 1.0, put)
     stage.send(1)
 
 
@@ -788,16 +774,15 @@
     def keep_columns(rows, lanes, value):
         t_ref[rows, lanes] = value.astype(BF16)
 
-    put = updates(s, step, -1, need(0), need(1), keep_columns)
     got = stage.front(0)
     stage.start_rest()
-    even_turn(s, got, order, swap, put)
-    unit, left, column_lanes = need(2), need(3), need(4)
+    even_turn(s, got, order, swap, updates(-step, need(0), keep_columns))
+    unit, left, column_lanes = need(1), need(2), need(3)
     for th in range(s.tiles):
         lanes = slice(th * s.tile, (th + 1) * s.tile)
         turned[:, lanes] = dot(t_ref[:, lanes], unit[...]).astype(BF16)
-    for b in row_blocks(s.extent):
-        rows = slice(b, b + 128)
+    for b in row_blocks(s.extent, ROWS):
+        rows = slice(b, b + ROWS)
         grown[rows, :] = (weight * dot(left[rows, :], turned[...])).astype(BF16)
     out = stage.results[1]
     for q in range(s.rows):
@@ -812,21 +797,19 @@
         ys_ref[rows, lanes] = value
         s_ref[rows, lanes] = value.astype(BF16)
 
-    ds_ref = need(6)
-    put = updates(s, step, 1, need(5), ds_ref, keep_rows)
-    even_turn(s, stage.front(1), order, swap, put)
-    total_in = need(7)
+    even_turn(s, stage.front(1), order, swap, updates(step, need(4), keep_rows))
+    total_in = need(5)
 
     def put_change(rows, lanes, value):
-        change = total_in[rows, lanes] + ratio * (ys_ref[rows, lanes] - ds_ref[rows, lanes].astype(F32))
+        change = total_in[rows, lanes] + ratio * ys_ref[rows, lanes]
         grown[rows, lanes] = (change + weight * value).astype(BF16)
 
     even_slope_part(
-        s, s_ref, t_ref, ys_ref, need(10), unit, need(8), need(9), need(11), need(12), turned, -1.0, put_change
-    )
-    row_lanes = need(13)
-    for b in row_blocks(s.extent):
-        fill(s, stage.results[0], b, dot(row_lanes[b : b + 128, :], grown[...], ((1,), (1,))).astype(BF16))
+        s, s_ref, t_ref, ys_ref, need(8), unit, need(6), need(7), need(9), need(10), turned, -1.0, put_change
+    )
+    row_lanes = need(11)
+    for b in row_blocks(s.extent, ROWS):
+        fill(s, stage.results[0], b, dot(row_lanes[b : b + ROWS, :], grown[...], ((1,), (1,))).astype(BF16))
     stage.send(0)
 
 
@@ -859,8 +842,8 @@
         left[b * block : (b + 1) * block, :] = (dot(own_ref[b], to_own) + dot(outer_ref[b], to_far)).astype(BF16)
     row, column = iotas(s.extent, s.extent)
     same = mask_to(row == column)
-    for b in row_blocks(s.extent):
-        rows = slice(b, b + 128)
+    for b in row_blocks(s.extent, ROWS):
+        rows = slice(b, b + ROWS)
         right[rows, :] = dot(same[rows, :], left[...], ((1,), (1,))).astype(BF16)
         left_rows[rows, :] = dot(post[rows, :], left[...]).astype(BF16)
         right_rows[rows, :] = dot(post[rows, :], left[...], ((1,), (1,))).astype(BF16)
@@ -975,6 +958,7 @@
         [pair],
         [(blocks, v) for v in range(planes * per_device)] + [tier_counts],
         temporaries=[held_b],
+        grant=MOST,
         flops=2 * cube,
     )[0]
     got = exchange(message)
@@ -985,6 +969,7 @@
         [block_diagonal, block_outer],
         temporaries=[held_b],
         scalars=[block_column],
+        grant=MOST,
         flops=4 * cube,
     )
     q_first = couplings.T
@@ -1017,6 +1002,7 @@
         [pair, state, state],
         [row_lanes, right_rows, column_lanes, left_rows],
         front=[(got, 0), (got, 1)],
+        grant=MOST,
         flops=4 * cube,
     )
     wa = shape(s.tiles, 4 * s.tile, s.tile, dtype=BF16)
@@ -1026,14 +1012,16 @@
         [wa, wb, wa, wb, shape(1, s.lanes)],
         [(got, 1), link_index, link_mirror, couplings],
         scalars=[weight_real, weight_imag, mode_rates],
+        grant=MOST,
         flops=cube,
     )
     tables = [unit, damp, q_first, right, wa_s, wb_s, left, wa_t, wb_t]
     shares = [STEP / 6.0, STEP / 3.0, STEP / 3.0, STEP / 6.0]
     steps = [0.25, 0.25, 0.5]
+    ratios = [share / step for share, step in zip(shares, steps)]
     got = exchange(message)
-    ks, kt = run_staged(
-        functools.partial(even_first_slope, s),
+    base_s, base_t = run_staged(
+        functools.partial(even_first_slope, s, steps[0]),
         [full, full],
         [s_now, t_now] + tables,
         temporaries=[held_b],
@@ -1045,29 +1033,27 @@
         message = run_staged(
             functools.partial(even_next, s, step),
             [pair],
-            [ks, s_now, right_rows, (got, 1), kt, t_now, left_rows],
+            [base_s, right_rows, (got, 1), base_t, left_rows],
             temporaries=[held_b, held_b, order, swap],
             front=[(got, 0)],
-            lead=3,
             flops=5 * cube,
         )[0]
         arrived, got = got, exchange(message)
-        ks, kt, total = run_staged(
-            functools.partial(even_slope, s, step, shares[section] / step, total is not None),
+        less = ratios[2] if section == 1 else 0.0
+        base_s, base_t, total = run_staged(
+            functools.partial(even_slope, s, step, steps[section + 1], ratios[section], less, total is not None),
             [full, full, full],
-            [ks, s_now, kt, t_now] + tables + ([] if total is None else [total]),
+            [base_s, base_t, s_now, t_now] + tables + ([] if total is None else [total]),
             temporaries=[held_b, held_b, held_b, held, held, order, swap],
             front=[(arrived, 0), (arrived, 1)],
             flops=15 * cube,
         )
     message = run_staged(
-        functools.partial(even_last, s, steps[2], shares[2] / steps[2], shares[3]),
+        functools.partial(even_last, s, steps[2], ratios[2], shares[3]),
         [pair],
-        [kt, t_now, unit, left, column_lanes, ks, s_now, total]
-        + [damp, q_first, right, wa_s, wb_s, row_lanes],
+        [base_t, unit, left, column_lanes, base_s, total, damp, q_first, right, wa_s, wb_s, row_lanes],
         temporaries=[held, held_b, held_b, held_b, held_b, order, swap],
         front=[(got, 1), (got, 0)],
-        lead=4,
         flops=12 * cube,
     )[0]
     got = exchange(message)

time: 184 us -> 182 us (0.989)
  local copies, waits for them, and re-layouts: 7.5 us -> 3.16 us
  waiting for transfers between devices: 60.5 us -> 62.7 us
    unnamed x47 -> x27, local copies, waits for them, and re-layouts: 7.5 us -> 3.16 us
    all_to_all x4, waiting for transfers between devices: 60.5 us -> 62.7 us  [exchange(): lax.all_to_all(message, BOTH, split_axis=0, concat_axis=0, tiled=True)]
  transfers between devices with their start and end apart: 4 -> 4, of which waited for: 4 -> 4; matrix products, arithmetic and copies ran while one was open for 2% -> 3% of each run, Pallas kernels for 18% -> 19%
where the time goes in v4:
time: 182 us; the launch traced here: 181 us
  waiting for transfers between devices  62.7 us (34%)
  Pallas kernels  60.7 us (33%)
  blocking collectives  29.9 us (16%)
  starting transfers between devices  19.2 us (11%)
  other arithmetic  4.79 us (3%)
  local copies, waits for them, and re-layouts  3.16 us (2%)
    all_to_all x4, waiting for transfers between devices, exchange(): lax.all_to_all(message, BOTH, split_axis=0, concat_axis=0, tiled=True)  62.7 us
    pallas_call x11, Pallas kernels, run_staged(): pl.pallas_call(kernel, out_shape=shapes, in_specs=[pl.BlockSpec(memory_sp...  60.7 us
    all_to_all x1, blocking collectives, exchange(): lax.all_to_all(message, BOTH, split_axis=0, concat_axis=0, tiled=True)  29.9 us
    all_to_all x4, starting transfers between devices, exchange(): lax.all_to_all(message, BOTH, split_axis=0, concat_axis=0, tiled=True)  19.2 us
  transfers between devices with their start and end apart: 4, of which 4 were waited for; matrix products, arithmetic and copies ran while one was open for 3% of the time, Pallas kernels for 19%

profile of v4, /device:TPU:0, one launch (start us, length us, event | category | flops | bytes accessed | tf_op | source)
XLA Modules:
  0.0 181.0 jit_solution(8992956932817929365)
XLA Ops:
  0.0 3.0 %shard_map.109 = bf16[32,2,16,512]{3,2,1,0:T(8,128)(2,1)} custom-call(f32[1,4,128,512]{3,2,1,0:T(8,128)} %bitcast.7, s32[2,4]{1,0:T(2,128)} %refs_1_.3), custom_call_target="tpu_custom_call" | custom-call | flops 536870912 | bytes 2097184 | tf_op jit(solution)/shard_map/pallas_call | solution.py:569
  3.0 7.3 %all-to-all-start = ((bf16[32,2,16,512]{3,2,1,0:T(8,128)(2,1)}), bf16[32,2,16,512]{3,2,1,0:T(8,128)(2,1)S(1)}, u32[]{:S(2)}, u32[]{:S(2)}) async-start(bf16[32,2,16,512]{3,2,1,0:T(8,128)(2,1)} %shard_map.109), calls=%async_computation | async-start | bytes 2097152 | tf_op jit(solution)/shard_map/all_to_all | solution.py:953
  10.4 3.8 %shard_map.110 = (bf16[512,512]{1,0:T(8,128)(2,1)}, bf16[512,512]{1,0:T(8,128)(2,1)}, bf16[512,512]{1,0:T(8,128)(2,1)}, bf16[512,512]{1,0:T(8,128)(2,1)}) custom-call(s32[8]{0:T(128)} %refs_0_.2, bf16[8,64,64]{2,1,0:T(8,128)(2,1)} %refs_1_.4, bf16[8,64,64]{2,1,0:T(8,128)(2,1)} %refs_2_.2), custom_call_target="tpu_custom_call" | custom-call | flops 1073741824 | bytes 2228224 | tf_op jit(solution)/shard_map/pallas_call | solution.py:569
  14.3 2.2 %fusion.17.refs_3_.refs_4_ = bf16[512,512]{1,0:T(8,128)(2,1)} fusion(s32[512]{0:T(512)S(1)} %get-tuple-element.60, s32[512]{0:T(512)S(1)} %get-tuple-element.67, s32[512]{0:T(512)S(1)} %get-tuple-element.61, s32[512]{0:T(512)S(1)} %get-tuple-element.68, s32[512]{0:T(512)S(1)} %get-tuple-element.59, s32[512]{0:T(512)S(1)} %get-tuple-element.62, ...), kind=kLoop, calls=%fused_computation.39 | loop fusion | flops 8912896 | bytes 542720 | tf_op jit(solution)/shard_map/convert_element_type | solution.py:992
  16.5 2.3 %fusion.18.refs_1_.refs_12_ = bf16[512,512]{1,0:T(8,128)(2,1)} fusion(s32[512]{0:T(512)S(1)} %get-tuple-element.45, s32[512]{0:T(512)S(1)} %get-tuple-element.55, s32[512]{0:T(512)S(1)} %get-tuple-element.46, s32[512]{0:T(512)S(1)} %get-tuple-element.56, s32[512]{0:T(512)S(1)} %get-tuple-element.47, s32[512]{0:T(512)S(1)} %get-tuple-element.57, ...), kind=kLoop, calls=%fused_computation.40 | loop fusion | flops 12582912 | bytes 547328 | tf_op jit(solution)/shard_map/convert_element_type | solution.py:985
  18.8 17.8 %all-to-all-done.refs_0_.refs_3_ = bf16[32,2,16,512]{3,2,1,0:T(8,128)(2,1)S(1)} async-done(((bf16[32,2,16,512]{3,2,1,0:T(8,128)(2,1)}), bf16[32,2,16,512]{3,2,1,0:T(8,128)(2,1)S(1)}, u32[]{:S(2)}, u32[]{:S(2)}) %all-to-all-start) | async-done | bytes 1048608 | tf_op jit(solution)/shard_map/all_to_all | solution.py:953
  36.6 0.0 copy-start.8
  36.6 1.0 copy-done.8
  37.6 4.1 %shard_map.111 = (bf16[32,2,16,512]{3,2,1,0:T(8,128)(2,1)}, bf16[512,512]{1,0:T(8,128)(2,1)}, bf16[512,512]{1,0:T(8,128)(2,1)}) custom-call(bf16[32,2,16,512]{3,2,1,0:T(8,128)(2,1)} %copy-done.8, bf16[512,512]{1,0:T(8,128)(2,1)} %fusion.18.refs_1_.refs_12_, bf16[512,512]{1,0:T(8,128)(2,1)} %get-tuple-element.25.refs_2_, ...), custom_call_target="tpu_custom_call" | custom-call | flops 1073741824 | bytes 5242880 | tf_op jit(solution)/shard_map/pallas_call | solution.py:569
  41.7 0.0 copy-start.10
  41.7 0.0 copy-start.7
  41.7 3.9 %all-to-all-start.1 = ((bf16[32,2,16,512]{3,2,1,0:T(8,128)(2,1)}), bf16[32,2,16,512]{3,2,1,0:T(8,128)(2,1)}, u32[]{:S(2)}, u32[]{:S(2)}) async-start(bf16[32,2,16,512]{3,2,1,0:T(8,128)(2,1)} %get-tuple-element.27), calls=%async_computation.1 | async-start | bytes 2097152 | tf_op jit(solution)/shard_map/all_to_all | solution.py:953
  45.6 0.0 copy-done.10
  45.6 0.0 copy-start.11
  45.7 0.7 copy.12.refs_4_
  46.3 0.0 copy-done.11
  46.3 0.0 copy-start.9
  46.3 0.7 copy.13.refs_5_
  47.0 0.0 copy-done.9
  47.0 0.1 copy.14
  47.2 0.2 select_convert_fusion.refs_2_.refs_5_
  47.4 0.0 copy-start.4
  47.4 0.0 copy-start.5
  47.4 5.4 %shard_map.112 = (bf16[4,512,128]{2,1,0:T(8,128)(2,1)}, bf16[512,512]{1,0:T(8,128)(2,1)}, bf16[4,512,128]{2,1,0:T(8,128)(2,1)}, bf16[512,512]{1,0:T(8,128)(2,1)}, f32[1,512]{1,0:T(1,128)}) custom-call(f32[4]{0:T(128)} %refs_0_.3, f32[4]{0:T(128)} %refs_1_.5, f32[4]{0:T(128)} %refs_2_.3, bf16[32,2,16,512]{3,2,1,0:T(8,128)(2,1)} %copy-done.8, ...), custom_call_target="tpu_custom_call" | custom-call | flops 268435456 | bytes 3156992 | tf_op jit(solution)/shard_map/pallas_call | solution.py:569
  52.8 0.0 copy-start.3
  52.8 0.0 copy-done.7
  52.8 0.0 copy-done.4
  52.8 0.0 copy-done.5
  52.9 0.6 copy-done.3
  53.5 0.0 copy-start
  53.5 0.0 copy-start.1
  53.5 7.3 %shard_map.113 = (f32[512,512]{1,0:T(8,128)}, f32[512,512]{1,0:T(8,128)}) custom-call(bf16[512,512]{1,0:T(8,128)(2,1)S(1)} %copy-done.4, bf16[512,512]{1,0:T(8,128)(2,1)S(1)} %copy-done.5, bf16[128,128]{1,0:T(8,128)(2,1)S(1)} %select_convert_fusion.refs_2_.refs_5_, f32[1,512]{1,0:T(1,128)S(1)} %copy-done.3, f32[512,4]{1,0:T(8,128)S(1)} %bitcast.3, ...), custom_call_target="tpu_custom_call" | custom-call | flops 3221225472 | bytes 6334464 | tf_op jit(solution)/shard_map/pallas_call | solution.py:569
  60.8 10.9 %all-to-all-done.1.refs_0_ = bf16[32,2,16,512]{3,2,1,0:T(8,128)(2,1)} async-done(((bf16[32,2,16,512]{3,2,1,0:T(8,128)(2,1)}), bf16[32,2,16,512]{3,2,1,0:T(8,128)(2,1)}, u32[]{:S(2)}, u32[]{:S(2)}) %all-to-all-start.1) | async-done | bytes 1048608 | tf_op jit(solution)/shard_map/all_to_all | solution.py:953
  71.7 0.0 copy-done
  71.7 0.0 copy-done.1
  71.7 4.3 %shard_map.114 = bf16[32,2,16,512]{3,2,1,0:T(8,128)(2,1)} custom-call(bf16[32,2,16,512]{3,2,1,0:T(8,128)(2,1)} %all-to-all-done.1.refs_0_, f32[512,512]{1,0:T(8,128)} %get-tuple-element.37.refs_1_, bf16[512,512]{1,0:T(8,128)(2,1)S(1)} %copy-done.1, f32[512,512]{1,0:T(8,128)} %get-tuple-element.38.refs_3_.refs_2_, bf16[512,512]{1,0:T(8,128)(2,1)S(1)} %copy-done), custom_call_target="tpu_custom_call" | custom-call | flops 1342177280 | bytes 5242880 | tf_op jit(solution)/shard_map/pallas_call | solution.py:569
  76.0 4.0 %all-to-all-start.2 = ((bf16[32,2,16,512]{3,2,1,0:T(8,128)(2,1)}), bf16[32,2,16,512]{3,2,1,0:T(8,128)(2,1)}, u32[]{:S(2)}, u32[]{:S(2)}) async-start(bf16[32,2,16,512]{3,2,1,0:T(8,128)(2,1)} %shard_map.114), calls=%async_computation.2 | async-start | bytes 2097152 | tf_op jit(solution)/shard_map/all_to_all | solution.py:953
  80.0 8.7 %shard_map.115 = (f32[512,512]{1,0:T(8,128)}, f32[512,512]{1,0:T(8,128)}, f32[512,512]{1,0:T(8,128)}) custom-call(bf16[32,2,16,512]{3,2,1,0:T(8,128)(2,1)} %all-to-all-done.1.refs_0_, f32[512,512]{1,0:T(8,128)} %get-tuple-element.37.refs_1_, f32[512,512]{1,0:T(8,128)} %get-tuple-element.38.refs_3_.refs_2_, bf16[512,512]{1,0:T(8,128)(2,1)S(1)} %copy-done.4, ...), custom_call_target="tpu_custom_call" | custom-call | flops 4026531840 | bytes 10528768 | tf_op jit(solution)/shard_map/pallas_call | solution.py:569
  88.8 17.2 %all-to-all-done.2.refs_0_ = bf16[32,2,16,512]{3,2,1,0:T(8,128)(2,1)} async-done(((bf16[32,2,16,512]{3,2,1,0:T(8,128)(2,1)}), bf16[32,2,16,512]{3,2,1,0:T(8,128)(2,1)}, u32[]{:S(2)}, u32[]{:S(2)}) %all-to-all-start.2) | async-done | bytes 1048608 | tf_op jit(solution)/shard_map/all_to_all | solution.py:953
  106.0 4.3 %shard_map.116 = bf16[32,2,16,512]{3,2,1,0:T(8,128)(2,1)} custom-call(bf16[32,2,16,512]{3,2,1,0:T(8,128)(2,1)} %all-to-all-done.2.refs_0_, f32[512,512]{1,0:T(8,128)} %get-tuple-element.39.refs_1_, bf16[512,512]{1,0:T(8,128)(2,1)S(1)} %copy-done.1, f32[512,512]{1,0:T(8,128)} %get-tuple-element.40.refs_3_.refs_2_, bf16[512,512]{1,0:T(8,128)(2,1)S(1)} %copy-done), custom_call_target="tpu_custom_call" | custom-call | flops 1342177280 | bytes 5242880 | tf_op jit(solution)/shard_map/pallas_call | solution.py:569
  110.3 4.0 %all-to-all-start.3 = ((bf16[32,2,16,512]{3,2,1,0:T(8,128)(2,1)}), bf16[32,2,16,512]{3,2,1,0:T(8,128)(2,1)}, u32[]{:S(2)}, u32[]{:S(2)}) async-start(bf16[32,2,16,512]{3,2,1,0:T(8,128)(2,1)} %shard_map.116), calls=%async_computation.3 | async-start | bytes 2097152 | tf_op jit(solution)/shard_map/all_to_all | solution.py:953
  114.3 0.0 copy-start.2
  114.3 0.0 copy-start.6
  114.4 9.1 %shard_map.117 = (f32[512,512]{1,0:T(8,128)}, f32[512,512]{1,0:T(8,128)}, f32[512,512]{1,0:T(8,128)}) custom-call(bf16[32,2,16,512]{3,2,1,0:T(8,128)(2,1)} %all-to-all-done.2.refs_0_, f32[512,512]{1,0:T(8,128)} %get-tuple-element.39.refs_1_, f32[512,512]{1,0:T(8,128)} %get-tuple-element.40.refs_3_.refs_2_, bf16[512,512]{1,0:T(8,128)(2,1)S(1)} %copy-done.4, ...), custom_call_target="tpu_custom_call" | custom-call | flops 4026531840 | bytes 11577344 | tf_op jit(solution)/shard_map/pallas_call | solution.py:569
  123.5 16.8 %all-to-all-done.3.refs_0_ = bf16[32,2,16,512]{3,2,1,0:T(8,128)(2,1)} async-done(((bf16[32,2,16,512]{3,2,1,0:T(8,128)(2,1)}), bf16[32,2,16,512]{3,2,1,0:T(8,128)(2,1)}, u32[]{:S(2)}, u32[]{:S(2)}) %all-to-all-start.3) | async-done | bytes 1048608 | tf_op jit(solution)/shard_map/all_to_all | solution.py:953
  140.3 0.0 copy-done.2
  140.3 0.0 copy-done.6
  140.3 7.8 %shard_map.118 = bf16[32,2,16,512]{3,2,1,0:T(8,128)(2,1)} custom-call(bf16[32,2,16,512]{3,2,1,0:T(8,128)(2,1)} %all-to-all-done.3.refs_0_, f32[512,512]{1,0:T(8,128)} %get-tuple-element.42.refs_1_, bf16[128,128]{1,0:T(8,128)(2,1)S(1)} %select_convert_fusion.refs_2_.refs_5_, bf16[512,512]{1,0:T(8,128)(2,1)S(1)} %copy-done.6, bf16[512,512]{1,0:T(8,128)(2,1)S(1)} %copy-done.2, ...), custom_call_target="tpu_custom_call" | custom-call | flops 3221225472 | bytes 8431616 | tf_op jit(solution)/shard_map/pallas_call | solution.py:569
  148.1 29.9 %all_to_all.25.refs_0_ = bf16[32,2,16,512]{3,2,1,0:T(8,128)(2,1)S(1)} all-to-all(bf16[32,2,16,512]{3,2,1,0:T(8,128)(2,1)} %shard_map.118), channel_id=1, replica_groups=mesh['aux'=8,'row'=4] {'aux','row'}, dimensions={0} | all-to-all | bytes 2097152 | tf_op jit(solution)/shard_map/all_to_all | solution.py:953
  177.9 2.8 %shard_map.119 = f32[1,4,128,512]{3,2,1,0:T(8,128)} custom-call(bf16[32,2,16,512]{3,2,1,0:T(8,128)(2,1)S(1)} %all_to_all.25.refs_0_, f32[1,4,128,512]{3,2,1,0:T(8,128)} %bitcast.8), custom_call_target="tpu_custom_call" | custom-call | flops 536870912 | bytes 3145728 | tf_op jit(solution)/shard_map/pallas_call | solution.py:569
  (17 shorter events, 0.1 us)
Async XLA Ops:
  3.0 33.6 %all-to-all-start = ((bf16[32,2,16,512]{3,2,1,0:T(8,128)(2,1)}), bf16[32,2,16,512]{3,2,1,0:T(8,128)(2,1)S(1)}, u32[]{:S(2)}, u32[]{:S(2)}) async-start(bf16[32,2,16,512]{3,2,1,0:T(8,128)(2,1)} %shard_map.109), calls=%async_computation | async-start | bytes 2097152 | tf_op jit(solution)/shard_map/all_to_all | solution.py:953
  36.6 1.0 copy-start.8
  41.7 4.0 %copy-start.10 = (s32[16,8]{0,1:T(8,128)S(1)}, s32[16,8]{0,1:T(8,128)}, u32[]{:S(2)}) copy-start(s32[16,8]{0,1:T(8,128)} %param.17) | copy-start | bytes 1540
  41.7 11.1 %copy-start.7 = (bf16[512,512]{1,0:T(8,128)(2,1)S(1)}, bf16[512,512]{1,0:T(8,128)(2,1)}, u32[]{:S(2)}) copy-start(bf16[512,512]{1,0:T(8,128)(2,1)} %get-tuple-element.31.refs_5_.refs_8_.refs_9_) | copy-start | bytes 1572868
  41.7 30.0 %all-to-all-start.1 = ((bf16[32,2,16,512]{3,2,1,0:T(8,128)(2,1)}), bf16[32,2,16,512]{3,2,1,0:T(8,128)(2,1)}, u32[]{:S(2)}, u32[]{:S(2)}) async-start(bf16[32,2,16,512]{3,2,1,0:T(8,128)(2,1)} %get-tuple-element.27), calls=%async_computation.1 | async-start | bytes 2097152 | tf_op jit(solution)/shard_map/all_to_all | solution.py:953
  45.6 0.7 copy-start.11
  46.3 0.7 copy-start.9
  47.4 5.4 %copy-start.4 = (bf16[512,512]{1,0:T(8,128)(2,1)S(1)}, bf16[512,512]{1,0:T(8,128)(2,1)}, u32[]{:S(2)}) copy-start(bf16[512,512]{1,0:T(8,128)(2,1)} %get-tuple-element.28.refs_0_.refs_3_) | copy-start | bytes 1572868
  47.4 5.4 %copy-start.5 = (bf16[512,512]{1,0:T(8,128)(2,1)S(1)}, bf16[512,512]{1,0:T(8,128)(2,1)}, u32[]{:S(2)}) copy-start(bf16[512,512]{1,0:T(8,128)(2,1)} %get-tuple-element.29.refs_1_.refs_4_) | copy-start | bytes 1572868
  52.8 0.7 copy-start.3
  53.5 18.2 %copy-start = (bf16[512,512]{1,0:T(8,128)(2,1)S(1)}, bf16[512,512]{1,0:T(8,128)(2,1)}, u32[]{:S(2)}) copy-start(bf16[512,512]{1,0:T(8,128)(2,1)} %get-tuple-element.26.refs_4_) | copy-start | bytes 1572868
  53.5 18.2 %copy-start.1 = (bf16[512,512]{1,0:T(8,128)(2,1)S(1)}, bf16[512,512]{1,0:T(8,128)(2,1)}, u32[]{:S(2)}) copy-start(bf16[512,512]{1,0:T(8,128)(2,1)} %get-tuple-element.25.refs_2_) | copy-start | bytes 1572868
  76.0 30.0 %all-to-all-start.2 = ((bf16[32,2,16,512]{3,2,1,0:T(8,128)(2,1)}), bf16[32,2,16,512]{3,2,1,0:T(8,128)(2,1)}, u32[]{:S(2)}, u32[]{:S(2)}) async-start(bf16[32,2,16,512]{3,2,1,0:T(8,128)(2,1)} %shard_map.114), calls=%async_computation.2 | async-start | bytes 2097152 | tf_op jit(solution)/shard_map/all_to_all | solution.py:953
  110.3 30.0 %all-to-all-start.3 = ((bf16[32,2,16,512]{3,2,1,0:T(8,128)(2,1)}), bf16[32,2,16,512]{3,2,1,0:T(8,128)(2,1)}, u32[]{:S(2)}, u32[]{:S(2)}) async-start(bf16[32,2,16,512]{3,2,1,0:T(8,128)(2,1)} %shard_map.116), calls=%async_computation.3 | async-start | bytes 2097152 | tf_op jit(solution)/shard_map/all_to_all | solution.py:953
  114.3 26.0 %copy-start.2 = (bf16[512,512]{1,0:T(8,128)(2,1)S(1)}, bf16[512,512]{1,0:T(8,128)(2,1)}, u32[]{:S(2)}) copy-start(bf16[512,512]{1,0:T(8,128)(2,1)} %fusion.17.refs_3_.refs_4_) | copy-start | bytes 1572868
  114.3 25.9 %copy-start.6 = (bf16[512,512]{1,0:T(8,128)(2,1)S(1)}, bf16[512,512]{1,0:T(8,128)(2,1)}, u32[]{:S(2)}) copy-start(bf16[512,512]{1,0:T(8,128)(2,1)} %get-tuple-element.34.refs_8_.refs_11_.refs_3_) | copy-start | bytes 1572868

commit v5 on v4

--- a/solution.py
+++ b/solution.py
@@ -635,14 +635,15 @@
     parts = s.band // s.devices
     row, lane = iotas(s.devices, s.tile)
     mine = (row == me) & (lane < s.za)
+    bands = []
     for q in range(s.rows):
         pieces = []
         for v in range(blocks):
             for g in range(s.groups):
                 pieces.append(columns_in[g * s.rows + q, :, v * s.band : (v + 1) * s.band])
-        t_ref[q * s.band : (q + 1) * s.band, :] = dot(
-            jnp.concatenate(pieces, axis=0), column_lanes[...], ((0,), (0,))
-        ).astype(BF16)
+        bands.append(jnp.concatenate(pieces, axis=0))
+    t_ref[...] = dot(jnp.concatenate(bands, axis=1), column_lanes[...], ((0,), (0,))).astype(BF16)
+    for q in range(s.rows):
         rows = slice(q * s.band, q * s.band + s.devices)
         first = q * parts * s.za
         kept = s_ref[: s.devices, first : first + s.tile].astype(F32)
@@ -697,6 +698,7 @@
 
 
 def even_slope_part(s, direct, mirror, y_ref, h, unit, damp, q_ref, wa, wb, turned, sign, put):
+    factors = [jnp.broadcast_to(q_ref[:, k : k + 1], (s.extent, s.tile)) for k in range(MODES)]
     for th in range(s.tiles):
         lanes = slice(th * s.tile, (th + 1) * s.tile)
         turned[:, lanes] = dot(direct[:, lanes], unit[...]).astype(BF16)
@@ -711,7 +713,7 @@
             total = total + sign * whole[:, lanes]
             fields = dot(source, wb[...])
             for k in range(MODES):
-                total = total + q_ref[rows, k : k + 1] * fields[:, k * s.tile : (k + 1) * s.tile]
+                total = total + factors[k][rows, :] * fields[:, k * s.tile : (k + 1) * s.tile]
             put(rows, lanes, total)
 
 
@@ -785,12 +787,13 @@
         rows = slice(b, b + ROWS)
         grown[rows, :] = (weight * dot(left[rows, :], turned[...])).astype(BF16)
     out = stage.results[1]
+    value = dot(column_lanes[...], grown[...], ((1,), (1,))).astype(BF16)
     for q in range(s.rows):
-        value = dot(column_lanes[...], grown[q * s.band : (q + 1) * s.band, :], ((1,), (1,))).astype(BF16)
         for v in range(s.extent // s.band):
             for g in range(s.groups):
                 at = (v * s.groups + g) * s.local
-                out[g * s.rows + q, :, v * s.band : (v + 1) * s.band] = value[at : at + s.local, :]
+                piece = value[at : at + s.local, q * s.band : (q + 1) * s.band]
+                out[g * s.rows + q, :, v * s.band : (v + 1) * s.band] = piece
     stage.send(1)
 
     def keep_rows(rows, lanes, value):
@@ -817,11 +820,11 @@
     (post,) = temporaries
     post[...] = post_matrix(s)
     everyone = slice(0, s.devices)
+    change = dot(post[...], flat_rows(stage.front(0), everyone), ((0,), (0,)))
+    change = change + dot(flat_rows(stage.front(1), everyone), post[...], ((0,), (0,)))
     for v in range(s.extent // s.band):
-        lanes = slice(v * s.band, (v + 1) * s.band)
-        change = dot(post[:, lanes], flat_rows(stage.front(0), everyone), ((0,), (0,)))
-        change = change + dot(flat_rows(stage.front(1), everyone, lanes), post[...], ((0,), (0,)))
-        stage.results[v][...] = (stage.need(v)[...].reshape(s.band, s.extent) + change).reshape(
+        rows = slice(v * s.band, (v + 1) * s.band)
+        stage.results[v][...] = (stage.need(v)[...].reshape(s.band, s.extent) + change[rows, :]).reshape(
             stage.results[v].shape
         )
         stage.send(v)

time: 182 us -> 181 us (level)
  no operation moved by 1% of the time
where the time goes in v5:
time: 181 us; the launch traced here: 180 us
  waiting for transfers between devices  62.8 us (35%)
  Pallas kernels  59.6 us (33%)
  blocking collectives  29.9 us (17%)
  starting transfers between devices  19.2 us (11%)
  other arithmetic  4.79 us (3%)
  local copies, waits for them, and re-layouts  3.16 us (2%)
    all_to_all x4, waiting for transfers between devices, exchange(): lax.all_to_all(message, BOTH, split_axis=0, concat_axis=0, tiled=True)  62.8 us
    pallas_call x11, Pallas kernels, run_staged(): pl.pallas_call(kernel, out_shape=shapes, in_specs=[pl.BlockSpec(memory_sp...  59.6 us
    all_to_all x1, blocking collectives, exchange(): lax.all_to_all(message, BOTH, split_axis=0, concat_axis=0, tiled=True)  29.9 us
    all_to_all x4, starting transfers between devices, exchange(): lax.all_to_all(message, BOTH, split_axis=0, concat_axis=0, tiled=True)  19.2 us
  transfers between devices with their start and end apart: 4, of which 4 were waited for; matrix products, arithmetic and copies ran while one was open for 3% of the time, Pallas kernels for 19%

profile of v5, /device:TPU:0, one launch (start us, length us, event | category | flops | bytes accessed | tf_op | source)
XLA Modules:
  0.0 180.1 jit_solution(16938510469114111117)
XLA Ops:
  0.0 3.0 %shard_map.109 = bf16[32,2,16,512]{3,2,1,0:T(8,128)(2,1)} custom-call(f32[1,4,128,512]{3,2,1,0:T(8,128)} %bitcast.7, s32[2,4]{1,0:T(2,128)} %refs_1_.3), custom_call_target="tpu_custom_call" | custom-call | flops 536870912 | bytes 2097184 | tf_op jit(solution)/shard_map/pallas_call | solution.py:569
  3.0 7.3 %all-to-all-start = ((bf16[32,2,16,512]{3,2,1,0:T(8,128)(2,1)}), bf16[32,2,16,512]{3,2,1,0:T(8,128)(2,1)S(1)}, u32[]{:S(2)}, u32[]{:S(2)}) async-start(bf16[32,2,16,512]{3,2,1,0:T(8,128)(2,1)} %shard_map.109), calls=%async_computation | async-start | bytes 2097152 | tf_op jit(solution)/shard_map/all_to_all | solution.py:956
  10.4 3.8 %shard_map.110 = (bf16[512,512]{1,0:T(8,128)(2,1)}, bf16[512,512]{1,0:T(8,128)(2,1)}, bf16[512,512]{1,0:T(8,128)(2,1)}, bf16[512,512]{1,0:T(8,128)(2,1)}) custom-call(s32[8]{0:T(128)} %refs_0_.2, bf16[8,64,64]{2,1,0:T(8,128)(2,1)} %refs_1_.4, bf16[8,64,64]{2,1,0:T(8,128)(2,1)} %refs_2_.2), custom_call_target="tpu_custom_call" | custom-call | flops 1073741824 | bytes 2228224 | tf_op jit(solution)/shard_map/pallas_call | solution.py:569
  14.3 2.2 %fusion.17.refs_3_.refs_4_ = bf16[512,512]{1,0:T(8,128)(2,1)} fusion(s32[512]{0:T(512)S(1)} %get-tuple-element.60, s32[512]{0:T(512)S(1)} %get-tuple-element.67, s32[512]{0:T(512)S(1)} %get-tuple-element.61, s32[512]{0:T(512)S(1)} %get-tuple-element.68, s32[512]{0:T(512)S(1)} %get-tuple-element.59, s32[512]{0:T(512)S(1)} %get-tuple-element.62, ...), kind=kLoop, calls=%fused_computation.39 | loop fusion | flops 8912896 | bytes 542720 | tf_op jit(solution)/shard_map/convert_element_type | solution.py:995
  16.5 2.3 %fusion.18.refs_1_.refs_12_ = bf16[512,512]{1,0:T(8,128)(2,1)} fusion(s32[512]{0:T(512)S(1)} %get-tuple-element.45, s32[512]{0:T(512)S(1)} %get-tuple-element.55, s32[512]{0:T(512)S(1)} %get-tuple-element.46, s32[512]{0:T(512)S(1)} %get-tuple-element.56, s32[512]{0:T(512)S(1)} %get-tuple-element.47, s32[512]{0:T(512)S(1)} %get-tuple-element.57, ...), kind=kLoop, calls=%fused_computation.40 | loop fusion | flops 12582912 | bytes 547328 | tf_op jit(solution)/shard_map/convert_element_type | solution.py:988
  18.8 17.8 %all-to-all-done.refs_0_.refs_3_ = bf16[32,2,16,512]{3,2,1,0:T(8,128)(2,1)S(1)} async-done(((bf16[32,2,16,512]{3,2,1,0:T(8,128)(2,1)}), bf16[32,2,16,512]{3,2,1,0:T(8,128)(2,1)S(1)}, u32[]{:S(2)}, u32[]{:S(2)}) %all-to-all-start) | async-done | bytes 1048608 | tf_op jit(solution)/shard_map/all_to_all | solution.py:956
  36.6 0.0 copy-start.8
  36.6 1.0 copy-done.8
  37.6 4.1 %shard_map.111 = (bf16[32,2,16,512]{3,2,1,0:T(8,128)(2,1)}, bf16[512,512]{1,0:T(8,128)(2,1)}, bf16[512,512]{1,0:T(8,128)(2,1)}) custom-call(bf16[32,2,16,512]{3,2,1,0:T(8,128)(2,1)} %copy-done.8, bf16[512,512]{1,0:T(8,128)(2,1)} %fusion.18.refs_1_.refs_12_, bf16[512,512]{1,0:T(8,128)(2,1)} %get-tuple-element.25.refs_2_, ...), custom_call_target="tpu_custom_call" | custom-call | flops 1073741824 | bytes 5242880 | tf_op jit(solution)/shard_map/pallas_call | solution.py:569
  41.7 0.0 copy-start.10
  41.7 0.0 copy-start.7
  41.7 3.9 %all-to-all-start.1 = ((bf16[32,2,16,512]{3,2,1,0:T(8,128)(2,1)}), bf16[32,2,16,512]{3,2,1,0:T(8,128)(2,1)}, u32[]{:S(2)}, u32[]{:S(2)}) async-start(bf16[32,2,16,512]{3,2,1,0:T(8,128)(2,1)} %get-tuple-element.27), calls=%async_computation.1 | async-start | bytes 2097152 | tf_op jit(solution)/shard_map/all_to_all | solution.py:956
  45.6 0.0 copy-done.10
  45.6 0.0 copy-start.11
  45.7 0.7 copy.12.refs_4_
  46.3 0.0 copy-done.11
  46.3 0.0 copy-start.9
  46.3 0.7 copy.13.refs_5_
  47.0 0.0 copy-done.9
  47.0 0.1 copy.14
  47.2 0.2 select_convert_fusion.refs_2_.refs_5_
  47.4 0.0 copy-start.4
  47.4 0.0 copy-start.5
  47.4 5.4 %shard_map.112 = (bf16[4,512,128]{2,1,0:T(8,128)(2,1)}, bf16[512,512]{1,0:T(8,128)(2,1)}, bf16[4,512,128]{2,1,0:T(8,128)(2,1)}, bf16[512,512]{1,0:T(8,128)(2,1)}, f32[1,512]{1,0:T(1,128)}) custom-call(f32[4]{0:T(128)} %refs_0_.3, f32[4]{0:T(128)} %refs_1_.5, f32[4]{0:T(128)} %refs_2_.3, bf16[32,2,16,512]{3,2,1,0:T(8,128)(2,1)} %copy-done.8, ...), custom_call_target="tpu_custom_call" | custom-call | flops 268435456 | bytes 3156992 | tf_op jit(solution)/shard_map/pallas_call | solution.py:569
  52.8 0.0 copy-start.3
  52.8 0.0 copy-done.7
  52.8 0.0 copy-done.4
  52.8 0.0 copy-done.5
  52.9 0.6 copy-done.3
  53.5 0.0 copy-start
  53.5 0.0 copy-start.1
  53.5 7.2 %shard_map.113 = (f32[512,512]{1,0:T(8,128)}, f32[512,512]{1,0:T(8,128)}) custom-call(bf16[512,512]{1,0:T(8,128)(2,1)S(1)} %copy-done.4, bf16[512,512]{1,0:T(8,128)(2,1)S(1)} %copy-done.5, bf16[128,128]{1,0:T(8,128)(2,1)S(1)} %select_convert_fusion.refs_2_.refs_5_, f32[1,512]{1,0:T(1,128)S(1)} %copy-done.3, f32[512,4]{1,0:T(8,128)S(1)} %bitcast.3, ...), custom_call_target="tpu_custom_call" | custom-call | flops 3221225472 | bytes 6334464 | tf_op jit(solution)/shard_map/pallas_call | solution.py:569
  60.7 10.9 %all-to-all-done.1.refs_0_ = bf16[32,2,16,512]{3,2,1,0:T(8,128)(2,1)} async-done(((bf16[32,2,16,512]{3,2,1,0:T(8,128)(2,1)}), bf16[32,2,16,512]{3,2,1,0:T(8,128)(2,1)}, u32[]{:S(2)}, u32[]{:S(2)}) %all-to-all-start.1) | async-done | bytes 1048608 | tf_op jit(solution)/shard_map/all_to_all | solution.py:956
  71.7 0.0 copy-done
  71.7 0.0 copy-done.1
  71.7 4.3 %shard_map.114 = bf16[32,2,16,512]{3,2,1,0:T(8,128)(2,1)} custom-call(bf16[32,2,16,512]{3,2,1,0:T(8,128)(2,1)} %all-to-all-done.1.refs_0_, f32[512,512]{1,0:T(8,128)} %get-tuple-element.37.refs_1_, bf16[512,512]{1,0:T(8,128)(2,1)S(1)} %copy-done.1, f32[512,512]{1,0:T(8,128)} %get-tuple-element.38.refs_3_.refs_2_, bf16[512,512]{1,0:T(8,128)(2,1)S(1)} %copy-done), custom_call_target="tpu_custom_call" | custom-call | flops 1342177280 | bytes 5242880 | tf_op jit(solution)/shard_map/pallas_call | solution.py:569
  76.0 4.0 %all-to-all-start.2 = ((bf16[32,2,16,512]{3,2,1,0:T(8,128)(2,1)}), bf16[32,2,16,512]{3,2,1,0:T(8,128)(2,1)}, u32[]{:S(2)}, u32[]{:S(2)}) async-start(bf16[32,2,16,512]{3,2,1,0:T(8,128)(2,1)} %shard_map.114), calls=%async_computation.2 | async-start | bytes 2097152 | tf_op jit(solution)/shard_map/all_to_all | solution.py:956
  80.0 8.7 %shard_map.115 = (f32[512,512]{1,0:T(8,128)}, f32[512,512]{1,0:T(8,128)}, f32[512,512]{1,0:T(8,128)}) custom-call(bf16[32,2,16,512]{3,2,1,0:T(8,128)(2,1)} %all-to-all-done.1.refs_0_, f32[512,512]{1,0:T(8,128)} %get-tuple-element.37.refs_1_, f32[512,512]{1,0:T(8,128)} %get-tuple-element.38.refs_3_.refs_2_, bf16[512,512]{1,0:T(8,128)(2,1)S(1)} %copy-done.4, ...), custom_call_target="tpu_custom_call" | custom-call | flops 4026531840 | bytes 10528768 | tf_op jit(solution)/shard_map/pallas_call | solution.py:569
  88.7 17.3 %all-to-all-done.2.refs_0_ = bf16[32,2,16,512]{3,2,1,0:T(8,128)(2,1)} async-done(((bf16[32,2,16,512]{3,2,1,0:T(8,128)(2,1)}), bf16[32,2,16,512]{3,2,1,0:T(8,128)(2,1)}, u32[]{:S(2)}, u32[]{:S(2)}) %all-to-all-start.2) | async-done | bytes 1048608 | tf_op jit(solution)/shard_map/all_to_all | solution.py:956
  106.0 4.3 %shard_map.116 = bf16[32,2,16,512]{3,2,1,0:T(8,128)(2,1)} custom-call(bf16[32,2,16,512]{3,2,1,0:T(8,128)(2,1)} %all-to-all-done.2.refs_0_, f32[512,512]{1,0:T(8,128)} %get-tuple-element.39.refs_1_, bf16[512,512]{1,0:T(8,128)(2,1)S(1)} %copy-done.1, f32[512,512]{1,0:T(8,128)} %get-tuple-element.40.refs_3_.refs_2_, bf16[512,512]{1,0:T(8,128)(2,1)S(1)} %copy-done), custom_call_target="tpu_custom_call" | custom-call | flops 1342177280 | bytes 5242880 | tf_op jit(solution)/shard_map/pallas_call | solution.py:569
  110.3 4.0 %all-to-all-start.3 = ((bf16[32,2,16,512]{3,2,1,0:T(8,128)(2,1)}), bf16[32,2,16,512]{3,2,1,0:T(8,128)(2,1)}, u32[]{:S(2)}, u32[]{:S(2)}) async-start(bf16[32,2,16,512]{3,2,1,0:T(8,128)(2,1)} %shard_map.116), calls=%async_computation.3 | async-start | bytes 2097152 | tf_op jit(solution)/shard_map/all_to_all | solution.py:956
  114.3 0.0 copy-start.2
  114.3 0.0 copy-start.6
  114.4 9.1 %shard_map.117 = (f32[512,512]{1,0:T(8,128)}, f32[512,512]{1,0:T(8,128)}, f32[512,512]{1,0:T(8,128)}) custom-call(bf16[32,2,16,512]{3,2,1,0:T(8,128)(2,1)} %all-to-all-done.2.refs_0_, f32[512,512]{1,0:T(8,128)} %get-tuple-element.39.refs_1_, f32[512,512]{1,0:T(8,128)} %get-tuple-element.40.refs_3_.refs_2_, bf16[512,512]{1,0:T(8,128)(2,1)S(1)} %copy-done.4, ...), custom_call_target="tpu_custom_call" | custom-call | flops 4026531840 | bytes 11577344 | tf_op jit(solution)/shard_map/pallas_call | solution.py:569
  123.4 16.8 %all-to-all-done.3.refs_0_ = bf16[32,2,16,512]{3,2,1,0:T(8,128)(2,1)} async-done(((bf16[32,2,16,512]{3,2,1,0:T(8,128)(2,1)}), bf16[32,2,16,512]{3,2,1,0:T(8,128)(2,1)}, u32[]{:S(2)}, u32[]{:S(2)}) %all-to-all-start.3) | async-done | bytes 1048608 | tf_op jit(solution)/shard_map/all_to_all | solution.py:956
  140.3 0.0 copy-done.2
  140.3 0.0 copy-done.6
  140.3 7.5 %shard_map.118 = bf16[32,2,16,512]{3,2,1,0:T(8,128)(2,1)} custom-call(bf16[32,2,16,512]{3,2,1,0:T(8,128)(2,1)} %all-to-all-done.3.refs_0_, f32[512,512]{1,0:T(8,128)} %get-tuple-element.42.refs_1_, bf16[128,128]{1,0:T(8,128)(2,1)S(1)} %select_convert_fusion.refs_2_.refs_5_, bf16[512,512]{1,0:T(8,128)(2,1)S(1)} %copy-done.6, bf16[512,512]{1,0:T(8,128)(2,1)S(1)} %copy-done.2, ...), custom_call_target="tpu_custom_call" | custom-call | flops 3221225472 | bytes 8431616 | tf_op jit(solution)/shard_map/pallas_call | solution.py:569
  147.8 29.9 %all_to_all.25.refs_0_ = bf16[32,2,16,512]{3,2,1,0:T(8,128)(2,1)S(1)} all-to-all(bf16[32,2,16,512]{3,2,1,0:T(8,128)(2,1)} %shard_map.118), channel_id=1, replica_groups=mesh['aux'=8,'row'=4] {'aux','row'}, dimensions={0} | all-to-all | bytes 2097152 | tf_op jit(solution)/shard_map/all_to_all | solution.py:956
  177.7 2.2 %shard_map.119 = f32[1,4,128,512]{3,2,1,0:T(8,128)} custom-call(bf16[32,2,16,512]{3,2,1,0:T(8,128)(2,1)S(1)} %all_to_all.25.refs_0_, f32[1,4,128,512]{3,2,1,0:T(8,128)} %bitcast.8), custom_call_target="tpu_custom_call" | custom-call | flops 536870912 | bytes 3145728 | tf_op jit(solution)/shard_map/pallas_call | solution.py:569
  (17 shorter events, 0.1 us)
Async XLA Ops:
  3.0 33.6 %all-to-all-start = ((bf16[32,2,16,512]{3,2,1,0:T(8,128)(2,1)}), bf16[32,2,16,512]{3,2,1,0:T(8,128)(2,1)S(1)}, u32[]{:S(2)}, u32[]{:S(2)}) async-start(bf16[32,2,16,512]{3,2,1,0:T(8,128)(2,1)} %shard_map.109), calls=%async_computation | async-start | bytes 2097152 | tf_op jit(solution)/shard_map/all_to_all | solution.py:956
  36.6 1.0 copy-start.8
  41.7 4.0 %copy-start.10 = (s32[16,8]{0,1:T(8,128)S(1)}, s32[16,8]{0,1:T(8,128)}, u32[]{:S(2)}) copy-start(s32[16,8]{0,1:T(8,128)} %param.17) | copy-start | bytes 1540
  41.7 11.1 %copy-start.7 = (bf16[512,512]{1,0:T(8,128)(2,1)S(1)}, bf16[512,512]{1,0:T(8,128)(2,1)}, u32[]{:S(2)}) copy-start(bf16[512,512]{1,0:T(8,128)(2,1)} %get-tuple-element.31.refs_5_.refs_8_.refs_9_) | copy-start | bytes 1572868
  41.7 30.0 %all-to-all-start.1 = ((bf16[32,2,16,512]{3,2,1,0:T(8,128)(2,1)}), bf16[32,2,16,512]{3,2,1,0:T(8,128)(2,1)}, u32[]{:S(2)}, u32[]{:S(2)}) async-start(bf16[32,2,16,512]{3,2,1,0:T(8,128)(2,1)} %get-tuple-element.27), calls=%async_computation.1 | async-start | bytes 2097152 | tf_op jit(solution)/shard_map/all_to_all | solution.py:956
  45.6 0.7 copy-start.11
  46.3 0.7 copy-start.9
  47.4 5.4 %copy-start.4 = (bf16[512,512]{1,0:T(8,128)(2,1)S(1)}, bf16[512,512]{1,0:T(8,128)(2,1)}, u32[]{:S(2)}) copy-start(bf16[512,512]{1,0:T(8,128)(2,1)} %get-tuple-element.28.refs_0_.refs_3_) | copy-start | bytes 1572868
  47.4 5.4 %copy-start.5 = (bf16[512,512]{1,0:T(8,128)(2,1)S(1)}, bf16[512,512]{1,0:T(8,128)(2,1)}, u32[]{:S(2)}) copy-start(bf16[512,512]{1,0:T(8,128)(2,1)} %get-tuple-element.29.refs_1_.refs_4_) | copy-start | bytes 1572868
  52.8 0.7 copy-start.3
  53.5 18.2 %copy-start = (bf16[512,512]{1,0:T(8,128)(2,1)S(1)}, bf16[512,512]{1,0:T(8,128)(2,1)}, u32[]{:S(2)}) copy-start(bf16[512,512]{1,0:T(8,128)(2,1)} %get-tuple-element.26.refs_4_) | copy-start | bytes 1572868
  53.5 18.2 %copy-start.1 = (bf16[512,512]{1,0:T(8,128)(2,1)S(1)}, bf16[512,512]{1,0:T(8,128)(2,1)}, u32[]{:S(2)}) copy-start(bf16[512,512]{1,0:T(8,128)(2,1)} %get-tuple-element.25.refs_2_) | copy-start | bytes 1572868
  76.0 30.0 %all-to-all-start.2 = ((bf16[32,2,16,512]{3,2,1,0:T(8,128)(2,1)}), bf16[32,2,16,512]{3,2,1,0:T(8,128)(2,1)}, u32[]{:S(2)}, u32[]{:S(2)}) async-start(bf16[32,2,16,512]{3,2,1,0:T(8,128)(2,1)} %shard_map.114), calls=%async_computation.2 | async-start | bytes 2097152 | tf_op jit(solution)/shard_map/all_to_all | solution.py:956
  110.3 30.0 %all-to-all-start.3 = ((bf16[32,2,16,512]{3,2,1,0:T(8,128)(2,1)}), bf16[32,2,16,512]{3,2,1,0:T(8,128)(2,1)}, u32[]{:S(2)}, u32[]{:S(2)}) async-start(bf16[32,2,16,512]{3,2,1,0:T(8,128)(2,1)} %shard_map.116), calls=%async_computation.3 | async-start | bytes 2097152 | tf_op jit(solution)/shard_map/all_to_all | solution.py:956
  114.3 26.0 %copy-start.2 = (bf16[512,512]{1,0:T(8,128)(2,1)S(1)}, bf16[512,512]{1,0:T(8,128)(2,1)}, u32[]{:S(2)}) copy-start(bf16[512,512]{1,0:T(8,128)(2,1)} %fusion.17.refs_3_.refs_4_) | copy-start | bytes 1572868
  114.3 25.9 %copy-start.6 = (bf16[512,512]{1,0:T(8,128)(2,1)S(1)}, bf16[512,512]{1,0:T(8,128)(2,1)}, u32[]{:S(2)}) copy-start(bf16[512,512]{1,0:T(8,128)(2,1)} %get-tuple-element.34.refs_8_.refs_11_.refs_3_) | copy-start | bytes 1572868

commit v6 on v5

--- a/solution.py
+++ b/solution.py
@@ -14,6 +14,7 @@
 BOTH = ("aux", "row")
 GRANT = 52 << 20
 MOST = 60 << 20
+TAKE = 44 << 20
 ROWS = 512
 
 F32 = jnp.float32
@@ -619,18 +620,13 @@
     stage.send(index)
 
 
-def even_take(s, stage, small, temporaries):
-    s_ref, t_ref = stage.results[2], stage.results[3]
+def take_rows(s, rows_in, row_lanes, s_ref):
+    rows = flat_rows(rows_in, slice(0, s.devices))
+    s_ref[...] = dot(rows, row_lanes[...], ((0,), (0,))).astype(BF16)
+
+
+def take_columns(s, columns_in, column_lanes, s_ref, t_ref):
     me = lax.axis_index("aux") * s.rows + lax.axis_index("row")
-    everyone = slice(0, s.devices)
-    rows_in, row_lanes = stage.front(0), stage.need(0)
-    for b in row_blocks(s.extent, ROWS):
-        s_ref[b : b + ROWS, :] = dot(
-            flat_rows(rows_in, everyone, slice(b, b + ROWS)), row_lanes[...], ((0,), (0,))
-        ).astype(BF16)
-    stage.send(2)
-    send_products(s, stage, stage.need(1), s_ref, 1)
-    columns_in, column_lanes = stage.front(1), stage.need(2)
     blocks = s.extent // s.band
     parts = s.band // s.devices
     row, lane = iotas(s.devices, s.tile)
@@ -648,7 +644,13 @@
         first = q * parts * s.za
         kept = s_ref[: s.devices, first : first + s.tile].astype(F32)
         t_ref[rows, : s.tile] = jnp.where(mine, kept, t_ref[rows, : s.tile].astype(F32)).astype(BF16)
-    stage.send(3)
+
+
+def even_take(s, stage, small, temporaries):
+    s_ref, t_ref = temporaries
+    take_rows(s, stage.front(0), stage.need(0), s_ref)
+    send_products(s, stage, stage.need(1), s_ref, 1)
+    take_columns(s, stage.front(1), stage.need(2), s_ref, t_ref)
     send_products(s, stage, stage.need(3), t_ref, 0)
 
 
@@ -727,8 +729,12 @@
 def even_first_slope(s, step, stage, small, temporaries):
     (turned,) = temporaries
     need = stage.need
-    first, second = stage.results
-    s_ref, t_ref, unit, damp, q_ref = need(0), need(1), need(2), need(3), need(4)
+    first, second, s_ref, t_ref = stage.results
+    take_rows(s, stage.front(0), need(0), s_ref)
+    stage.send(2)
+    take_columns(s, stage.front(1), need(1), s_ref, t_ref)
+    stage.send(3)
+    unit, damp, q_ref = need(2), need(3), need(4)
     put = put_base(first, s_ref, step)
     even_slope_part(s, s_ref, t_ref, s_ref, need(5), unit, damp, q_ref, need(6), need(7), turned, -1.0, put)
     stage.send(0)
@@ -1000,14 +1006,15 @@
     wide, size = s.fold * s.tile, max(256, 16 * s.local)
     swap, order = pltpu.VMEM((wide, wide), BF16), pltpu.VMEM((size, size), BF16)
 
-    message, s_now, t_now = run_staged(
+    message = run_staged(
         functools.partial(even_take, s),
-        [pair, state, state],
+        [pair],
         [row_lanes, right_rows, column_lanes, left_rows],
+        temporaries=[held_b, held_b],
         front=[(got, 0), (got, 1)],
-        grant=MOST,
+        grant=TAKE,
         flops=4 * cube,
-    )
+    )[0]
     wa = shape(s.tiles, 4 * s.tile, s.tile, dtype=BF16)
     wb = shape(4 * s.tile, MODES * s.tile, dtype=BF16)
     wa_s, wb_s, wa_t, wb_t, damp = run_staged(
@@ -1022,12 +1029,13 @@
     shares = [STEP / 6.0, STEP / 3.0, STEP / 3.0, STEP / 6.0]
     steps = [0.25, 0.25, 0.5]
     ratios = [share / step for share, step in zip(shares, steps)]
-    got = exchange(message)
-    base_s, base_t = run_staged(
+    begun, got = got, exchange(message)
+    base_s, base_t, s_now, t_now = run_staged(
         functools.partial(even_first_slope, s, steps[0]),
-        [full, full],
-        [s_now, t_now] + tables,
+        [full, full, state, state],
+        [row_lanes, column_lanes] + tables,
         temporaries=[held_b],
+        front=[(begun, 0), (begun, 1)],
         flops=12 * cube,
     )
     total = None

time: 181 us -> 179 us (0.989)
  other arithmetic: 4.79 us -> 2.93 us
  transfers between devices with their start and end apart: 4 -> 4, of which waited for: 4 -> 4; matrix products, arithmetic and copies ran while one was open for 3% -> 2% of each run, Pallas kernels for 19% -> 19%
where the time goes in v6:
time: 179 us; the launch traced here: 178 us
  waiting for transfers between devices  63.3 us (35%)
  Pallas kernels  58.9 us (33%)
  blocking collectives  29.9 us (17%)
  starting transfers between devices  19.2 us (11%)
  local copies, waits for them, and re-layouts  3.03 us (2%)
  other arithmetic  2.93 us (2%)
    all_to_all x4, waiting for transfers between devices, exchange(): lax.all_to_all(message, BOTH, split_axis=0, concat_axis=0, tiled=True)  63.3 us
    pallas_call x11, Pallas kernels, run_staged(): pl.pallas_call(kernel, out_shape=shapes, in_specs=[pl.BlockSpec(memory_sp...  58.9 us
    all_to_all x1, blocking collectives, exchange(): lax.all_to_all(message, BOTH, split_axis=0, concat_axis=0, tiled=True)  29.9 us
    all_to_all x4, starting transfers between devices, exchange(): lax.all_to_all(message, BOTH, split_axis=0, concat_axis=0, tiled=True)  19.2 us
  transfers between devices with their start and end apart: 4, of which 4 were waited for; matrix products, arithmetic and copies ran while one was open for 2% of the time, Pallas kernels for 19%

profile of v6, /device:TPU:0, one launch (start us, length us, event | category | flops | bytes accessed | tf_op | source)
XLA Modules:
  0.0 177.9 jit_solution(11497721351099103033)
XLA Ops:
  0.0 3.0 %shard_map.109 = bf16[32,2,16,512]{3,2,1,0:T(8,128)(2,1)} custom-call(f32[1,4,128,512]{3,2,1,0:T(8,128)} %bitcast.7, s32[2,4]{1,0:T(2,128)} %refs_1_.3), custom_call_target="tpu_custom_call" | custom-call | flops 536870912 | bytes 2097184 | tf_op jit(solution)/shard_map/pallas_call | solution.py:570
  3.0 7.3 %all-to-all-start = ((bf16[32,2,16,512]{3,2,1,0:T(8,128)(2,1)}), bf16[32,2,16,512]{3,2,1,0:T(8,128)(2,1)S(1)}, u32[]{:S(2)}, u32[]{:S(2)}) async-start(bf16[32,2,16,512]{3,2,1,0:T(8,128)(2,1)} %shard_map.109), calls=%async_computation | async-start | bytes 2097152 | tf_op jit(solution)/shard_map/all_to_all | solution.py:962
  10.4 3.8 %shard_map.110 = (bf16[512,512]{1,0:T(8,128)(2,1)}, bf16[512,512]{1,0:T(8,128)(2,1)}, bf16[512,512]{1,0:T(8,128)(2,1)}, bf16[512,512]{1,0:T(8,128)(2,1)}) custom-call(s32[8]{0:T(128)} %refs_0_.2, bf16[8,64,64]{2,1,0:T(8,128)(2,1)} %refs_1_.4, bf16[8,64,64]{2,1,0:T(8,128)(2,1)} %refs_2_.2), custom_call_target="tpu_custom_call" | custom-call | flops 1073741824 | bytes 2228224 | tf_op jit(solution)/shard_map/pallas_call | solution.py:570
  14.3 0.0 copy-start.1
  14.3 0.0 copy-start.2
  14.3 1.2 fusion.17.refs_3_.refs_2_.refs_4_
  15.6 0.0 copy-start.3
  15.6 1.4 fusion.18.refs_1_.refs_12_
  17.0 0.0 copy-start.5
  17.0 19.6 %all-to-all-done.refs_0_.refs_3_ = bf16[32,2,16,512]{3,2,1,0:T(8,128)(2,1)S(1)} async-done(((bf16[32,2,16,512]{3,2,1,0:T(8,128)(2,1)}), bf16[32,2,16,512]{3,2,1,0:T(8,128)(2,1)S(1)}, u32[]{:S(2)}, u32[]{:S(2)}) %all-to-all-start) | async-done | bytes 1048608 | tf_op jit(solution)/shard_map/all_to_all | solution.py:962
  36.6 0.0 copy-start
  36.6 0.0 copy-done.1
  36.6 0.0 copy-done.2
  36.6 2.9 %shard_map.111 = bf16[32,2,16,512]{3,2,1,0:T(8,128)(2,1)} custom-call(bf16[32,2,16,512]{3,2,1,0:T(8,128)(2,1)S(1)} %all-to-all-done.refs_0_.refs_3_, bf16[512,512]{1,0:T(8,128)(2,1)S(1)} %fusion.18.refs_1_.refs_12_, bf16[512,512]{1,0:T(8,128)(2,1)S(1)} %copy-done.2, bf16[512,512]{1,0:T(8,128)(2,1)S(1)} %fusion.17.refs_3_.refs_2_.refs_4_, ...), custom_call_target="tpu_custom_call" | custom-call | flops 1073741824 | bytes 4194304 | tf_op jit(solution)/shard_map/pallas_call | solution.py:570
  39.5 0.0 copy-done.3
  39.5 0.0 copy-done
  39.5 0.0 copy-start.14
  39.6 3.9 %all-to-all-start.1 = ((bf16[32,2,16,512]{3,2,1,0:T(8,128)(2,1)}), bf16[32,2,16,512]{3,2,1,0:T(8,128)(2,1)}, u32[]{:S(2)}, u32[]{:S(2)}) async-start(bf16[32,2,16,512]{3,2,1,0:T(8,128)(2,1)} %shard_map.111), calls=%async_computation.1 | async-start | bytes 2097152 | tf_op jit(solution)/shard_map/all_to_all | solution.py:962
  43.5 0.0 copy-done.14
  43.5 0.0 copy-start.15
  43.5 0.7 copy.12.refs_4_
  44.2 0.0 copy-done.15
  44.2 0.0 copy-start.13
  44.2 0.7 copy.13.refs_5_
  44.9 0.0 copy-done.13
  44.9 0.1 copy.14
  45.1 0.2 select_convert_fusion.refs_3_.refs_5_.refs_2_
  45.3 5.2 %shard_map.112 = (bf16[4,512,128]{2,1,0:T(8,128)(2,1)}, bf16[512,512]{1,0:T(8,128)(2,1)}, bf16[4,512,128]{2,1,0:T(8,128)(2,1)}, bf16[512,512]{1,0:T(8,128)(2,1)}, f32[1,512]{1,0:T(1,128)}) custom-call(f32[4]{0:T(128)} %refs_0_.3, f32[4]{0:T(128)} %refs_1_.5, f32[4]{0:T(128)} %refs_2_.3, bf16[32,2,16,512]{3,2,1,0:T(8,128)(2,1)} %copy-done, ...), custom_call_target="tpu_custom_call" | custom-call | flops 268435456 | bytes 3156992 | tf_op jit(solution)/shard_map/pallas_call | solution.py:570
  50.5 0.0 copy-start.6
  50.5 0.0 copy-done.5
  50.5 0.7 copy-done.6
  51.2 7.9 %shard_map.113 = (f32[512,512]{1,0:T(8,128)}, f32[512,512]{1,0:T(8,128)}, bf16[512,512]{1,0:T(8,128)(2,1)S(1)}, bf16[512,512]{1,0:T(8,128)(2,1)S(1)}) custom-call(bf16[32,2,16,512]{3,2,1,0:T(8,128)(2,1)} %copy-done, bf16[512,512]{1,0:T(8,128)(2,1)S(1)} %fusion.18.refs_1_.refs_12_, bf16[512,512]{1,0:T(8,128)(2,1)} %copy-done.3, ...), custom_call_target="tpu_custom_call" | custom-call | flops 3221225472 | bytes 8431616 | tf_op jit(solution)/shard_map/pallas_call | solution.py:570
  59.1 0.0 copy-start.11
  59.1 0.8 copy-done.11
  59.9 0.0 copy-start.9
  59.9 9.7 %all-to-all-done.1.refs_0_ = bf16[32,2,16,512]{3,2,1,0:T(8,128)(2,1)} async-done(((bf16[32,2,16,512]{3,2,1,0:T(8,128)(2,1)}), bf16[32,2,16,512]{3,2,1,0:T(8,128)(2,1)}, u32[]{:S(2)}, u32[]{:S(2)}) %all-to-all-start.1) | async-done | bytes 1048608 | tf_op jit(solution)/shard_map/all_to_all | solution.py:962
  69.5 4.3 %shard_map.114 = bf16[32,2,16,512]{3,2,1,0:T(8,128)(2,1)} custom-call(bf16[32,2,16,512]{3,2,1,0:T(8,128)(2,1)} %all-to-all-done.1.refs_0_, f32[512,512]{1,0:T(8,128)} %get-tuple-element.33.refs_1_, bf16[512,512]{1,0:T(8,128)(2,1)S(1)} %copy-done.2, f32[512,512]{1,0:T(8,128)} %get-tuple-element.34.refs_3_.refs_2_, bf16[512,512]{1,0:T(8,128)(2,1)S(1)} %copy-done.1), custom_call_target="tpu_custom_call" | custom-call | flops 1342177280 | bytes 5242880 | tf_op jit(solution)/shard_map/pallas_call | solution.py:570
  73.9 0.0 copy-start.8
  73.9 0.0 copy-start.12
  73.9 4.0 %all-to-all-start.2 = ((bf16[32,2,16,512]{3,2,1,0:T(8,128)(2,1)}), bf16[32,2,16,512]{3,2,1,0:T(8,128)(2,1)}, u32[]{:S(2)}, u32[]{:S(2)}) async-start(bf16[32,2,16,512]{3,2,1,0:T(8,128)(2,1)} %shard_map.114), calls=%async_computation.2 | async-start | bytes 2097152 | tf_op jit(solution)/shard_map/all_to_all | solution.py:962
  77.9 0.0 copy-done.9
  77.9 0.0 copy-done.8
  77.9 0.0 copy-done.12
  77.9 8.7 %shard_map.115 = (f32[512,512]{1,0:T(8,128)}, f32[512,512]{1,0:T(8,128)}, f32[512,512]{1,0:T(8,128)}) custom-call(bf16[32,2,16,512]{3,2,1,0:T(8,128)(2,1)} %all-to-all-done.1.refs_0_, f32[512,512]{1,0:T(8,128)} %get-tuple-element.33.refs_1_, f32[512,512]{1,0:T(8,128)} %get-tuple-element.34.refs_3_.refs_2_, bf16[512,512]{1,0:T(8,128)(2,1)S(1)} %get-tuple-element.35.refs_3_, ...), custom_call_target="tpu_custom_call" | custom-call | flops 4026531840 | bytes 10528768 | tf_op jit(solution)/shard_map/pallas_call | solution.py:570
  86.6 17.2 %all-to-all-done.2.refs_0_ = bf16[32,2,16,512]{3,2,1,0:T(8,128)(2,1)} async-done(((bf16[32,2,16,512]{3,2,1,0:T(8,128)(2,1)}), bf16[32,2,16,512]{3,2,1,0:T(8,128)(2,1)}, u32[]{:S(2)}, u32[]{:S(2)}) %all-to-all-start.2) | async-done | bytes 1048608 | tf_op jit(solution)/shard_map/all_to_all | solution.py:962
  103.9 4.3 %shard_map.116 = bf16[32,2,16,512]{3,2,1,0:T(8,128)(2,1)} custom-call(bf16[32,2,16,512]{3,2,1,0:T(8,128)(2,1)} %all-to-all-done.2.refs_0_, f32[512,512]{1,0:T(8,128)} %get-tuple-element.37.refs_1_, bf16[512,512]{1,0:T(8,128)(2,1)S(1)} %copy-done.2, f32[512,512]{1,0:T(8,128)} %get-tuple-element.38.refs_3_.refs_2_, bf16[512,512]{1,0:T(8,128)(2,1)S(1)} %copy-done.1), custom_call_target="tpu_custom_call" | custom-call | flops 1342177280 | bytes 5242880 | tf_op jit(solution)/shard_map/pallas_call | solution.py:570
  108.2 0.0 copy-start.10
  108.2 4.0 %all-to-all-start.3 = ((bf16[32,2,16,512]{3,2,1,0:T(8,128)(2,1)}), bf16[32,2,16,512]{3,2,1,0:T(8,128)(2,1)}, u32[]{:S(2)}, u32[]{:S(2)}) async-start(bf16[32,2,16,512]{3,2,1,0:T(8,128)(2,1)} %shard_map.116), calls=%async_computation.3 | async-start | bytes 2097152 | tf_op jit(solution)/shard_map/all_to_all | solution.py:962
  112.2 0.0 copy-done.10
  112.2 0.0 copy-start.4
  112.2 0.0 copy-start.7
  112.2 9.1 %shard_map.117 = (f32[512,512]{1,0:T(8,128)}, f32[512,512]{1,0:T(8,128)}, f32[512,512]{1,0:T(8,128)}) custom-call(bf16[32,2,16,512]{3,2,1,0:T(8,128)(2,1)} %all-to-all-done.2.refs_0_, f32[512,512]{1,0:T(8,128)} %get-tuple-element.37.refs_1_, f32[512,512]{1,0:T(8,128)} %get-tuple-element.38.refs_3_.refs_2_, bf16[512,512]{1,0:T(8,128)(2,1)S(1)} %copy-done.10, ...), custom_call_target="tpu_custom_call" | custom-call | flops 4026531840 | bytes 11577344 | tf_op jit(solution)/shard_map/pallas_call | solution.py:570
  121.3 16.8 %all-to-all-done.3.refs_0_ = bf16[32,2,16,512]{3,2,1,0:T(8,128)(2,1)} async-done(((bf16[32,2,16,512]{3,2,1,0:T(8,128)(2,1)}), bf16[32,2,16,512]{3,2,1,0:T(8,128)(2,1)}, u32[]{:S(2)}, u32[]{:S(2)}) %all-to-all-start.3) | async-done | bytes 1048608 | tf_op jit(solution)/shard_map/all_to_all | solution.py:962
  138.1 0.0 copy-done.4
  138.2 0.0 copy-done.7
  138.2 7.5 %shard_map.118 = bf16[32,2,16,512]{3,2,1,0:T(8,128)(2,1)} custom-call(bf16[32,2,16,512]{3,2,1,0:T(8,128)(2,1)} %all-to-all-done.3.refs_0_, f32[512,512]{1,0:T(8,128)} %get-tuple-element.40.refs_1_, bf16[128,128]{1,0:T(8,128)(2,1)S(1)} %select_convert_fusion.refs_3_.refs_5_.refs_2_, bf16[512,512]{1,0:T(8,128)(2,1)S(1)} %copy-done.7, ...), custom_call_target="tpu_custom_call" | custom-call | flops 3221225472 | bytes 8431616 | tf_op jit(solution)/shard_map/pallas_call | solution.py:570
  145.7 29.9 %all_to_all.25.refs_0_ = bf16[32,2,16,512]{3,2,1,0:T(8,128)(2,1)S(1)} all-to-all(bf16[32,2,16,512]{3,2,1,0:T(8,128)(2,1)} %shard_map.118), channel_id=1, replica_groups=mesh['aux'=8,'row'=4] {'aux','row'}, dimensions={0} | all-to-all | bytes 2097152 | tf_op jit(solution)/shard_map/all_to_all | solution.py:962
  175.6 2.2 %shard_map.119 = f32[1,4,128,512]{3,2,1,0:T(8,128)} custom-call(bf16[32,2,16,512]{3,2,1,0:T(8,128)(2,1)S(1)} %all_to_all.25.refs_0_, f32[1,4,128,512]{3,2,1,0:T(8,128)} %bitcast.8), custom_call_target="tpu_custom_call" | custom-call | flops 536870912 | bytes 3145728 | tf_op jit(solution)/shard_map/pallas_call | solution.py:570
  (17 shorter events, 0.1 us)
Async XLA Ops:
  3.0 33.6 %all-to-all-start = ((bf16[32,2,16,512]{3,2,1,0:T(8,128)(2,1)}), bf16[32,2,16,512]{3,2,1,0:T(8,128)(2,1)S(1)}, u32[]{:S(2)}, u32[]{:S(2)}) async-start(bf16[32,2,16,512]{3,2,1,0:T(8,128)(2,1)} %shard_map.109), calls=%async_computation | async-start | bytes 2097152 | tf_op jit(solution)/shard_map/all_to_all | solution.py:962
  14.3 22.3 %copy-start.1 = (bf16[512,512]{1,0:T(8,128)(2,1)S(1)}, bf16[512,512]{1,0:T(8,128)(2,1)}, u32[]{:S(2)}) copy-start(bf16[512,512]{1,0:T(8,128)(2,1)} %get-tuple-element.25.refs_4_) | copy-start | bytes 1572868
  14.3 22.3 %copy-start.2 = (bf16[512,512]{1,0:T(8,128)(2,1)S(1)}, bf16[512,512]{1,0:T(8,128)(2,1)}, u32[]{:S(2)}) copy-start(bf16[512,512]{1,0:T(8,128)(2,1)} %get-tuple-element.24.refs_2_) | copy-start | bytes 1572868
  15.6 24.0 %copy-start.3 = (bf16[512,512]{1,0:T(8,128)(2,1)}, bf16[512,512]{1,0:T(8,128)(2,1)S(1)}, u32[]{:S(2)}) copy-start(bf16[512,512]{1,0:T(8,128)(2,1)S(1)} %fusion.17.refs_3_.refs_2_.refs_4_) | copy-start | bytes 1572868
  17.0 33.5 %copy-start.5 = (bf16[512,512]{1,0:T(8,128)(2,1)}, bf16[512,512]{1,0:T(8,128)(2,1)S(1)}, u32[]{:S(2)}) copy-start(bf16[512,512]{1,0:T(8,128)(2,1)S(1)} %fusion.18.refs_1_.refs_12_) | copy-start | bytes 1572868
  36.6 2.9 %copy-start = (bf16[32,2,16,512]{3,2,1,0:T(8,128)(2,1)}, bf16[32,2,16,512]{3,2,1,0:T(8,128)(2,1)S(1)}, u32[]{:S(2)}) copy-start(bf16[32,2,16,512]{3,2,1,0:T(8,128)(2,1)S(1)} %all-to-all-done.refs_0_.refs_3_) | copy-start | bytes 3145732
  39.5 4.0 %copy-start.14 = (s32[16,8]{0,1:T(8,128)S(1)}, s32[16,8]{0,1:T(8,128)}, u32[]{:S(2)}) copy-start(s32[16,8]{0,1:T(8,128)} %param.17) | copy-start | bytes 1540
  39.6 30.0 %all-to-all-start.1 = ((bf16[32,2,16,512]{3,2,1,0:T(8,128)(2,1)}), bf16[32,2,16,512]{3,2,1,0:T(8,128)(2,1)}, u32[]{:S(2)}, u32[]{:S(2)}) async-start(bf16[32,2,16,512]{3,2,1,0:T(8,128)(2,1)} %shard_map.111), calls=%async_computation.1 | async-start | bytes 2097152 | tf_op jit(solution)/shard_map/all_to_all | solution.py:962
  43.5 0.7 copy-start.15
  44.2 0.7 copy-start.13
  50.5 0.7 copy-start.6
  59.1 0.8 copy-start.11
  59.9 18.0 %copy-start.9 = (bf16[512,512]{1,0:T(8,128)(2,1)}, bf16[512,512]{1,0:T(8,128)(2,1)S(1)}, u32[]{:S(2)}) copy-start(bf16[512,512]{1,0:T(8,128)(2,1)S(1)} %get-tuple-element.35.refs_3_) | copy-start | bytes 1572868
  73.9 4.0 %copy-start.8 = (bf16[512,512]{1,0:T(8,128)(2,1)S(1)}, bf16[512,512]{1,0:T(8,128)(2,1)}, u32[]{:S(2)}) copy-start(bf16[512,512]{1,0:T(8,128)(2,1)} %get-tuple-element.27.refs_6_.refs_8_.refs_9_) | copy-start | bytes 1572868
  73.9 4.0 %copy-start.12 = (bf16[512,512]{1,0:T(8,128)(2,1)S(1)}, bf16[512,512]{1,0:T(8,128)(2,1)}, u32[]{:S(2)}) copy-start(bf16[512,512]{1,0:T(8,128)(2,1)} %copy-done.11) | copy-start | bytes 1572868
  73.9 30.0 %all-to-all-start.2 = ((bf16[32,2,16,512]{3,2,1,0:T(8,128)(2,1)}), bf16[32,2,16,512]{3,2,1,0:T(8,128)(2,1)}, u32[]{:S(2)}, u32[]{:S(2)}) async-start(bf16[32,2,16,512]{3,2,1,0:T(8,128)(2,1)} %shard_map.114), calls=%async_computation.2 | async-start | bytes 2097152 | tf_op jit(solution)/shard_map/all_to_all | solution.py:962
  108.2 4.0 %copy-start.10 = (bf16[512,512]{1,0:T(8,128)(2,1)S(1)}, bf16[512,512]{1,0:T(8,128)(2,1)}, u32[]{:S(2)}) copy-start(bf16[512,512]{1,0:T(8,128)(2,1)} %copy-done.9) | copy-start | bytes 1572868
  108.2 30.0 %all-to-all-start.3 = ((bf16[32,2,16,512]{3,2,1,0:T(8,128)(2,1)}), bf16[32,2,16,512]{3,2,1,0:T(8,128)(2,1)}, u32[]{:S(2)}, u32[]{:S(2)}) async-start(bf16[32,2,16,512]{3,2,1,0:T(8,128)(2,1)} %shard_map.116), calls=%async_computation.3 | async-start | bytes 2097152 | tf_op jit(solution)/shard_map/all_to_all | solution.py:962
  112.2 25.9 %copy-start.4 = (bf16[512,512]{1,0:T(8,128)(2,1)S(1)}, bf16[512,512]{1,0:T(8,128)(2,1)}, u32[]{:S(2)}) copy-start(bf16[512,512]{1,0:T(8,128)(2,1)} %copy-done.3) | copy-start | bytes 1572868
  112.2 25.9 %copy-start.7 = (bf16[512,512]{1,0:T(8,128)(2,1)S(1)}, bf16[512,512]{1,0:T(8,128)(2,1)}, u32[]{:S(2)}) copy-start(bf16[512,512]{1,0:T(8,128)(2,1)} %get-tuple-element.30.refs_9_.refs_11_.refs_3_) | copy-start | bytes 1572868

commit v7 on v6

--- a/solution.py
+++ b/solution.py
@@ -516,8 +516,11 @@
         known = len(self.coming)
         self.coming += [self.copy(a, b) for a, b in zip(self.sources[known:], self.buffers[known:])]
 
-    def send(self, index):
-        self.going.append(self.copy(self.results[index], self.targets[index]))
+    def send(self, index, rows=None):
+        made, target = self.results[index], self.targets[index]
+        if rows is not None:
+            made, target = made.at[rows], target.at[rows]
+        self.going.append(self.copy(made, target))
 
     def finish(self):
         for made in self.going:
@@ -543,7 +546,7 @@
     tall = lambda x, part: x.shape if part is None else x.shape[:1] + x.shape[2:]
     buffers = [pltpu.VMEM(tall(arrays[k], part), arrays[k].dtype) for k, part in views]
     results = [pltpu.VMEM(tall(shapes[k], part), shapes[k].dtype) for k, part in places]
-    count = len(buffers) + len(results)
+    count = len(buffers) + 2 * len(results)
 
     def kernel(*refs):
         small, refs = refs[: len(scalars)], refs[len(scalars) :]
@@ -615,9 +618,10 @@
 
 
 def send_products(s, stage, matrix, state_ref, index):
-    for b in row_blocks(s.extent, ROWS):
-        fill(s, stage.results[index], b, dot(matrix[b : b + ROWS, :], state_ref[...]).astype(BF16))
-    stage.send(index)
+    half = s.extent // 2
+    for b in row_blocks(s.extent, half):
+        fill(s, stage.results[index], b, dot(matrix[b : b + half, :], state_ref[...]).astype(BF16))
+        stage.send(index, slice(b // s.local, (b + half) // s.local))
 
 
 def take_rows(s, rows_in, row_lanes, s_ref):

time: 179 us -> 179 us (level)
  transfers between devices with their start and end apart: 4 -> 4, of which waited for: 4 -> 4; matrix products, arithmetic and copies ran while one was open for 2% -> 2% of each run, Pallas kernels for 19% -> 20%
where the time goes in v7:
time: 179 us; the launch traced here: 178 us
  waiting for transfers between devices  63.1 us (35%)
  Pallas kernels  59 us (33%)
  blocking collectives  29.9 us (17%)
  starting transfers between devices  19.2 us (11%)
  local copies, waits for them, and re-layouts  3.03 us (2%)
  other arithmetic  2.93 us (2%)
    all_to_all x4, waiting for transfers between devices, exchange(): lax.all_to_all(message, BOTH, split_axis=0, concat_axis=0, tiled=True)  63.1 us
    pallas_call x11, Pallas kernels, run_staged(): pl.pallas_call(kernel, out_shape=shapes, in_specs=[pl.BlockSpec(memory_sp...  59 us
    all_to_all x1, blocking collectives, exchange(): lax.all_to_all(message, BOTH, split_axis=0, concat_axis=0, tiled=True)  29.9 us
    all_to_all x4, starting transfers between devices, exchange(): lax.all_to_all(message, BOTH, split_axis=0, concat_axis=0, tiled=True)  19.2 us
  transfers between devices with their start and end apart: 4, of which 4 were waited for; matrix products, arithmetic and copies ran while one was open for 2% of the time, Pallas kernels for 20%

profile of v7, /device:TPU:0, one launch (start us, length us, event | category | flops | bytes accessed | tf_op | source)
XLA Modules:
  0.0 177.8 jit_solution(440955549201004539)
XLA Ops:
  0.0 3.1 %shard_map.109 = bf16[32,2,16,512]{3,2,1,0:T(8,128)(2,1)} custom-call(f32[1,4,128,512]{3,2,1,0:T(8,128)} %bitcast.7, s32[2,4]{1,0:T(2,128)} %refs_1_.3), custom_call_target="tpu_custom_call" | custom-call | flops 536870912 | bytes 2097184 | tf_op jit(solution)/shard_map/pallas_call | solution.py:573
  3.1 7.3 %all-to-all-start = ((bf16[32,2,16,512]{3,2,1,0:T(8,128)(2,1)}), bf16[32,2,16,512]{3,2,1,0:T(8,128)(2,1)S(1)}, u32[]{:S(2)}, u32[]{:S(2)}) async-start(bf16[32,2,16,512]{3,2,1,0:T(8,128)(2,1)} %shard_map.109), calls=%async_computation | async-start | bytes 2097152 | tf_op jit(solution)/shard_map/all_to_all | solution.py:966
  10.4 3.8 %shard_map.110 = (bf16[512,512]{1,0:T(8,128)(2,1)}, bf16[512,512]{1,0:T(8,128)(2,1)}, bf16[512,512]{1,0:T(8,128)(2,1)}, bf16[512,512]{1,0:T(8,128)(2,1)}) custom-call(s32[8]{0:T(128)} %refs_0_.2, bf16[8,64,64]{2,1,0:T(8,128)(2,1)} %refs_1_.4, bf16[8,64,64]{2,1,0:T(8,128)(2,1)} %refs_2_.2), custom_call_target="tpu_custom_call" | custom-call | flops 1073741824 | bytes 2228224 | tf_op jit(solution)/shard_map/pallas_call | solution.py:573
  14.4 0.0 copy-start.1
  14.4 0.0 copy-start.2
  14.4 1.2 fusion.17.refs_3_.refs_2_.refs_4_
  15.6 0.0 copy-start.3
  15.6 1.4 fusion.18.refs_1_.refs_12_
  17.1 0.0 copy-start.5
  17.1 19.5 %all-to-all-done.refs_0_.refs_3_ = bf16[32,2,16,512]{3,2,1,0:T(8,128)(2,1)S(1)} async-done(((bf16[32,2,16,512]{3,2,1,0:T(8,128)(2,1)}), bf16[32,2,16,512]{3,2,1,0:T(8,128)(2,1)S(1)}, u32[]{:S(2)}, u32[]{:S(2)}) %all-to-all-start) | async-done | bytes 1048608 | tf_op jit(solution)/shard_map/all_to_all | solution.py:966
  36.6 0.0 copy-start
  36.6 0.0 copy-done.1
  36.6 0.0 copy-done.2
  36.6 2.8 %shard_map.111 = bf16[32,2,16,512]{3,2,1,0:T(8,128)(2,1)} custom-call(bf16[32,2,16,512]{3,2,1,0:T(8,128)(2,1)S(1)} %all-to-all-done.refs_0_.refs_3_, bf16[512,512]{1,0:T(8,128)(2,1)S(1)} %fusion.18.refs_1_.refs_12_, bf16[512,512]{1,0:T(8,128)(2,1)S(1)} %copy-done.2, bf16[512,512]{1,0:T(8,128)(2,1)S(1)} %fusion.17.refs_3_.refs_2_.refs_4_, ...), custom_call_target="tpu_custom_call" | custom-call | flops 1073741824 | bytes 4194304 | tf_op jit(solution)/shard_map/pallas_call | solution.py:573
  39.5 0.0 copy-done.3
  39.5 0.0 copy-done
  39.5 0.0 copy-start.14
  39.5 3.9 %all-to-all-start.1 = ((bf16[32,2,16,512]{3,2,1,0:T(8,128)(2,1)}), bf16[32,2,16,512]{3,2,1,0:T(8,128)(2,1)}, u32[]{:S(2)}, u32[]{:S(2)}) async-start(bf16[32,2,16,512]{3,2,1,0:T(8,128)(2,1)} %shard_map.111), calls=%async_computation.1 | async-start | bytes 2097152 | tf_op jit(solution)/shard_map/all_to_all | solution.py:966
  43.5 0.0 copy-done.14
  43.5 0.0 copy-start.15
  43.5 0.7 copy.12.refs_4_
  44.1 0.0 copy-done.15
  44.2 0.0 copy-start.13
  44.2 0.7 copy.13.refs_5_
  44.8 0.0 copy-done.13
  44.9 0.1 copy.14
  45.1 0.2 select_convert_fusion.refs_3_.refs_5_.refs_2_
  45.2 5.3 %shard_map.112 = (bf16[4,512,128]{2,1,0:T(8,128)(2,1)}, bf16[512,512]{1,0:T(8,128)(2,1)}, bf16[4,512,128]{2,1,0:T(8,128)(2,1)}, bf16[512,512]{1,0:T(8,128)(2,1)}, f32[1,512]{1,0:T(1,128)}) custom-call(f32[4]{0:T(128)} %refs_0_.3, f32[4]{0:T(128)} %refs_1_.5, f32[4]{0:T(128)} %refs_2_.3, bf16[32,2,16,512]{3,2,1,0:T(8,128)(2,1)} %copy-done, ...), custom_call_target="tpu_custom_call" | custom-call | flops 268435456 | bytes 3156992 | tf_op jit(solution)/shard_map/pallas_call | solution.py:573
  50.5 0.0 copy-start.6
  50.5 0.0 copy-done.5
  50.5 0.7 copy-done.6
  51.2 7.9 %shard_map.113 = (f32[512,512]{1,0:T(8,128)}, f32[512,512]{1,0:T(8,128)}, bf16[512,512]{1,0:T(8,128)(2,1)S(1)}, bf16[512,512]{1,0:T(8,128)(2,1)S(1)}) custom-call(bf16[32,2,16,512]{3,2,1,0:T(8,128)(2,1)} %copy-done, bf16[512,512]{1,0:T(8,128)(2,1)S(1)} %fusion.18.refs_1_.refs_12_, bf16[512,512]{1,0:T(8,128)(2,1)} %copy-done.3, ...), custom_call_target="tpu_custom_call" | custom-call | flops 3221225472 | bytes 8431616 | tf_op jit(solution)/shard_map/pallas_call | solution.py:573
  59.1 0.0 copy-start.11
  59.1 0.8 copy-done.11
  59.9 0.0 copy-start.9
  59.9 9.6 %all-to-all-done.1.refs_0_ = bf16[32,2,16,512]{3,2,1,0:T(8,128)(2,1)} async-done(((bf16[32,2,16,512]{3,2,1,0:T(8,128)(2,1)}), bf16[32,2,16,512]{3,2,1,0:T(8,128)(2,1)}, u32[]{:S(2)}, u32[]{:S(2)}) %all-to-all-start.1) | async-done | bytes 1048608 | tf_op jit(solution)/shard_map/all_to_all | solution.py:966
  69.5 4.2 %shard_map.114 = bf16[32,2,16,512]{3,2,1,0:T(8,128)(2,1)} custom-call(bf16[32,2,16,512]{3,2,1,0:T(8,128)(2,1)} %all-to-all-done.1.refs_0_, f32[512,512]{1,0:T(8,128)} %get-tuple-element.33.refs_1_, bf16[512,512]{1,0:T(8,128)(2,1)S(1)} %copy-done.2, f32[512,512]{1,0:T(8,128)} %get-tuple-element.34.refs_3_.refs_2_, bf16[512,512]{1,0:T(8,128)(2,1)S(1)} %copy-done.1), custom_call_target="tpu_custom_call" | custom-call | flops 1342177280 | bytes 5242880 | tf_op jit(solution)/shard_map/pallas_call | solution.py:573
  73.7 0.0 copy-start.8
  73.7 0.0 copy-start.12
  73.7 4.0 %all-to-all-start.2 = ((bf16[32,2,16,512]{3,2,1,0:T(8,128)(2,1)}), bf16[32,2,16,512]{3,2,1,0:T(8,128)(2,1)}, u32[]{:S(2)}, u32[]{:S(2)}) async-start(bf16[32,2,16,512]{3,2,1,0:T(8,128)(2,1)} %shard_map.114), calls=%async_computation.2 | async-start | bytes 2097152 | tf_op jit(solution)/shard_map/all_to_all | solution.py:966
  77.7 0.0 copy-done.9
  77.7 0.0 copy-done.8
  77.7 0.0 copy-done.12
  77.8 8.8 %shard_map.115 = (f32[512,512]{1,0:T(8,128)}, f32[512,512]{1,0:T(8,128)}, f32[512,512]{1,0:T(8,128)}) custom-call(bf16[32,2,16,512]{3,2,1,0:T(8,128)(2,1)} %all-to-all-done.1.refs_0_, f32[512,512]{1,0:T(8,128)} %get-tuple-element.33.refs_1_, f32[512,512]{1,0:T(8,128)} %get-tuple-element.34.refs_3_.refs_2_, bf16[512,512]{1,0:T(8,128)(2,1)S(1)} %get-tuple-element.35.refs_3_, ...), custom_call_target="tpu_custom_call" | custom-call | flops 4026531840 | bytes 10528768 | tf_op jit(solution)/shard_map/pallas_call | solution.py:573
  86.5 17.2 %all-to-all-done.2.refs_0_ = bf16[32,2,16,512]{3,2,1,0:T(8,128)(2,1)} async-done(((bf16[32,2,16,512]{3,2,1,0:T(8,128)(2,1)}), bf16[32,2,16,512]{3,2,1,0:T(8,128)(2,1)}, u32[]{:S(2)}, u32[]{:S(2)}) %all-to-all-start.2) | async-done | bytes 1048608 | tf_op jit(solution)/shard_map/all_to_all | solution.py:966
  103.7 4.2 %shard_map.116 = bf16[32,2,16,512]{3,2,1,0:T(8,128)(2,1)} custom-call(bf16[32,2,16,512]{3,2,1,0:T(8,128)(2,1)} %all-to-all-done.2.refs_0_, f32[512,512]{1,0:T(8,128)} %get-tuple-element.37.refs_1_, bf16[512,512]{1,0:T(8,128)(2,1)S(1)} %copy-done.2, f32[512,512]{1,0:T(8,128)} %get-tuple-element.38.refs_3_.refs_2_, bf16[512,512]{1,0:T(8,128)(2,1)S(1)} %copy-done.1), custom_call_target="tpu_custom_call" | custom-call | flops 1342177280 | bytes 5242880 | tf_op jit(solution)/shard_map/pallas_call | solution.py:573
  108.0 0.0 copy-start.10
  108.0 4.0 %all-to-all-start.3 = ((bf16[32,2,16,512]{3,2,1,0:T(8,128)(2,1)}), bf16[32,2,16,512]{3,2,1,0:T(8,128)(2,1)}, u32[]{:S(2)}, u32[]{:S(2)}) async-start(bf16[32,2,16,512]{3,2,1,0:T(8,128)(2,1)} %shard_map.116), calls=%async_computation.3 | async-start | bytes 2097152 | tf_op jit(solution)/shard_map/all_to_all | solution.py:966
  112.0 0.0 copy-done.10
  112.0 0.0 copy-start.4
  112.0 0.0 copy-start.7
  112.0 9.1 %shard_map.117 = (f32[512,512]{1,0:T(8,128)}, f32[512,512]{1,0:T(8,128)}, f32[512,512]{1,0:T(8,128)}) custom-call(bf16[32,2,16,512]{3,2,1,0:T(8,128)(2,1)} %all-to-all-done.2.refs_0_, f32[512,512]{1,0:T(8,128)} %get-tuple-element.37.refs_1_, f32[512,512]{1,0:T(8,128)} %get-tuple-element.38.refs_3_.refs_2_, bf16[512,512]{1,0:T(8,128)(2,1)S(1)} %copy-done.10, ...), custom_call_target="tpu_custom_call" | custom-call | flops 4026531840 | bytes 11577344 | tf_op jit(solution)/shard_map/pallas_call | solution.py:573
  121.1 16.8 %all-to-all-done.3.refs_0_ = bf16[32,2,16,512]{3,2,1,0:T(8,128)(2,1)} async-done(((bf16[32,2,16,512]{3,2,1,0:T(8,128)(2,1)}), bf16[32,2,16,512]{3,2,1,0:T(8,128)(2,1)}, u32[]{:S(2)}, u32[]{:S(2)}) %all-to-all-start.3) | async-done | bytes 1048608 | tf_op jit(solution)/shard_map/all_to_all | solution.py:966
  137.9 0.0 copy-done.4
  137.9 0.0 copy-done.7
  137.9 7.5 %shard_map.118 = bf16[32,2,16,512]{3,2,1,0:T(8,128)(2,1)} custom-call(bf16[32,2,16,512]{3,2,1,0:T(8,128)(2,1)} %all-to-all-done.3.refs_0_, f32[512,512]{1,0:T(8,128)} %get-tuple-element.40.refs_1_, bf16[128,128]{1,0:T(8,128)(2,1)S(1)} %select_convert_fusion.refs_3_.refs_5_.refs_2_, bf16[512,512]{1,0:T(8,128)(2,1)S(1)} %copy-done.7, ...), custom_call_target="tpu_custom_call" | custom-call | flops 3221225472 | bytes 8431616 | tf_op jit(solution)/shard_map/pallas_call | solution.py:573
  145.5 29.9 %all_to_all.25.refs_0_ = bf16[32,2,16,512]{3,2,1,0:T(8,128)(2,1)S(1)} all-to-all(bf16[32,2,16,512]{3,2,1,0:T(8,128)(2,1)} %shard_map.118), channel_id=1, replica_groups=mesh['aux'=8,'row'=4] {'aux','row'}, dimensions={0} | all-to-all | bytes 2097152 | tf_op jit(solution)/shard_map/all_to_all | solution.py:966
  175.4 2.2 %shard_map.119 = f32[1,4,128,512]{3,2,1,0:T(8,128)} custom-call(bf16[32,2,16,512]{3,2,1,0:T(8,128)(2,1)S(1)} %all_to_all.25.refs_0_, f32[1,4,128,512]{3,2,1,0:T(8,128)} %bitcast.8), custom_call_target="tpu_custom_call" | custom-call | flops 536870912 | bytes 3145728 | tf_op jit(solution)/shard_map/pallas_call | solution.py:573
  (17 shorter events, 0.1 us)
Async XLA Ops:
  3.1 33.6 %all-to-all-start = ((bf16[32,2,16,512]{3,2,1,0:T(8,128)(2,1)}), bf16[32,2,16,512]{3,2,1,0:T(8,128)(2,1)S(1)}, u32[]{:S(2)}, u32[]{:S(2)}) async-start(bf16[32,2,16,512]{3,2,1,0:T(8,128)(2,1)} %shard_map.109), calls=%async_computation | async-start | bytes 2097152 | tf_op jit(solution)/shard_map/all_to_all | solution.py:966
  14.4 22.2 %copy-start.1 = (bf16[512,512]{1,0:T(8,128)(2,1)S(1)}, bf16[512,512]{1,0:T(8,128)(2,1)}, u32[]{:S(2)}) copy-start(bf16[512,512]{1,0:T(8,128)(2,1)} %get-tuple-element.25.refs_4_) | copy-start | bytes 1572868
  14.4 22.2 %copy-start.2 = (bf16[512,512]{1,0:T(8,128)(2,1)S(1)}, bf16[512,512]{1,0:T(8,128)(2,1)}, u32[]{:S(2)}) copy-start(bf16[512,512]{1,0:T(8,128)(2,1)} %get-tuple-element.24.refs_2_) | copy-start | bytes 1572868
  15.6 23.9 %copy-start.3 = (bf16[512,512]{1,0:T(8,128)(2,1)}, bf16[512,512]{1,0:T(8,128)(2,1)S(1)}, u32[]{:S(2)}) copy-start(bf16[512,512]{1,0:T(8,128)(2,1)S(1)} %fusion.17.refs_3_.refs_2_.refs_4_) | copy-start | bytes 1572868
  17.1 33.4 %copy-start.5 = (bf16[512,512]{1,0:T(8,128)(2,1)}, bf16[512,512]{1,0:T(8,128)(2,1)S(1)}, u32[]{:S(2)}) copy-start(bf16[512,512]{1,0:T(8,128)(2,1)S(1)} %fusion.18.refs_1_.refs_12_) | copy-start | bytes 1572868
  36.6 2.9 %copy-start = (bf16[32,2,16,512]{3,2,1,0:T(8,128)(2,1)}, bf16[32,2,16,512]{3,2,1,0:T(8,128)(2,1)S(1)}, u32[]{:S(2)}) copy-start(bf16[32,2,16,512]{3,2,1,0:T(8,128)(2,1)S(1)} %all-to-all-done.refs_0_.refs_3_) | copy-start | bytes 3145732
  39.5 4.0 %copy-start.14 = (s32[16,8]{0,1:T(8,128)S(1)}, s32[16,8]{0,1:T(8,128)}, u32[]{:S(2)}) copy-start(s32[16,8]{0,1:T(8,128)} %param.17) | copy-start | bytes 1540
  39.5 30.0 %all-to-all-start.1 = ((bf16[32,2,16,512]{3,2,1,0:T(8,128)(2,1)}), bf16[32,2,16,512]{3,2,1,0:T(8,128)(2,1)}, u32[]{:S(2)}, u32[]{:S(2)}) async-start(bf16[32,2,16,512]{3,2,1,0:T(8,128)(2,1)} %shard_map.111), calls=%async_computation.1 | async-start | bytes 2097152 | tf_op jit(solution)/shard_map/all_to_all | solution.py:966
  43.5 0.7 copy-start.15
  44.2 0.7 copy-start.13
  50.5 0.7 copy-start.6
  59.1 0.8 copy-start.11
  59.9 17.8 %copy-start.9 = (bf16[512,512]{1,0:T(8,128)(2,1)}, bf16[512,512]{1,0:T(8,128)(2,1)S(1)}, u32[]{:S(2)}) copy-start(bf16[512,512]{1,0:T(8,128)(2,1)S(1)} %get-tuple-element.35.refs_3_) | copy-start | bytes 1572868
  73.7 4.0 %copy-start.8 = (bf16[512,512]{1,0:T(8,128)(2,1)S(1)}, bf16[512,512]{1,0:T(8,128)(2,1)}, u32[]{:S(2)}) copy-start(bf16[512,512]{1,0:T(8,128)(2,1)} %get-tuple-element.27.refs_6_.refs_8_.refs_9_) | copy-start | bytes 1572868
  73.7 4.0 %copy-start.12 = (bf16[512,512]{1,0:T(8,128)(2,1)S(1)}, bf16[512,512]{1,0:T(8,128)(2,1)}, u32[]{:S(2)}) copy-start(bf16[512,512]{1,0:T(8,128)(2,1)} %copy-done.11) | copy-start | bytes 1572868
  73.7 30.0 %all-to-all-start.2 = ((bf16[32,2,16,512]{3,2,1,0:T(8,128)(2,1)}), bf16[32,2,16,512]{3,2,1,0:T(8,128)(2,1)}, u32[]{:S(2)}, u32[]{:S(2)}) async-start(bf16[32,2,16,512]{3,2,1,0:T(8,128)(2,1)} %shard_map.114), calls=%async_computation.2 | async-start | bytes 2097152 | tf_op jit(solution)/shard_map/all_to_all | solution.py:966
  108.0 4.0 %copy-start.10 = (bf16[512,512]{1,0:T(8,128)(2,1)S(1)}, bf16[512,512]{1,0:T(8,128)(2,1)}, u32[]{:S(2)}) copy-start(bf16[512,512]{1,0:T(8,128)(2,1)} %copy-done.9) | copy-start | bytes 1572868
  108.0 30.0 %all-to-all-start.3 = ((bf16[32,2,16,512]{3,2,1,0:T(8,128)(2,1)}), bf16[32,2,16,512]{3,2,1,0:T(8,128)(2,1)}, u32[]{:S(2)}, u32[]{:S(2)}) async-start(bf16[32,2,16,512]{3,2,1,0:T(8,128)(2,1)} %shard_map.116), calls=%async_computation.3 | async-start | bytes 2097152 | tf_op jit(solution)/shard_map/all_to_all | solution.py:966
  112.0 25.9 %copy-start.4 = (bf16[512,512]{1,0:T(8,128)(2,1)S(1)}, bf16[512,512]{1,0:T(8,128)(2,1)}, u32[]{:S(2)}) copy-start(bf16[512,512]{1,0:T(8,128)(2,1)} %copy-done.3) | copy-start | bytes 1572868
  112.0 25.9 %copy-start.7 = (bf16[512,512]{1,0:T(8,128)(2,1)S(1)}, bf16[512,512]{1,0:T(8,128)(2,1)}, u32[]{:S(2)}) copy-start(bf16[512,512]{1,0:T(8,128)(2,1)} %get-tuple-element.30.refs_9_.refs_11_.refs_3_) | copy-start | bytes 1572868
